TPU v7x, 128 devices: a whole 4x4x4 slice. The times are simulated.
128 devices in a mesh: rows: 16 (over y, z), rep: 8 (over x, core).
Axes of the slice: x: 4, y: 4, z: 4, core: 2. Of those that a mesh axis runs over, the one named last changes fastest.
Arguments:
- features: bfloat16 [65536, 128], P('rows'), may hold values from -6 to 6
- tile_values: bfloat16 [16, 8, 512, 128, 128], P('rows', 'rep'), may hold values from -0.1875 to 0.1875
- tile_rows: int32 [16, 8, 512], P('rows', 'rep'), may hold values from 0 to 31
- tile_slots: int32 [16, 8, 512], P('rows', 'rep'), may hold values from 0 to 127
- tile_counts: int32 [16, 8], P('rows', 'rep'), may hold values from 64 to 512, as said below
- fetch_lists: int32 [16, 16, 8], P('rows'), may hold values from 0 to 31, as said below
- filter_weights: bfloat16 [4, 128, 256], replicated, may hold values from -0.5 to 0.5
Outputs:
- convolved: bfloat16 [65536, 256], P(('rows', 'rep'))
Inputs may be any that keep to these rules, and one draw needn't show every extreme that they name: Tile slots from tile_counts[r, j] on carry no part of the operator; one device has all 512 slots live. `fetch_lists`: the 8 entries of one reader and one owner are distinct.
All inputs are finite; a program needn't handle non-finite values.
Results may differ from a plain program's by a relative error of at most 0.0065.
Values may be sent and summed in bfloat16 or wider, within the bound.
No kernel may reach another device: no remote copies, remote signals or barrier semaphores. Data moves between devices by JAX's collectives and lax.ppermute only.
A program may use at most 128 MiB of HBM per device.

v0:
```python
import jax
import jax.numpy as jnp
from jax import lax
from jax.experimental import pallas as pl
from jax.experimental.pallas import tpu as pltpu
from jax.sharding import PartitionSpec as P


UNROLL = 32
CORES = 2


def tile_sums(fetched, values, rows_of, slots_of, scalars, row_blocks, whole_blocks):
    replicas, _, sub, width = fetched.shape
    tile = values.shape[1]
    chips = replicas // CORES
    per = row_blocks // replicas

    def body(scalar, rows, slot, fetched, vals, peer, mine, acc):
        count = scalar[0]
        chip = scalar[1]
        core = scalar[2]

        def clear(block, carry):
            acc[block] = jnp.zeros((tile, width), jnp.float32)
            return carry

        lax.fori_loop(0, row_blocks + 1, clear, 0)

        def group(step, carry):
            products = []
            for unit in range(UNROLL):
                t = step * UNROLL + unit
                block = fetched[:, slot[t]].reshape(tile, width)
                target = jnp.where(t < count, rows[t], row_blocks)
                products.append(
                    (target, jnp.dot(vals[t], block, preferred_element_type=jnp.float32))
                )
            for target, product in products:
                acc[target] += product
            return carry

        lax.fori_loop(0, (count + UNROLL - 1) // UNROLL, group, 0)

        for hops in range(chips):
            for out, from_core in ((peer, 1 - core), (mine, core)):
                rank = lax.rem(chip + hops, chips) * CORES + from_core
                if whole_blocks:
                    share = acc[pl.ds(rank * per, per)].reshape(per * replicas, sub, width)
                else:
                    share = acc[pl.ds(0, row_blocks), pl.ds(pl.multiple_of(rank * sub, sub), sub), :]
                out[hops] = share.astype(out.dtype)

    smem = pl.BlockSpec(memory_space=pltpu.SMEM)
    vmem = pl.BlockSpec(memory_space=pltpu.VMEM)
    shape = (chips, row_blocks, sub, width)
    return pl.pallas_call(
        body,
        out_shape=(
            pltpu.VMEM(shape, jnp.bfloat16),
            pltpu.VMEM(shape, jnp.float32),
        ),
        in_specs=[smem, smem, smem, vmem, vmem],
        out_specs=(vmem, vmem),
        scratch_shapes=[pltpu.VMEM((row_blocks + 1, tile, width), jnp.float32)],
        compiler_params=pltpu.CompilerParams(vmem_limit_bytes=16 * 2**20),
        name="tile_sums",
    )(
        scalars,
        rows_of,
        slots_of,
        pltpu.with_memory_space_constraint(fetched, pltpu.VMEM),
        pltpu.with_memory_space_constraint(values, pltpu.VMEM),
    )


def load_live(values, scalars, after):
    def body(scalar, values, after, out, semaphore):
        groups = (scalar[0] + UNROLL - 1) // UNROLL

        def copy(step):
            part = pl.ds(step * UNROLL, UNROLL)
            return pltpu.make_async_copy(values.at[part], out.at[part], semaphore.at[step])

        def start(step, carry):
            copy(step).start()
            return carry

        def wait(step, carry):
            copy(step).wait()
            return carry

        lax.fori_loop(0, groups, start, 0)
        lax.fori_loop(0, groups, wait, 0)

    return pl.pallas_call(
        body,
        out_shape=pltpu.VMEM(values.shape, values.dtype),
        in_specs=[
            pl.BlockSpec(memory_space=pltpu.SMEM),
            pl.BlockSpec(memory_space=pltpu.HBM),
            pl.BlockSpec(memory_space=pl.ANY),
        ],
        out_specs=pl.BlockSpec(memory_space=pltpu.VMEM),
        scratch_shapes=[pltpu.SemaphoreType.DMA((values.shape[0] // UNROLL,))],
        compiler_params=pltpu.CompilerParams(vmem_limit_bytes=2 * 2**20),
        name="load_live",
    )(scalars, pltpu.with_memory_space_constraint(values, pltpu.HBM), after)


def on_device(
    features, tile_values, tile_rows, tile_slots, tile_counts, fetch_lists, filter_weights
):
    values = tile_values[0, 0]
    rows_of = tile_rows[0, 0]
    slots_of = tile_slots[0, 0]
    wanted = fetch_lists[0]
    tile = values.shape[1]
    local_rows, width = features.shape
    row_blocks = local_rows // tile
    replicas = lax.axis_size("rep")
    chips = replicas // CORES
    sub = tile // replicas
    rank = lax.axis_index("rep")
    share_rows = local_rows // replicas
    degree_last = filter_weights.shape[0] - 1
    chip, core = rank // CORES, rank % CORES
    places = [
        ((chip + hops) % chips * CORES + core, (chip + hops) % chips * CORES + 1 - core)
        for hops in range(chips)
    ]
    scalars = jnp.stack([tile_counts[0, 0], chip, core, *sum(places, ())]).astype(jnp.int32)

    def along(x, hops):
        step = CORES * hops
        return lax.ppermute(x, "rep", [((i + step) % replicas, i) for i in range(replicas)])

    def partner(x):
        return lax.ppermute(x, "rep", [(i, i ^ 1) for i in range(replicas)])

    def gather(sent):
        slots = sent.shape[0]
        half = slots // 2
        low, high = sent[:half], sent[half:]
        before_low, after_high = along(low, -1), along(high, 1)
        before_high, after_low = along(high, -1), along(low, 1)
        other = partner(sent)
        live = load_live(values, scalars, sent)
        before_low, live = lax.optimization_barrier((before_low, live))
        far_low, far_high = along(before_low, -1), along(after_high, 1)
        fetched = jnp.zeros((replicas, slots, sub, width), sent.dtype)

        def put(fetched, array, hops, other_core, start):
            place = places[hops][other_core]
            return lax.dynamic_update_slice(
                fetched, array[None], (place, start, 0, 0), allow_negative_indices=False
            )

        fetched = put(fetched, sent, 0, 0, 0)
        fetched = put(fetched, other, 0, 1, 0)
        for array, hops, start in (
            (before_low, -1, 0),
            (after_high, 1, half),
            (before_high, -1, half),
            (after_low, 1, 0),
            (far_low, 2, 0),
            (far_high, 2, half),
        ):
            fetched = put(fetched, array, hops, 0, start)
            crossed = partner(array)
            fetched = put(fetched, crossed, hops, 1, start)
        return fetched, live

    def reduce(peer, mine):
        sums = mine + partner(peer).astype(jnp.float32)
        sent = [sums[hops].astype(jnp.bfloat16) for hops in range(chips)]
        half = row_blocks // 2
        low, high = along(sent[2][:half], -1), along(sent[2][half:], 1)
        parts = [along(sent[1], -1), along(sent[3], 1)]
        parts.append(jnp.concatenate([along(low, -1), along(high, 1)], 0))
        total = sums[0]
        for part in parts:
            total = total + part.astype(jnp.float32)
        return total

    served = lax.all_to_all(wanted, "rows", split_axis=0, concat_axis=0, tiled=True)
    terms = [
        lax.dynamic_slice_in_dim(
            features.reshape(row_blocks, tile, width), rank * sub, sub, 1
        )
    ]
    own = [lax.dynamic_slice_in_dim(features, rank * share_rows, share_rows, 0)]

    def step(degree):
        last = degree == degree_last
        if last:
            swapped = jnp.stack(terms[1:], 1).reshape(
                replicas, row_blocks // replicas, degree_last - 1, sub, width
            )
            swapped = lax.all_to_all(swapped, "rep", split_axis=0, concat_axis=0, tiled=True)
            swapped = swapped.transpose(2, 1, 0, 3, 4).reshape(degree_last - 1, share_rows, width)
            own.extend(swapped[k] for k in range(degree_last - 1))
        sent = lax.all_to_all(
            terms[-1][served], "rows", split_axis=0, concat_axis=0, tiled=True
        ).reshape(-1, sub, width)
        fetched, live = gather(sent)
        peer, mine = tile_sums(
            fetched, live, rows_of, slots_of, scalars, row_blocks, whole_blocks=last
        )
        total = reduce(peer, mine)
        if last:
            total = total.reshape(share_rows, width)
            before = own[-2]
        else:
            before = terms[-2] if degree > 1 else None
        following = total if degree == 1 else 2.0 * total - before.astype(jnp.float32)
        (own if last else terms).append(following.astype(jnp.bfloat16))

    for degree in range(1, degree_last + 1):
        step(degree)
    output = jnp.zeros((share_rows, filter_weights.shape[2]), jnp.float32)
    for degree in range(degree_last + 1):
        output = output + jnp.dot(
            own[degree], filter_weights[degree], preferred_element_type=jnp.float32
        )
    return output.astype(jnp.bfloat16)


def solution(mesh):
    return jax.shard_map(
        on_device,
        mesh=mesh,
        in_specs=(
            P("rows", None),
            P("rows", "rep", None, None, None),
            P("rows", "rep", None),
            P("rows", "rep", None),
            P("rows", "rep"),
            P("rows", None, None),
            P(),
        ),
        out_specs=P(("rows", "rep"), None),
        check_vma=False,
    )
```

profile of v0, /device:TPU:0, one launch (start us, length us, event | category | flops | bytes accessed | tf_op | source)
XLA Modules:
  0.0 206.6 jit_solution(4529034848439919357)
XLA Ops:
  0.0 1.4 copy.20
  1.4 8.2 %all-to-all-start = ((s32[16,1,8]{2,1,0:T(1,128)}), s32[16,1,8]{2,1,0:T(1,128)S(1)}, u32[]{:S(2)}, u32[]{:S(2)}) async-start(s32[16,1,8]{2,1,0:T(1,128)} %copy.20), calls=%async_computation | async-start | bytes 16384 | tf_op jit(solution)/shard_map/all_to_all | solution.py:186
  9.5 0.9 constant_dynamic-slice_fusion
  10.5 6.6 %all-to-all-done = s32[16,1,8]{2,1,0:T(1,128)S(1)} async-done(((s32[16,1,8]{2,1,0:T(1,128)}), s32[16,1,8]{2,1,0:T(1,128)S(1)}, u32[]{:S(2)}, u32[]{:S(2)}) %all-to-all-start) | async-done | bytes 544 | tf_op jit(solution)/shard_map/all_to_all | solution.py:186
  18.0 13.1 %all_to_all.32 = bf16[16,8,16,128]{3,2,1,0:T(8,128)(2,1)S(1)} all-to-all(bf16[16,8,16,128]{3,2,1,0:T(8,128)(2,1)S(1)} %bitcast.232), channel_id=1, replica_groups=mesh['rows'=16,'rep'=8] {'rows'}, dimensions={0} | all-to-all | bytes 1048576 | tf_op jit(solution)/shard_map/all_to_all | solution.py:203
  31.1 1.6 collective-permute-start.1
  32.7 1.7 collective-permute-start.3
  35.5 3.0 %collective-permute-start.7 = (bf16[64,16,128]{2,1,0:T(8,128)(2,1)S(1)}, bf16[64,16,128]{2,1,0:T(8,128)(2,1)S(1)}, u32[]{:S(2)}, u32[]{:S(2)}) collective-permute-start(bf16[64,16,128]{2,1,0:T(8,128)(2,1)S(1)} %bitcast.240), channel_id=1, source_target_pairs={{2,0},{3,1},{4,2},{5,3},{6,4},{7,5},{0,6},{1,7},{10,8},{11,9},{12,... | collective-permute-start | bytes 786440 | tf_op jit(solution)/shard_map/ppermute | solution.py:136
  38.5 3.5 %load_live.3.vals = bf16[512,128,128]{2,1,0:T(8,128)(2,1)S(1)} custom-call(s32[11]{0:T(128)S(1)} %stack.52.scalar, bf16[512,128,128]{2,1,0:T(8,128)(2,1)} %bitcast.227, bf16[128,16,128]{2,1,0:T(8,128)(2,1)S(1)} %bitcast.213), custom_call_target="tpu_custom_call" | custom-call | tf_op jit(solution)/shard_map/load_live/pallas_call | solution.py:96
  43.4 2.7 %collective-permute-start.11 = (bf16[64,16,128]{2,1,0:T(8,128)(2,1)S(1)}, bf16[64,16,128]{2,1,0:T(8,128)(2,1)S(1)}, u32[]{:S(2)}, u32[]{:S(2)}) collective-permute-start(bf16[64,16,128]{2,1,0:T(8,128)(2,1)S(1)} %collective-permute-done.3), channel_id=1, source_target_pairs={{2,0},{3,1},{4,2},{5,3},{6,4},{7,5},{0,6},{1,7},{10,8},{11,9},{12,... | collective-permute-start | bytes 786440 | tf_op jit(solution)/shard_map/ppermute | solution.py:136
  48.0 4.7 %collective-permute-done.9 = bf16[64,16,128]{2,1,0:T(8,128)(2,1)S(1)} collective-permute-done((bf16[64,16,128]{2,1,0:T(8,128)(2,1)S(1)}, bf16[64,16,128]{2,1,0:T(8,128)(2,1)S(1)}, u32[]{:S(2)}, u32[]{:S(2)}) %collective-permute-start.9) | collective-permute-done | bytes 262176 | tf_op jit(solution)/shard_map/ppermute | solution.py:136
  54.6 3.9 %tile_sums.3 = (bf16[4,32,16,128]{3,2,1,0:T(8,128)(2,1)S(1)}, f32[4,32,16,128]{3,2,1,0:T(8,128)S(1)}) custom-call(s32[11]{0:T(128)S(1)} %stack.52.scalar, s32[512]{0:T(512)S(1)} %bitcast.221, s32[512]{0:T(512)S(1)} %bitcast.224, bf16[8,128,16,128]{3,2,1,0:T(8,128)(2,1)S(1)} %bitcast_dynamic-update-slice_fusion.30.fetched, ...), custom_call_target="tpu_custom_call" | custom-call | tf_op jit(solution)/shard_map/tile_sums/pallas_call | solution.py:57
  59.2 1.5 collective-permute-done.13
  61.1 3.2 %collective-permute-start.15 = (bf16[32,16,128]{2,1,0:T(8,128)(2,1)S(1)}, bf16[32,16,128]{2,1,0:T(8,128)(2,1)S(1)}, u32[]{:S(2)}, u32[]{:S(2)}) collective-permute-start(bf16[32,16,128]{2,1,0:T(8,128)(2,1)S(1)} %get-tuple-element.50), channel_id=1, source_target_pairs={{2,0},{3,1},{4,2},{5,3},{6,4},{7,5},{0,6},{1,7},{10,8},{11,9},{12,... | collective-permute-start | bytes 393224 | tf_op jit(solution)/shard_map/ppermute | solution.py:136
  64.3 3.2 %collective-permute-start.18 = (bf16[16,16,128]{2,1,0:T(8,128)(2,1)S(1)}, bf16[16,16,128]{2,1,0:T(8,128)(2,1)S(1)}, u32[]{:S(2)}, u32[]{:S(2)}) collective-permute-start(bf16[16,16,128]{2,1,0:T(8,128)(2,1)S(1)} %get-tuple-element.48), channel_id=1, source_target_pairs={{2,0},{3,1},{4,2},{5,3},{6,4},{7,5},{0,6},{1,7},{10,8},{11,9},{12,... | collective-permute-start | bytes 196616 | tf_op jit(solution)/shard_map/ppermute | solution.py:136
  67.5 2.2 %collective-permute-done.16 = bf16[16,16,128]{2,1,0:T(8,128)(2,1)S(1)} collective-permute-done((bf16[16,16,128]{2,1,0:T(8,128)(2,1)S(1)}, bf16[16,16,128]{2,1,0:T(8,128)(2,1)S(1)}, u32[]{:S(2)}, u32[]{:S(2)}) %collective-permute-start.16) | collective-permute-done | bytes 65568 | tf_op jit(solution)/shard_map/ppermute | solution.py:136
  69.8 3.2 %collective-permute-start.19 = (bf16[16,16,128]{2,1,0:T(8,128)(2,1)S(1)}, bf16[16,16,128]{2,1,0:T(8,128)(2,1)S(1)}, u32[]{:S(2)}, u32[]{:S(2)}) collective-permute-start(bf16[16,16,128]{2,1,0:T(8,128)(2,1)S(1)} %collective-permute-done.18), channel_id=1, source_target_pairs={{2,0},{3,1},{4,2},{5,3},{6,4},{7,5},{0,6},{1,7},{10,8},{11,9},{12,... | collective-permute-start | bytes 196616 | tf_op jit(solution)/shard_map/ppermute | solution.py:136
  73.0 2.2 %collective-permute-done.17 = bf16[16,16,128]{2,1,0:T(8,128)(2,1)S(1)} collective-permute-done((bf16[16,16,128]{2,1,0:T(8,128)(2,1)S(1)}, bf16[16,16,128]{2,1,0:T(8,128)(2,1)S(1)}, u32[]{:S(2)}, u32[]{:S(2)}) %collective-permute-start.17) | collective-permute-done | bytes 65568 | tf_op jit(solution)/shard_map/ppermute | solution.py:136
  76.0 17.4 %all_to_all.33 = bf16[16,8,16,128]{3,2,1,0:T(8,128)(2,1)S(1)} all-to-all(bf16[16,8,16,128]{3,2,1,0:T(8,128)(2,1)S(1)} %bitcast.234), channel_id=1, replica_groups=mesh['rows'=16,'rep'=8] {'rows'}, dimensions={0} | all-to-all | bytes 1048576 | tf_op jit(solution)/shard_map/all_to_all | solution.py:203
  93.6 3.3 %collective-permute-start.23 = (bf16[64,16,128]{2,1,0:T(8,128)(2,1)S(1)}, bf16[64,16,128]{2,1,0:T(8,128)(2,1)S(1)}, u32[]{:S(2)}, u32[]{:S(2)}) collective-permute-start(bf16[64,16,128]{2,1,0:T(8,128)(2,1)S(1)} %bitcast.249), channel_id=1, source_target_pairs={{2,0},{3,1},{4,2},{5,3},{6,4},{7,5},{0,6},{1,7},{10,8},{11,9},{12,... | collective-permute-start | bytes 786440 | tf_op jit(solution)/shard_map/ppermute | solution.py:136
  96.8 3.5 %load_live.4.vals = bf16[512,128,128]{2,1,0:T(8,128)(2,1)S(1)} custom-call(s32[11]{0:T(128)S(1)} %stack.52.scalar, bf16[512,128,128]{2,1,0:T(8,128)(2,1)} %bitcast.228, bf16[128,16,128]{2,1,0:T(8,128)(2,1)S(1)} %bitcast.219), custom_call_target="tpu_custom_call" | custom-call | tf_op jit(solution)/shard_map/load_live/pallas_call | solution.py:96
  100.4 3.2 %collective-permute-start.27 = (bf16[64,16,128]{2,1,0:T(8,128)(2,1)S(1)}, bf16[64,16,128]{2,1,0:T(8,128)(2,1)S(1)}, u32[]{:S(2)}, u32[]{:S(2)}) collective-permute-start(bf16[64,16,128]{2,1,0:T(8,128)(2,1)S(1)} %bitcast.248), channel_id=1, source_target_pairs={{2,0},{3,1},{4,2},{5,3},{6,4},{7,5},{0,6},{1,7},{10,8},{11,9},{12,... | collective-permute-start | bytes 786440 | tf_op jit(solution)/shard_map/ppermute | solution.py:136
  104.9 2.8 %collective-permute-start.31 = (bf16[64,16,128]{2,1,0:T(8,128)(2,1)S(1)}, bf16[64,16,128]{2,1,0:T(8,128)(2,1)S(1)}, u32[]{:S(2)}, u32[]{:S(2)}) collective-permute-start(bf16[64,16,128]{2,1,0:T(8,128)(2,1)S(1)} %collective-permute-done.23), channel_id=1, source_target_pairs={{2,0},{3,1},{4,2},{5,3},{6,4},{7,5},{0,6},{1,7},{10,8},{11,9},{12,... | collective-permute-start | bytes 786440 | tf_op jit(solution)/shard_map/ppermute | solution.py:136
  107.8 3.0 %collective-permute-done.25 = bf16[64,16,128]{2,1,0:T(8,128)(2,1)S(1)} collective-permute-done((bf16[64,16,128]{2,1,0:T(8,128)(2,1)S(1)}, bf16[64,16,128]{2,1,0:T(8,128)(2,1)S(1)}, u32[]{:S(2)}, u32[]{:S(2)}) %collective-permute-start.25) | collective-permute-done | bytes 262176 | tf_op jit(solution)/shard_map/ppermute | solution.py:136
  111.4 4.6 %collective-permute-done.29 = bf16[64,16,128]{2,1,0:T(8,128)(2,1)S(1)} collective-permute-done((bf16[64,16,128]{2,1,0:T(8,128)(2,1)S(1)}, bf16[64,16,128]{2,1,0:T(8,128)(2,1)S(1)}, u32[]{:S(2)}, u32[]{:S(2)}) %collective-permute-start.29) | collective-permute-done | bytes 262176 | tf_op jit(solution)/shard_map/ppermute | solution.py:136
  117.9 3.9 %tile_sums.4 = (bf16[4,32,16,128]{3,2,1,0:T(8,128)(2,1)S(1)}, f32[4,32,16,128]{3,2,1,0:T(8,128)S(1)}) custom-call(s32[11]{0:T(128)S(1)} %stack.52.scalar, s32[512]{0:T(512)S(1)} %bitcast.222, s32[512]{0:T(512)S(1)} %bitcast.225, bf16[8,128,16,128]{3,2,1,0:T(8,128)(2,1)S(1)} %bitcast_dynamic-update-slice_fusion.18.fetched, ...), custom_call_target="tpu_custom_call" | custom-call | tf_op jit(solution)/shard_map/tile_sums/pallas_call | solution.py:57
  122.6 1.5 collective-permute-done.33
  124.4 3.2 %collective-permute-start.35 = (bf16[32,16,128]{2,1,0:T(8,128)(2,1)S(1)}, bf16[32,16,128]{2,1,0:T(8,128)(2,1)S(1)}, u32[]{:S(2)}, u32[]{:S(2)}) collective-permute-start(bf16[32,16,128]{2,1,0:T(8,128)(2,1)S(1)} %get-tuple-element.44), channel_id=1, source_target_pairs={{2,0},{3,1},{4,2},{5,3},{6,4},{7,5},{0,6},{1,7},{10,8},{11,9},{12,... | collective-permute-start | bytes 393224 | tf_op jit(solution)/shard_map/ppermute | solution.py:136
  127.6 3.2 %collective-permute-start.38 = (bf16[16,16,128]{2,1,0:T(8,128)(2,1)S(1)}, bf16[16,16,128]{2,1,0:T(8,128)(2,1)S(1)}, u32[]{:S(2)}, u32[]{:S(2)}) collective-permute-start(bf16[16,16,128]{2,1,0:T(8,128)(2,1)S(1)} %get-tuple-element.42), channel_id=1, source_target_pairs={{2,0},{3,1},{4,2},{5,3},{6,4},{7,5},{0,6},{1,7},{10,8},{11,9},{12,... | collective-permute-start | bytes 196616 | tf_op jit(solution)/shard_map/ppermute | solution.py:136
  130.9 2.2 %collective-permute-done.36 = bf16[16,16,128]{2,1,0:T(8,128)(2,1)S(1)} collective-permute-done((bf16[16,16,128]{2,1,0:T(8,128)(2,1)S(1)}, bf16[16,16,128]{2,1,0:T(8,128)(2,1)S(1)}, u32[]{:S(2)}, u32[]{:S(2)}) %collective-permute-start.36) | collective-permute-done | bytes 65568 | tf_op jit(solution)/shard_map/ppermute | solution.py:136
  133.1 3.2 %collective-permute-start.39 = (bf16[16,16,128]{2,1,0:T(8,128)(2,1)S(1)}, bf16[16,16,128]{2,1,0:T(8,128)(2,1)S(1)}, u32[]{:S(2)}, u32[]{:S(2)}) collective-permute-start(bf16[16,16,128]{2,1,0:T(8,128)(2,1)S(1)} %collective-permute-done.38), channel_id=1, source_target_pairs={{2,0},{3,1},{4,2},{5,3},{6,4},{7,5},{0,6},{1,7},{10,8},{11,9},{12,... | collective-permute-start | bytes 196616 | tf_op jit(solution)/shard_map/ppermute | solution.py:136
  136.3 2.2 %collective-permute-done.37 = bf16[16,16,128]{2,1,0:T(8,128)(2,1)S(1)} collective-permute-done((bf16[16,16,128]{2,1,0:T(8,128)(2,1)S(1)}, bf16[16,16,128]{2,1,0:T(8,128)(2,1)S(1)}, u32[]{:S(2)}, u32[]{:S(2)}) %collective-permute-start.37) | collective-permute-done | bytes 65568 | tf_op jit(solution)/shard_map/ppermute | solution.py:136
  138.6 1.0 fusion.12
  140.3 17.7 %all_to_all.34 = bf16[16,8,16,128]{3,2,1,0:T(8,128)(2,1)S(1)} all-to-all(bf16[16,8,16,128]{3,2,1,0:T(8,128)(2,1)S(1)} %bitcast.233), channel_id=1, replica_groups=mesh['rows'=16,'rep'=8] {'rows'}, dimensions={0} | all-to-all | bytes 1048576 | tf_op jit(solution)/shard_map/all_to_all | solution.py:203
  158.1 3.3 %collective-permute-start.43 = (bf16[64,16,128]{2,1,0:T(8,128)(2,1)S(1)}, bf16[64,16,128]{2,1,0:T(8,128)(2,1)S(1)}, u32[]{:S(2)}, u32[]{:S(2)}) collective-permute-start(bf16[64,16,128]{2,1,0:T(8,128)(2,1)S(1)} %bitcast.245), channel_id=1, source_target_pairs={{2,0},{3,1},{4,2},{5,3},{6,4},{7,5},{0,6},{1,7},{10,8},{11,9},{12,... | collective-permute-start | bytes 786440 | tf_op jit(solution)/shard_map/ppermute | solution.py:136
  162.1 3.4 %all-to-all-start.3 = ((bf16[8,4,2,16,128]{4,3,1,2,0:T(8,128)(2,1)}), bf16[8,4,2,16,128]{4,3,1,2,0:T(8,128)(2,1)S(1)}, u32[]{:S(2)}, u32[]{:S(2)}) async-start(bf16[8,4,2,16,128]{4,3,1,2,0:T(8,128)(2,1)} %pad_maximum_fusion), calls=%async_computation.3 | async-start | bytes 524288 | tf_op jit(solution)/shard_map/all_to_all | solution.py:200
  165.6 3.5 %load_live.5.vals = bf16[512,128,128]{2,1,0:T(8,128)(2,1)S(1)} custom-call(s32[11]{0:T(128)S(1)} %stack.52.scalar, bf16[512,128,128]{2,1,0:T(8,128)(2,1)} %bitcast.229, bf16[128,16,128]{2,1,0:T(8,128)(2,1)S(1)} %bitcast.216), custom_call_target="tpu_custom_call" | custom-call | tf_op jit(solution)/shard_map/load_live/pallas_call | solution.py:96
  169.1 1.0 collective-permute-start.45
  170.1 2.6 %collective-permute-start.47 = (bf16[64,16,128]{2,1,0:T(8,128)(2,1)S(1)}, bf16[64,16,128]{2,1,0:T(8,128)(2,1)S(1)}, u32[]{:S(2)}, u32[]{:S(2)}) collective-permute-start(bf16[64,16,128]{2,1,0:T(8,128)(2,1)S(1)} %bitcast.244), channel_id=1, source_target_pairs={{2,0},{3,1},{4,2},{5,3},{6,4},{7,5},{0,6},{1,7},{10,8},{11,9},{12,... | collective-permute-start | bytes 786440 | tf_op jit(solution)/shard_map/ppermute | solution.py:136
  173.6 3.2 %collective-permute-start.51 = (bf16[64,16,128]{2,1,0:T(8,128)(2,1)S(1)}, bf16[64,16,128]{2,1,0:T(8,128)(2,1)S(1)}, u32[]{:S(2)}, u32[]{:S(2)}) collective-permute-start(bf16[64,16,128]{2,1,0:T(8,128)(2,1)S(1)} %collective-permute-done.43), channel_id=1, source_target_pairs={{2,0},{3,1},{4,2},{5,3},{6,4},{7,5},{0,6},{1,7},{10,8},{11,9},{12,... | collective-permute-start | bytes 786440 | tf_op jit(solution)/shard_map/ppermute | solution.py:136
  176.9 2.8 %collective-permute-done.45 = bf16[64,16,128]{2,1,0:T(8,128)(2,1)S(1)} collective-permute-done((bf16[64,16,128]{2,1,0:T(8,128)(2,1)S(1)}, bf16[64,16,128]{2,1,0:T(8,128)(2,1)S(1)}, u32[]{:S(2)}, u32[]{:S(2)}) %collective-permute-start.45) | collective-permute-done | bytes 262176 | tf_op jit(solution)/shard_map/ppermute | solution.py:136
  180.4 4.8 %collective-permute-done.49 = bf16[64,16,128]{2,1,0:T(8,128)(2,1)S(1)} collective-permute-done((bf16[64,16,128]{2,1,0:T(8,128)(2,1)S(1)}, bf16[64,16,128]{2,1,0:T(8,128)(2,1)S(1)}, u32[]{:S(2)}, u32[]{:S(2)}) %collective-permute-start.49) | collective-permute-done | bytes 262176 | tf_op jit(solution)/shard_map/ppermute | solution.py:136
  187.1 3.9 %tile_sums.5 = (bf16[4,32,16,128]{3,2,1,0:T(8,128)(2,1)S(1)}, f32[4,32,16,128]{3,2,1,0:T(8,128)S(1)}) custom-call(s32[11]{0:T(128)S(1)} %stack.52.scalar, s32[512]{0:T(512)S(1)} %bitcast.223, s32[512]{0:T(512)S(1)} %bitcast.226, bf16[8,128,16,128]{3,2,1,0:T(8,128)(2,1)S(1)} %bitcast_dynamic-update-slice_fusion.6.fetched, ...), custom_call_target="tpu_custom_call" | custom-call | tf_op jit(solution)/shard_map/tile_sums/pallas_call | solution.py:57
  191.7 1.1 fusion.17
  193.5 3.2 %collective-permute-start.58 = (bf16[16,16,128]{2,1,0:T(8,128)(2,1)S(1)}, bf16[16,16,128]{2,1,0:T(8,128)(2,1)S(1)}, u32[]{:S(2)}, u32[]{:S(2)}) collective-permute-start(bf16[16,16,128]{2,1,0:T(8,128)(2,1)S(1)} %get-tuple-element.36), channel_id=1, source_target_pairs={{2,0},{3,1},{4,2},{5,3},{6,4},{7,5},{0,6},{1,7},{10,8},{11,9},{12,... | collective-permute-start | bytes 196616 | tf_op jit(solution)/shard_map/ppermute | solution.py:136
  196.8 3.2 %collective-permute-start.55 = (bf16[32,16,128]{2,1,0:T(8,128)(2,1)S(1)}, bf16[32,16,128]{2,1,0:T(8,128)(2,1)S(1)}, u32[]{:S(2)}, u32[]{:S(2)}) collective-permute-start(bf16[32,16,128]{2,1,0:T(8,128)(2,1)S(1)} %get-tuple-element.38), channel_id=1, source_target_pairs={{2,0},{3,1},{4,2},{5,3},{6,4},{7,5},{0,6},{1,7},{10,8},{11,9},{12,... | collective-permute-start | bytes 393224 | tf_op jit(solution)/shard_map/ppermute | solution.py:136
  200.1 3.2 %collective-permute-start.59 = (bf16[16,16,128]{2,1,0:T(8,128)(2,1)S(1)}, bf16[16,16,128]{2,1,0:T(8,128)(2,1)S(1)}, u32[]{:S(2)}, u32[]{:S(2)}) collective-permute-start(bf16[16,16,128]{2,1,0:T(8,128)(2,1)S(1)} %collective-permute-done.58), channel_id=1, source_target_pairs={{2,0},{3,1},{4,2},{5,3},{6,4},{7,5},{0,6},{1,7},{10,8},{11,9},{12,... | collective-permute-start | bytes 196616 | tf_op jit(solution)/shard_map/ppermute | solution.py:136
  203.6 1.9 collective-permute-done.57
  (169 shorter events, 21.1 us)
Async XLA Ops:
  1.4 15.7 %all-to-all-start = ((s32[16,1,8]{2,1,0:T(1,128)}), s32[16,1,8]{2,1,0:T(1,128)S(1)}, u32[]{:S(2)}, u32[]{:S(2)}) async-start(s32[16,1,8]{2,1,0:T(1,128)} %copy.20), calls=%async_computation | async-start | bytes 16384 | tf_op jit(solution)/shard_map/all_to_all | solution.py:186
  31.1 12.3 %collective-permute-start = (bf16[128,16,128]{2,1,0:T(8,128)(2,1)S(1)}, bf16[128,16,128]{2,1,0:T(8,128)(2,1)S(1)}, u32[]{:S(2)}, u32[]{:S(2)}) collective-permute-start(bf16[128,16,128]{2,1,0:T(8,128)(2,1)S(1)} %bitcast.212), channel_id=1, source_target_pairs={{0,1},{1,0},{2,3},{3,2},{4,5},{5,4},{6,7},{7,6},{8,9},{9,8},{10,11... | collective-permute-start | bytes 1572872 | tf_op jit(solution)/shard_map/ppermute | solution.py:139
  31.1 11.5 %collective-permute-start.1 = (bf16[64,16,128]{2,1,0:T(8,128)(2,1)S(1)}, bf16[64,16,128]{2,1,0:T(8,128)(2,1)S(1)}, u32[]{:S(2)}, u32[]{:S(2)}) collective-permute-start(bf16[64,16,128]{2,1,0:T(8,128)(2,1)S(1)} %bitcast.239), channel_id=1, source_target_pairs={{6,0},{7,1},{0,2},{1,3},{2,4},{3,5},{4,6},{5,7},{14,8},{15,9},{8,1... | collective-permute-start | bytes 786440 | tf_op jit(solution)/shard_map/ppermute | solution.py:136
  32.7 10.0 %collective-permute-start.3 = (bf16[64,16,128]{2,1,0:T(8,128)(2,1)S(1)}, bf16[64,16,128]{2,1,0:T(8,128)(2,1)S(1)}, u32[]{:S(2)}, u32[]{:S(2)}) collective-permute-start(bf16[64,16,128]{2,1,0:T(8,128)(2,1)S(1)} %bitcast.241), channel_id=1, source_target_pairs={{2,0},{3,1},{4,2},{5,3},{6,4},{7,5},{0,6},{1,7},{10,8},{11,9},{12,... | collective-permute-start | bytes 786440 | tf_op jit(solution)/shard_map/ppermute | solution.py:136
  35.2 11.6 %collective-permute-start.5 = (bf16[64,16,128]{2,1,0:T(8,128)(2,1)S(1)}, bf16[64,16,128]{2,1,0:T(8,128)(2,1)S(1)}, u32[]{:S(2)}, u32[]{:S(2)}) collective-permute-start(bf16[64,16,128]{2,1,0:T(8,128)(2,1)S(1)} %bitcast.242), channel_id=1, source_target_pairs={{6,0},{7,1},{0,2},{1,3},{2,4},{3,5},{4,6},{5,7},{14,8},{15,9},{8,1... | collective-permute-start | bytes 786440 | tf_op jit(solution)/shard_map/ppermute | solution.py:136
  35.5 12.0 %collective-permute-start.7 = (bf16[64,16,128]{2,1,0:T(8,128)(2,1)S(1)}, bf16[64,16,128]{2,1,0:T(8,128)(2,1)S(1)}, u32[]{:S(2)}, u32[]{:S(2)}) collective-permute-start(bf16[64,16,128]{2,1,0:T(8,128)(2,1)S(1)} %bitcast.240), channel_id=1, source_target_pairs={{2,0},{3,1},{4,2},{5,3},{6,4},{7,5},{0,6},{1,7},{10,8},{11,9},{12,... | collective-permute-start | bytes 786440 | tf_op jit(solution)/shard_map/ppermute | solution.py:136
  42.7 9.9 %collective-permute-start.9 = (bf16[64,16,128]{2,1,0:T(8,128)(2,1)S(1)}, bf16[64,16,128]{2,1,0:T(8,128)(2,1)S(1)}, u32[]{:S(2)}, u32[]{:S(2)}) collective-permute-start(bf16[64,16,128]{2,1,0:T(8,128)(2,1)S(1)} %collective-permute-done.1), channel_id=1, source_target_pairs={{6,0},{7,1},{0,2},{1,3},{2,4},{3,5},{4,6},{5,7},{14,8},{15,9},{8,1... | collective-permute-start | bytes 786440 | tf_op jit(solution)/shard_map/ppermute | solution.py:136
  43.4 9.3 %collective-permute-start.11 = (bf16[64,16,128]{2,1,0:T(8,128)(2,1)S(1)}, bf16[64,16,128]{2,1,0:T(8,128)(2,1)S(1)}, u32[]{:S(2)}, u32[]{:S(2)}) collective-permute-start(bf16[64,16,128]{2,1,0:T(8,128)(2,1)S(1)} %collective-permute-done.3), channel_id=1, source_target_pairs={{2,0},{3,1},{4,2},{5,3},{6,4},{7,5},{0,6},{1,7},{10,8},{11,9},{12,... | collective-permute-start | bytes 786440 | tf_op jit(solution)/shard_map/ppermute | solution.py:136
  46.7 6.5 %collective-permute-start.4 = (bf16[64,16,128]{2,1,0:T(8,128)(2,1)S(1)}, bf16[64,16,128]{2,1,0:T(8,128)(2,1)S(1)}, u32[]{:S(2)}, u32[]{:S(2)}) collective-permute-start(bf16[64,16,128]{2,1,0:T(8,128)(2,1)S(1)} %collective-permute-done.3), channel_id=1, source_target_pairs={{0,1},{1,0},{2,3},{3,2},{4,5},{5,4},{6,7},{7,6},{8,9},{9,8},{10,11... | collective-permute-start | bytes 786440 | tf_op jit(solution)/shard_map/ppermute | solution.py:139
  47.5 5.9 %collective-permute-start.6 = (bf16[64,16,128]{2,1,0:T(8,128)(2,1)S(1)}, bf16[64,16,128]{2,1,0:T(8,128)(2,1)S(1)}, u32[]{:S(2)}, u32[]{:S(2)}) collective-permute-start(bf16[64,16,128]{2,1,0:T(8,128)(2,1)S(1)} %collective-permute-done.5), channel_id=1, source_target_pairs={{0,1},{1,0},{2,3},{3,2},{4,5},{5,4},{6,7},{7,6},{8,9},{9,8},{10,11... | collective-permute-start | bytes 786440 | tf_op jit(solution)/shard_map/ppermute | solution.py:139
  47.5 6.0 %collective-permute-start.8 = (bf16[64,16,128]{2,1,0:T(8,128)(2,1)S(1)}, bf16[64,16,128]{2,1,0:T(8,128)(2,1)S(1)}, u32[]{:S(2)}, u32[]{:S(2)}) collective-permute-start(bf16[64,16,128]{2,1,0:T(8,128)(2,1)S(1)} %collective-permute-done.7), channel_id=1, source_target_pairs={{0,1},{1,0},{2,3},{3,2},{4,5},{5,4},{6,7},{7,6},{8,9},{9,8},{10,11... | collective-permute-start | bytes 786440 | tf_op jit(solution)/shard_map/ppermute | solution.py:139
  61.0 12.0 %collective-permute-start.14 = (bf16[32,16,128]{2,1,0:T(8,128)(2,1)S(1)}, bf16[32,16,128]{2,1,0:T(8,128)(2,1)S(1)}, u32[]{:S(2)}, u32[]{:S(2)}) collective-permute-start(bf16[32,16,128]{2,1,0:T(8,128)(2,1)S(1)} %get-tuple-element.49), channel_id=1, source_target_pairs={{6,0},{7,1},{0,2},{1,3},{2,4},{3,5},{4,6},{5,7},{14,8},{15,9},{8,1... | collective-permute-start | bytes 393224 | tf_op jit(solution)/shard_map/ppermute | solution.py:136
  61.1 11.9 %collective-permute-start.15 = (bf16[32,16,128]{2,1,0:T(8,128)(2,1)S(1)}, bf16[32,16,128]{2,1,0:T(8,128)(2,1)S(1)}, u32[]{:S(2)}, u32[]{:S(2)}) collective-permute-start(bf16[32,16,128]{2,1,0:T(8,128)(2,1)S(1)} %get-tuple-element.50), channel_id=1, source_target_pairs={{2,0},{3,1},{4,2},{5,3},{6,4},{7,5},{0,6},{1,7},{10,8},{11,9},{12,... | collective-permute-start | bytes 393224 | tf_op jit(solution)/shard_map/ppermute | solution.py:136
  64.3 5.5 %collective-permute-start.16 = (bf16[16,16,128]{2,1,0:T(8,128)(2,1)S(1)}, bf16[16,16,128]{2,1,0:T(8,128)(2,1)S(1)}, u32[]{:S(2)}, u32[]{:S(2)}) collective-permute-start(bf16[16,16,128]{2,1,0:T(8,128)(2,1)S(1)} %get-tuple-element.47), channel_id=1, source_target_pairs={{6,0},{7,1},{0,2},{1,3},{2,4},{3,5},{4,6},{5,7},{14,8},{15,9},{8,1... | collective-permute-start | bytes 196616 | tf_op jit(solution)/shard_map/ppermute | solution.py:136
  64.3 5.5 %collective-permute-start.18 = (bf16[16,16,128]{2,1,0:T(8,128)(2,1)S(1)}, bf16[16,16,128]{2,1,0:T(8,128)(2,1)S(1)}, u32[]{:S(2)}, u32[]{:S(2)}) collective-permute-start(bf16[16,16,128]{2,1,0:T(8,128)(2,1)S(1)} %get-tuple-element.48), channel_id=1, source_target_pairs={{2,0},{3,1},{4,2},{5,3},{6,4},{7,5},{0,6},{1,7},{10,8},{11,9},{12,... | collective-permute-start | bytes 196616 | tf_op jit(solution)/shard_map/ppermute | solution.py:136
  69.8 5.5 %collective-permute-start.17 = (bf16[16,16,128]{2,1,0:T(8,128)(2,1)S(1)}, bf16[16,16,128]{2,1,0:T(8,128)(2,1)S(1)}, u32[]{:S(2)}, u32[]{:S(2)}) collective-permute-start(bf16[16,16,128]{2,1,0:T(8,128)(2,1)S(1)} %collective-permute-done.16), channel_id=1, source_target_pairs={{6,0},{7,1},{0,2},{1,3},{2,4},{3,5},{4,6},{5,7},{14,8},{15,9},{8,1... | collective-permute-start | bytes 196616 | tf_op jit(solution)/shard_map/ppermute | solution.py:136
  93.4 11.5 %collective-permute-start.20 = (bf16[128,16,128]{2,1,0:T(8,128)(2,1)S(1)}, bf16[128,16,128]{2,1,0:T(8,128)(2,1)S(1)}, u32[]{:S(2)}, u32[]{:S(2)}) collective-permute-start(bf16[128,16,128]{2,1,0:T(8,128)(2,1)S(1)} %bitcast.218), channel_id=1, source_target_pairs={{0,1},{1,0},{2,3},{3,2},{4,5},{5,4},{6,7},{7,6},{8,9},{9,8},{10,11... | collective-permute-start | bytes 1572872 | tf_op jit(solution)/shard_map/ppermute | solution.py:139
  93.5 10.8 %collective-permute-start.21 = (bf16[64,16,128]{2,1,0:T(8,128)(2,1)S(1)}, bf16[64,16,128]{2,1,0:T(8,128)(2,1)S(1)}, u32[]{:S(2)}, u32[]{:S(2)}) collective-permute-start(bf16[64,16,128]{2,1,0:T(8,128)(2,1)S(1)} %bitcast.247), channel_id=1, source_target_pairs={{6,0},{7,1},{0,2},{1,3},{2,4},{3,5},{4,6},{5,7},{14,8},{15,9},{8,1... | collective-permute-start | bytes 786440 | tf_op jit(solution)/shard_map/ppermute | solution.py:136
  93.6 10.8 %collective-permute-start.23 = (bf16[64,16,128]{2,1,0:T(8,128)(2,1)S(1)}, bf16[64,16,128]{2,1,0:T(8,128)(2,1)S(1)}, u32[]{:S(2)}, u32[]{:S(2)}) collective-permute-start(bf16[64,16,128]{2,1,0:T(8,128)(2,1)S(1)} %bitcast.249), channel_id=1, source_target_pairs={{2,0},{3,1},{4,2},{5,3},{6,4},{7,5},{0,6},{1,7},{10,8},{11,9},{12,... | collective-permute-start | bytes 786440 | tf_op jit(solution)/shard_map/ppermute | solution.py:136
  100.4 10.5 %collective-permute-start.25 = (bf16[64,16,128]{2,1,0:T(8,128)(2,1)S(1)}, bf16[64,16,128]{2,1,0:T(8,128)(2,1)S(1)}, u32[]{:S(2)}, u32[]{:S(2)}) collective-permute-start(bf16[64,16,128]{2,1,0:T(8,128)(2,1)S(1)} %bitcast.250), channel_id=1, source_target_pairs={{6,0},{7,1},{0,2},{1,3},{2,4},{3,5},{4,6},{5,7},{14,8},{15,9},{8,1... | collective-permute-start | bytes 786440 | tf_op jit(solution)/shard_map/ppermute | solution.py:136
  100.4 10.4 %collective-permute-start.27 = (bf16[64,16,128]{2,1,0:T(8,128)(2,1)S(1)}, bf16[64,16,128]{2,1,0:T(8,128)(2,1)S(1)}, u32[]{:S(2)}, u32[]{:S(2)}) collective-permute-start(bf16[64,16,128]{2,1,0:T(8,128)(2,1)S(1)} %bitcast.248), channel_id=1, source_target_pairs={{2,0},{3,1},{4,2},{5,3},{6,4},{7,5},{0,6},{1,7},{10,8},{11,9},{12,... | collective-permute-start | bytes 786440 | tf_op jit(solution)/shard_map/ppermute | solution.py:136
  104.3 7.0 %collective-permute-start.22 = (bf16[64,16,128]{2,1,0:T(8,128)(2,1)S(1)}, bf16[64,16,128]{2,1,0:T(8,128)(2,1)S(1)}, u32[]{:S(2)}, u32[]{:S(2)}) collective-permute-start(bf16[64,16,128]{2,1,0:T(8,128)(2,1)S(1)} %collective-permute-done.21), channel_id=1, source_target_pairs={{0,1},{1,0},{2,3},{3,2},{4,5},{5,4},{6,7},{7,6},{8,9},{9,8},{10,11... | collective-permute-start | bytes 786440 | tf_op jit(solution)/shard_map/ppermute | solution.py:139
  104.4 11.6 %collective-permute-start.29 = (bf16[64,16,128]{2,1,0:T(8,128)(2,1)S(1)}, bf16[64,16,128]{2,1,0:T(8,128)(2,1)S(1)}, u32[]{:S(2)}, u32[]{:S(2)}) collective-permute-start(bf16[64,16,128]{2,1,0:T(8,128)(2,1)S(1)} %collective-permute-done.21), channel_id=1, source_target_pairs={{6,0},{7,1},{0,2},{1,3},{2,4},{3,5},{4,6},{5,7},{14,8},{15,9},{8,1... | collective-permute-start | bytes 786440 | tf_op jit(solution)/shard_map/ppermute | solution.py:136
  104.9 11.1 %collective-permute-start.31 = (bf16[64,16,128]{2,1,0:T(8,128)(2,1)S(1)}, bf16[64,16,128]{2,1,0:T(8,128)(2,1)S(1)}, u32[]{:S(2)}, u32[]{:S(2)}) collective-permute-start(bf16[64,16,128]{2,1,0:T(8,128)(2,1)S(1)} %collective-permute-done.23), channel_id=1, source_target_pairs={{2,0},{3,1},{4,2},{5,3},{6,4},{7,5},{0,6},{1,7},{10,8},{11,9},{12,... | collective-permute-start | bytes 786440 | tf_op jit(solution)/shard_map/ppermute | solution.py:136
  110.8 5.8 %collective-permute-start.24 = (bf16[64,16,128]{2,1,0:T(8,128)(2,1)S(1)}, bf16[64,16,128]{2,1,0:T(8,128)(2,1)S(1)}, u32[]{:S(2)}, u32[]{:S(2)}) collective-permute-start(bf16[64,16,128]{2,1,0:T(8,128)(2,1)S(1)} %collective-permute-done.23), channel_id=1, source_target_pairs={{0,1},{1,0},{2,3},{3,2},{4,5},{5,4},{6,7},{7,6},{8,9},{9,8},{10,11... | collective-permute-start | bytes 786440 | tf_op jit(solution)/shard_map/ppermute | solution.py:139
  110.8 5.9 %collective-permute-start.26 = (bf16[64,16,128]{2,1,0:T(8,128)(2,1)S(1)}, bf16[64,16,128]{2,1,0:T(8,128)(2,1)S(1)}, u32[]{:S(2)}, u32[]{:S(2)}) collective-permute-start(bf16[64,16,128]{2,1,0:T(8,128)(2,1)S(1)} %collective-permute-done.25), channel_id=1, source_target_pairs={{0,1},{1,0},{2,3},{3,2},{4,5},{5,4},{6,7},{7,6},{8,9},{9,8},{10,11... | collective-permute-start | bytes 786440 | tf_op jit(solution)/shard_map/ppermute | solution.py:139
  111.3 5.5 %collective-permute-start.28 = (bf16[64,16,128]{2,1,0:T(8,128)(2,1)S(1)}, bf16[64,16,128]{2,1,0:T(8,128)(2,1)S(1)}, u32[]{:S(2)}, u32[]{:S(2)}) collective-permute-start(bf16[64,16,128]{2,1,0:T(8,128)(2,1)S(1)} %collective-permute-done.27), channel_id=1, source_target_pairs={{0,1},{1,0},{2,3},{3,2},{4,5},{5,4},{6,7},{7,6},{8,9},{9,8},{10,11... | collective-permute-start | bytes 786440 | tf_op jit(solution)/shard_map/ppermute | solution.py:139
  124.3 12.0 %collective-permute-start.34 = (bf16[32,16,128]{2,1,0:T(8,128)(2,1)S(1)}, bf16[32,16,128]{2,1,0:T(8,128)(2,1)S(1)}, u32[]{:S(2)}, u32[]{:S(2)}) collective-permute-start(bf16[32,16,128]{2,1,0:T(8,128)(2,1)S(1)} %get-tuple-element.43), channel_id=1, source_target_pairs={{6,0},{7,1},{0,2},{1,3},{2,4},{3,5},{4,6},{5,7},{14,8},{15,9},{8,1... | collective-permute-start | bytes 393224 | tf_op jit(solution)/shard_map/ppermute | solution.py:136
  124.4 11.9 %collective-permute-start.35 = (bf16[32,16,128]{2,1,0:T(8,128)(2,1)S(1)}, bf16[32,16,128]{2,1,0:T(8,128)(2,1)S(1)}, u32[]{:S(2)}, u32[]{:S(2)}) collective-permute-start(bf16[32,16,128]{2,1,0:T(8,128)(2,1)S(1)} %get-tuple-element.44), channel_id=1, source_target_pairs={{2,0},{3,1},{4,2},{5,3},{6,4},{7,5},{0,6},{1,7},{10,8},{11,9},{12,... | collective-permute-start | bytes 393224 | tf_op jit(solution)/shard_map/ppermute | solution.py:136
  127.6 5.5 %collective-permute-start.36 = (bf16[16,16,128]{2,1,0:T(8,128)(2,1)S(1)}, bf16[16,16,128]{2,1,0:T(8,128)(2,1)S(1)}, u32[]{:S(2)}, u32[]{:S(2)}) collective-permute-start(bf16[16,16,128]{2,1,0:T(8,128)(2,1)S(1)} %get-tuple-element.41), channel_id=1, source_target_pairs={{6,0},{7,1},{0,2},{1,3},{2,4},{3,5},{4,6},{5,7},{14,8},{15,9},{8,1... | collective-permute-start | bytes 196616 | tf_op jit(solution)/shard_map/ppermute | solution.py:136
  127.6 5.5 %collective-permute-start.38 = (bf16[16,16,128]{2,1,0:T(8,128)(2,1)S(1)}, bf16[16,16,128]{2,1,0:T(8,128)(2,1)S(1)}, u32[]{:S(2)}, u32[]{:S(2)}) collective-permute-start(bf16[16,16,128]{2,1,0:T(8,128)(2,1)S(1)} %get-tuple-element.42), channel_id=1, source_target_pairs={{2,0},{3,1},{4,2},{5,3},{6,4},{7,5},{0,6},{1,7},{10,8},{11,9},{12,... | collective-permute-start | bytes 196616 | tf_op jit(solution)/shard_map/ppermute | solution.py:136
  158.0 15.6 %collective-permute-start.40 = (bf16[128,16,128]{2,1,0:T(8,128)(2,1)S(1)}, bf16[128,16,128]{2,1,0:T(8,128)(2,1)S(1)}, u32[]{:S(2)}, u32[]{:S(2)}) collective-permute-start(bf16[128,16,128]{2,1,0:T(8,128)(2,1)S(1)} %bitcast.215), channel_id=1, source_target_pairs={{0,1},{1,0},{2,3},{3,2},{4,5},{5,4},{6,7},{7,6},{8,9},{9,8},{10,11... | collective-permute-start | bytes 1572872 | tf_op jit(solution)/shard_map/ppermute | solution.py:139
  158.0 15.3 %collective-permute-start.41 = (bf16[64,16,128]{2,1,0:T(8,128)(2,1)S(1)}, bf16[64,16,128]{2,1,0:T(8,128)(2,1)S(1)}, u32[]{:S(2)}, u32[]{:S(2)}) collective-permute-start(bf16[64,16,128]{2,1,0:T(8,128)(2,1)S(1)} %bitcast.243), channel_id=1, source_target_pairs={{6,0},{7,1},{0,2},{1,3},{2,4},{3,5},{4,6},{5,7},{14,8},{15,9},{8,1... | collective-permute-start | bytes 786440 | tf_op jit(solution)/shard_map/ppermute | solution.py:136
  158.1 15.4 %collective-permute-start.43 = (bf16[64,16,128]{2,1,0:T(8,128)(2,1)S(1)}, bf16[64,16,128]{2,1,0:T(8,128)(2,1)S(1)}, u32[]{:S(2)}, u32[]{:S(2)}) collective-permute-start(bf16[64,16,128]{2,1,0:T(8,128)(2,1)S(1)} %bitcast.245), channel_id=1, source_target_pairs={{2,0},{3,1},{4,2},{5,3},{6,4},{7,5},{0,6},{1,7},{10,8},{11,9},{12,... | collective-permute-start | bytes 786440 | tf_op jit(solution)/shard_map/ppermute | solution.py:136
  162.1 30.6 %all-to-all-start.3 = ((bf16[8,4,2,16,128]{4,3,1,2,0:T(8,128)(2,1)}), bf16[8,4,2,16,128]{4,3,1,2,0:T(8,128)(2,1)S(1)}, u32[]{:S(2)}, u32[]{:S(2)}) async-start(bf16[8,4,2,16,128]{4,3,1,2,0:T(8,128)(2,1)} %pad_maximum_fusion), calls=%async_computation.3 | async-start | bytes 524288 | tf_op jit(solution)/shard_map/all_to_all | solution.py:200
  169.1 10.7 %collective-permute-start.45 = (bf16[64,16,128]{2,1,0:T(8,128)(2,1)S(1)}, bf16[64,16,128]{2,1,0:T(8,128)(2,1)S(1)}, u32[]{:S(2)}, u32[]{:S(2)}) collective-permute-start(bf16[64,16,128]{2,1,0:T(8,128)(2,1)S(1)} %bitcast.246), channel_id=1, source_target_pairs={{6,0},{7,1},{0,2},{1,3},{2,4},{3,5},{4,6},{5,7},{14,8},{15,9},{8,1... | collective-permute-start | bytes 786440 | tf_op jit(solution)/shard_map/ppermute | solution.py:136
  170.1 9.7 %collective-permute-start.47 = (bf16[64,16,128]{2,1,0:T(8,128)(2,1)S(1)}, bf16[64,16,128]{2,1,0:T(8,128)(2,1)S(1)}, u32[]{:S(2)}, u32[]{:S(2)}) collective-permute-start(bf16[64,16,128]{2,1,0:T(8,128)(2,1)S(1)} %bitcast.244), channel_id=1, source_target_pairs={{2,0},{3,1},{4,2},{5,3},{6,4},{7,5},{0,6},{1,7},{10,8},{11,9},{12,... | collective-permute-start | bytes 786440 | tf_op jit(solution)/shard_map/ppermute | solution.py:136
  173.3 7.0 %collective-permute-start.42 = (bf16[64,16,128]{2,1,0:T(8,128)(2,1)S(1)}, bf16[64,16,128]{2,1,0:T(8,128)(2,1)S(1)}, u32[]{:S(2)}, u32[]{:S(2)}) collective-permute-start(bf16[64,16,128]{2,1,0:T(8,128)(2,1)S(1)} %collective-permute-done.41), channel_id=1, source_target_pairs={{0,1},{1,0},{2,3},{3,2},{4,5},{5,4},{6,7},{7,6},{8,9},{9,8},{10,11... | collective-permute-start | bytes 786440 | tf_op jit(solution)/shard_map/ppermute | solution.py:139
  173.6 11.6 %collective-permute-start.49 = (bf16[64,16,128]{2,1,0:T(8,128)(2,1)S(1)}, bf16[64,16,128]{2,1,0:T(8,128)(2,1)S(1)}, u32[]{:S(2)}, u32[]{:S(2)}) collective-permute-start(bf16[64,16,128]{2,1,0:T(8,128)(2,1)S(1)} %collective-permute-done.41), channel_id=1, source_target_pairs={{6,0},{7,1},{0,2},{1,3},{2,4},{3,5},{4,6},{5,7},{14,8},{15,9},{8,1... | collective-permute-start | bytes 786440 | tf_op jit(solution)/shard_map/ppermute | solution.py:136
  173.6 11.6 %collective-permute-start.51 = (bf16[64,16,128]{2,1,0:T(8,128)(2,1)S(1)}, bf16[64,16,128]{2,1,0:T(8,128)(2,1)S(1)}, u32[]{:S(2)}, u32[]{:S(2)}) collective-permute-start(bf16[64,16,128]{2,1,0:T(8,128)(2,1)S(1)} %collective-permute-done.43), channel_id=1, source_target_pairs={{2,0},{3,1},{4,2},{5,3},{6,4},{7,5},{0,6},{1,7},{10,8},{11,9},{12,... | collective-permute-start | bytes 786440 | tf_op jit(solution)/shard_map/ppermute | solution.py:136
  179.8 6.0 %collective-permute-start.44 = (bf16[64,16,128]{2,1,0:T(8,128)(2,1)S(1)}, bf16[64,16,128]{2,1,0:T(8,128)(2,1)S(1)}, u32[]{:S(2)}, u32[]{:S(2)}) collective-permute-start(bf16[64,16,128]{2,1,0:T(8,128)(2,1)S(1)} %collective-permute-done.43), channel_id=1, source_target_pairs={{0,1},{1,0},{2,3},{3,2},{4,5},{5,4},{6,7},{7,6},{8,9},{9,8},{10,11... | collective-permute-start | bytes 786440 | tf_op jit(solution)/shard_map/ppermute | solution.py:139
  179.8 6.1 %collective-permute-start.46 = (bf16[64,16,128]{2,1,0:T(8,128)(2,1)S(1)}, bf16[64,16,128]{2,1,0:T(8,128)(2,1)S(1)}, u32[]{:S(2)}, u32[]{:S(2)}) collective-permute-start(bf16[64,16,128]{2,1,0:T(8,128)(2,1)S(1)} %collective-permute-done.45), channel_id=1, source_target_pairs={{0,1},{1,0},{2,3},{3,2},{4,5},{5,4},{6,7},{7,6},{8,9},{9,8},{10,11... | collective-permute-start | bytes 786440 | tf_op jit(solution)/shard_map/ppermute | solution.py:139
  180.3 5.7 %collective-permute-start.48 = (bf16[64,16,128]{2,1,0:T(8,128)(2,1)S(1)}, bf16[64,16,128]{2,1,0:T(8,128)(2,1)S(1)}, u32[]{:S(2)}, u32[]{:S(2)}) collective-permute-start(bf16[64,16,128]{2,1,0:T(8,128)(2,1)S(1)} %collective-permute-done.47), channel_id=1, source_target_pairs={{0,1},{1,0},{2,3},{3,2},{4,5},{5,4},{6,7},{7,6},{8,9},{9,8},{10,11... | collective-permute-start | bytes 786440 | tf_op jit(solution)/shard_map/ppermute | solution.py:139
  193.4 6.6 %collective-permute-start.56 = (bf16[16,16,128]{2,1,0:T(8,128)(2,1)S(1)}, bf16[16,16,128]{2,1,0:T(8,128)(2,1)S(1)}, u32[]{:S(2)}, u32[]{:S(2)}) collective-permute-start(bf16[16,16,128]{2,1,0:T(8,128)(2,1)S(1)} %get-tuple-element.35), channel_id=1, source_target_pairs={{6,0},{7,1},{0,2},{1,3},{2,4},{3,5},{4,6},{5,7},{14,8},{15,9},{8,1... | collective-permute-start | bytes 196616 | tf_op jit(solution)/shard_map/ppermute | solution.py:136
  193.5 6.6 %collective-permute-start.58 = (bf16[16,16,128]{2,1,0:T(8,128)(2,1)S(1)}, bf16[16,16,128]{2,1,0:T(8,128)(2,1)S(1)}, u32[]{:S(2)}, u32[]{:S(2)}) collective-permute-start(bf16[16,16,128]{2,1,0:T(8,128)(2,1)S(1)} %get-tuple-element.36), channel_id=1, source_target_pairs={{2,0},{3,1},{4,2},{5,3},{6,4},{7,5},{0,6},{1,7},{10,8},{11,9},{12,... | collective-permute-start | bytes 196616 | tf_op jit(solution)/shard_map/ppermute | solution.py:136
  196.7 6.9 %collective-permute-start.54 = (bf16[32,16,128]{2,1,0:T(8,128)(2,1)S(1)}, bf16[32,16,128]{2,1,0:T(8,128)(2,1)S(1)}, u32[]{:S(2)}, u32[]{:S(2)}) collective-permute-start(bf16[32,16,128]{2,1,0:T(8,128)(2,1)S(1)} %get-tuple-element.37), channel_id=1, source_target_pairs={{6,0},{7,1},{0,2},{1,3},{2,4},{3,5},{4,6},{5,7},{14,8},{15,9},{8,1... | collective-permute-start | bytes 393224 | tf_op jit(solution)/shard_map/ppermute | solution.py:136
  196.8 6.8 %collective-permute-start.55 = (bf16[32,16,128]{2,1,0:T(8,128)(2,1)S(1)}, bf16[32,16,128]{2,1,0:T(8,128)(2,1)S(1)}, u32[]{:S(2)}, u32[]{:S(2)}) collective-permute-start(bf16[32,16,128]{2,1,0:T(8,128)(2,1)S(1)} %get-tuple-element.38), channel_id=1, source_target_pairs={{2,0},{3,1},{4,2},{5,3},{6,4},{7,5},{0,6},{1,7},{10,8},{11,9},{12,... | collective-permute-start | bytes 393224 | tf_op jit(solution)/shard_map/ppermute | solution.py:136
  200.0 5.5 %collective-permute-start.57 = (bf16[16,16,128]{2,1,0:T(8,128)(2,1)S(1)}, bf16[16,16,128]{2,1,0:T(8,128)(2,1)S(1)}, u32[]{:S(2)}, u32[]{:S(2)}) collective-permute-start(bf16[16,16,128]{2,1,0:T(8,128)(2,1)S(1)} %collective-permute-done.56), channel_id=1, source_target_pairs={{6,0},{7,1},{0,2},{1,3},{2,4},{3,5},{4,6},{5,7},{14,8},{15,9},{8,1... | collective-permute-start | bytes 196616 | tf_op jit(solution)/shard_map/ppermute | solution.py:136
  (17 other events, 72.6 us)
where the time goes:
time: 207 us
  starting transfers between devices  76.9 us (37%)
  blocking collectives  48.1 us (23%)
  waiting for transfers between devices  44.7 us (22%)
  Pallas kernels  22.2 us (11%)
  local copies, waits for them, and re-layouts  8.44 us (4%)
  matrix products  2.45 us (1%)
  other arithmetic  2.4 us (1%)
    ppermute x36, starting transfers between devices, along(): lax.ppermute(x, 'rep', [((i + step) % replicas, i) for i in range(replica...  59.5 us
    all_to_all x3, blocking collectives, step(): lax.all_to_all(terms[-1][served], 'rows', split_axis=0, concat_axis=0, ti...  48.1 us
    ppermute x36, waiting for transfers between devices, along(): lax.ppermute(x, 'rep', [((i + step) % replicas, i) for i in range(replica...  32.1 us
    pallas_call x3, Pallas kernels, tile_sums(): pl.pallas_call(body, out_shape=(pltpu.VMEM(shape, jnp.bfloat16), pltpu.VM...  11.6 us
    pallas_call x3, Pallas kernels, load_live(): pl.pallas_call(body, out_shape=pltpu.VMEM(values.shape, values.dtype), in...  10.5 us
    all_to_all x1, starting transfers between devices, on_device(): lax.all_to_all(wanted, 'rows', split_axis=0, concat_axis=0, tiled=True)  8.16 us
    all_to_all x1, waiting for transfers between devices, on_device(): lax.all_to_all(wanted, 'rows', split_axis=0, concat_axis=0, tiled=True)  6.58 us
    ppermute x24, waiting for transfers between devices, partner(): return lax.ppermute(x, 'rep', [(i, i ^ 1) for i in range(replicas)])  5.95 us
  transfers between devices with their start and end apart: 62, of which 23 were waited for; matrix products, arithmetic and copies ran while one was open for 3% of the time, Pallas kernels for 7%

commit v1 on v0

--- a/solution.py
+++ b/solution.py
@@ -141,13 +141,9 @@
     def gather(sent):
         slots = sent.shape[0]
         half = slots // 2
-        low, high = sent[:half], sent[half:]
-        before_low, after_high = along(low, -1), along(high, 1)
-        before_high, after_low = along(high, -1), along(low, 1)
-        other = partner(sent)
+        before, after, other = along(sent, -1), along(sent, 1), partner(sent)
+        first, second = along(before[:half], -1), along(after[half:], 1)
         live = load_live(values, scalars, sent)
-        before_low, live = lax.optimization_barrier((before_low, live))
-        far_low, far_high = along(before_low, -1), along(after_high, 1)
         fetched = jnp.zeros((replicas, slots, sub, width), sent.dtype)
 
         def put(fetched, array, hops, other_core, start):
@@ -158,26 +154,35 @@
 
         fetched = put(fetched, sent, 0, 0, 0)
         fetched = put(fetched, other, 0, 1, 0)
-        for array, hops, start in (
-            (before_low, -1, 0),
-            (after_high, 1, half),
-            (before_high, -1, half),
-            (after_low, 1, 0),
-            (far_low, 2, 0),
-            (far_high, 2, half),
-        ):
+        for array, hops, start in ((before, -1, 0), (after, 1, 0), (first, 2, 0), (second, 2, half)):
             fetched = put(fetched, array, hops, 0, start)
-            crossed = partner(array)
-            fetched = put(fetched, crossed, hops, 1, start)
+            fetched = put(fetched, partner(array), hops, 1, start)
         return fetched, live
 
-    def reduce(peer, mine):
+    def reduce(peer, mine, degree):
         sums = mine + partner(peer).astype(jnp.float32)
-        sent = [sums[hops].astype(jnp.bfloat16) for hops in range(chips)]
-        half = row_blocks // 2
-        low, high = along(sent[2][:half], -1), along(sent[2][half:], 1)
-        parts = [along(sent[1], -1), along(sent[3], 1)]
-        parts.append(jnp.concatenate([along(low, -1), along(high, 1)], 0))
+        sent = sums.astype(jnp.bfloat16)
+        if degree == 1:
+            order = (jnp.arange(chips) - chip) % chips
+            groups = [list(range(c, replicas, CORES)) for c in range(CORES)]
+            moved = lax.all_to_all(
+                sent[order], "rep", split_axis=0, concat_axis=0, axis_index_groups=groups, tiled=True
+            )
+            total = sums[0]
+            for place in range(chips):
+                part = moved[place].astype(jnp.float32)
+                total = total + jnp.where(place == chip, jnp.zeros_like(part), part)
+            return total
+        if degree == 2:
+            parts = [along(sent[hops], -hops) for hops in range(1, chips)]
+        else:
+            half = row_blocks // 2
+            low = along(jnp.concatenate([sent[1], sent[2][:half]], 0), -1)
+            high = along(jnp.concatenate([sent[3], sent[2][half:]], 0), 1)
+            parts = [low[:row_blocks], high[:row_blocks]]
+            parts.append(
+                jnp.concatenate([along(low[row_blocks:], -1), along(high[row_blocks:], 1)], 0)
+            )
         total = sums[0]
         for part in parts:
             total = total + part.astype(jnp.float32)
@@ -207,7 +212,7 @@
         peer, mine = tile_sums(
             fetched, live, rows_of, slots_of, scalars, row_blocks, whole_blocks=last
         )
-        total = reduce(peer, mine)
+        total = reduce(peer, mine, degree)
         if last:
             total = total.reshape(share_rows, width)
             before = own[-2]

time: 207 us -> 230 us (1.11)
  waiting for transfers between devices: 44.7 us -> 88.1 us
  starting transfers between devices: 76.9 us -> 52.7 us
    ppermute x36 -> x19, starting transfers between devices: 59.5 us -> 31.1 us  [along(): lax.ppermute(x, 'rep', [((i + step) % replicas, i) for i in range(replica...]
    ppermute x36 -> x19, waiting for transfers between devices: 32.1 us -> 59 us  [along(): lax.ppermute(x, 'rep', [((i + step) % replicas, i) for i in range(replica...]
    all_to_all x0 -> x1, waiting for transfers between devices: none -> 10 us  [reduce(): lax.all_to_all(sent[order], 'rep', split_axis=0, concat_axis=0, axis_inde...]
    all_to_all x1, waiting for transfers between devices: 0.01 us -> 6.38 us  [step(): lax.all_to_all(swapped, 'rep', split_axis=0, concat_axis=0, tiled=True)]
    all_to_all x0 -> x1, starting transfers between devices: none -> 4.43 us  [reduce(): lax.all_to_all(sent[order], 'rep', split_axis=0, concat_axis=0, axis_inde...]
    ppermute x24 -> x18, starting transfers between devices: 5.79 us -> 4.56 us  [partner(): return lax.ppermute(x, 'rep', [(i, i ^ 1) for i in range(replicas)])]
    ppermute x24 -> x18, waiting for transfers between devices: 5.95 us -> 6.1 us  [partner(): return lax.ppermute(x, 'rep', [(i, i ^ 1) for i in range(replicas)])]
  transfers between devices with their start and end apart: 62 -> 40, of which waited for: 23 -> 21; matrix products, arithmetic and copies ran while one was open for 3% -> 3% of each run, Pallas kernels for 7% -> 5%
where the time goes in v1:
time: 230 us; the launch traced here: 229 us
  waiting for transfers between devices  88.1 us (38%)
  starting transfers between devices  52.7 us (23%)
  blocking collectives  49.8 us (22%)
  Pallas kernels  22.1 us (10%)
  local copies, waits for them, and re-layouts  9.75 us (4%)
  other arithmetic  2.49 us (1%)
  matrix products  2.44 us (1%)
    ppermute x19, waiting for transfers between devices, along(): lax.ppermute(x, 'rep', [((i + step) % replicas, i) for i in range(replica...  59 us
    all_to_all x3, blocking collectives, step(): lax.all_to_all(terms[-1][served], 'rows', split_axis=0, concat_axis=0, ti...  49.8 us
    ppermute x19, starting transfers between devices, along(): lax.ppermute(x, 'rep', [((i + step) % replicas, i) for i in range(replica...  31.1 us
    pallas_call x3, Pallas kernels, tile_sums(): pl.pallas_call(body, out_shape=(pltpu.VMEM(shape, jnp.bfloat16), pltpu.VM...  11.6 us
    pallas_call x3, Pallas kernels, load_live(): pl.pallas_call(body, out_shape=pltpu.VMEM(values.shape, values.dtype), in...  10.5 us
    all_to_all x1, waiting for transfers between devices, reduce(): lax.all_to_all(sent[order], 'rep', split_axis=0, concat_axis=0, axis_inde...  10 us
    all_to_all x1, starting transfers between devices, on_device(): lax.all_to_all(wanted, 'rows', split_axis=0, concat_axis=0, tiled=True)  8.16 us
    all_to_all x1, waiting for transfers between devices, on_device(): lax.all_to_all(wanted, 'rows', split_axis=0, concat_axis=0, tiled=True)  6.58 us
  transfers between devices with their start and end apart: 40, of which 21 were waited for; matrix products, arithmetic and copies ran while one was open for 3% of the time, Pallas kernels for 5%

profile of v1, /device:TPU:0, one launch (start us, length us, event | category | flops | bytes accessed | tf_op | source)
XLA Modules:
  0.0 228.7 jit_solution(17259657654701027162)
XLA Ops:
  0.0 1.4 copy.20
  1.4 8.2 %all-to-all-start = ((s32[16,1,8]{2,1,0:T(1,128)}), s32[16,1,8]{2,1,0:T(1,128)S(1)}, u32[]{:S(2)}, u32[]{:S(2)}) async-start(s32[16,1,8]{2,1,0:T(1,128)} %copy.20), calls=%async_computation | async-start | bytes 16384 | tf_op jit(solution)/shard_map/all_to_all | solution.py:191
  9.5 0.9 constant_dynamic-slice_fusion
  10.5 6.6 %all-to-all-done = s32[16,1,8]{2,1,0:T(1,128)S(1)} async-done(((s32[16,1,8]{2,1,0:T(1,128)}), s32[16,1,8]{2,1,0:T(1,128)S(1)}, u32[]{:S(2)}, u32[]{:S(2)}) %all-to-all-start) | async-done | bytes 544 | tf_op jit(solution)/shard_map/all_to_all | solution.py:191
  18.0 13.1 %all_to_all.37 = bf16[16,8,16,128]{3,2,1,0:T(8,128)(2,1)S(1)} all-to-all(bf16[16,8,16,128]{3,2,1,0:T(8,128)(2,1)S(1)} %bitcast.192), channel_id=1, replica_groups=mesh['rows'=16,'rep'=8] {'rows'}, dimensions={0} | all-to-all | bytes 1048576 | tf_op jit(solution)/shard_map/all_to_all | solution.py:208
  31.1 1.5 collective-permute-start.1
  32.6 1.7 collective-permute-start.3
  35.1 8.3 %collective-permute-done.1 = bf16[128,16,128]{2,1,0:T(8,128)(2,1)S(1)} collective-permute-done((bf16[128,16,128]{2,1,0:T(8,128)(2,1)S(1)}, bf16[128,16,128]{2,1,0:T(8,128)(2,1)S(1)}, u32[]{:S(2)}, u32[]{:S(2)}) %collective-permute-start.1) | collective-permute-done | bytes 524320 | tf_op jit(solution)/shard_map/ppermute | solution.py:136
  44.0 3.5 %load_live.3.vals = bf16[512,128,128]{2,1,0:T(8,128)(2,1)S(1)} custom-call(s32[11]{0:T(128)S(1)} %stack.50.scalar, bf16[512,128,128]{2,1,0:T(8,128)(2,1)} %bitcast.186, bf16[128,16,128]{2,1,0:T(8,128)(2,1)S(1)} %bitcast.169), custom_call_target="tpu_custom_call" | custom-call | tf_op jit(solution)/shard_map/load_live/pallas_call | solution.py:96
  47.7 3.3 %collective-permute-start.7 = (bf16[64,16,128]{2,1,0:T(8,128)(2,1)S(1)}, bf16[64,16,128]{2,1,0:T(8,128)(2,1)S(1)}, u32[]{:S(2)}, u32[]{:S(2)}) collective-permute-start(bf16[64,16,128]{2,1,0:T(8,128)(2,1)S(1)} %slice.143), channel_id=1, source_target_pairs={{2,0},{3,1},{4,2},{5,3},{6,4},{7,5},{0,6},{1,7},{10,8},{11,9},{12,... | collective-permute-start | bytes 786440 | tf_op jit(solution)/shard_map/ppermute | solution.py:136
  51.4 6.5 %collective-permute-done.5 = bf16[64,16,128]{2,1,0:T(8,128)(2,1)S(1)} collective-permute-done((bf16[64,16,128]{2,1,0:T(8,128)(2,1)S(1)}, bf16[64,16,128]{2,1,0:T(8,128)(2,1)S(1)}, u32[]{:S(2)}, u32[]{:S(2)}) %collective-permute-start.5) | collective-permute-done | bytes 262176 | tf_op jit(solution)/shard_map/ppermute | solution.py:136
  58.7 0.7 collective-permute-done.6
  59.9 3.9 %tile_sums.3 = (bf16[4,32,16,128]{3,2,1,0:T(8,128)(2,1)S(1)}, f32[4,32,16,128]{3,2,1,0:T(8,128)S(1)}) custom-call(s32[11]{0:T(128)S(1)} %stack.50.scalar, s32[512]{0:T(512)S(1)} %bitcast.180, s32[512]{0:T(512)S(1)} %bitcast.183, bf16[8,128,16,128]{3,2,1,0:T(8,128)(2,1)S(1)} %bitcast_dynamic-update-slice_fusion.26.fetched, ...), custom_call_target="tpu_custom_call" | custom-call | tf_op jit(solution)/shard_map/tile_sums/pallas_call | solution.py:57
  64.5 1.5 collective-permute-done.9
  66.1 1.4 gather_fusion.1
  67.5 4.4 %all-to-all-start.2 = ((bf16[4,32,16,128]{3,2,1,0:T(8,128)(2,1)}), bf16[4,32,16,128]{3,2,1,0:T(8,128)(2,1)S(1)}, u32[]{:S(2)}, u32[]{:S(2)}) async-start(bf16[4,32,16,128]{3,2,1,0:T(8,128)(2,1)} %gather_fusion.1), calls=%async_computation.2 | async-start | bytes 1048576 | tf_op jit(solution)/shard_map/all_to_all | solution.py:168
  72.0 10.0 %all-to-all-done.2 = bf16[4,32,16,128]{3,2,1,0:T(8,128)(2,1)S(1)} async-done(((bf16[4,32,16,128]{3,2,1,0:T(8,128)(2,1)}), bf16[4,32,16,128]{3,2,1,0:T(8,128)(2,1)S(1)}, u32[]{:S(2)}, u32[]{:S(2)}) %all-to-all-start.2) | async-done | bytes 524320 | tf_op jit(solution)/shard_map/all_to_all | solution.py:168
  82.8 18.2 %all_to_all.38 = bf16[16,8,16,128]{3,2,1,0:T(8,128)(2,1)S(1)} all-to-all(bf16[16,8,16,128]{3,2,1,0:T(8,128)(2,1)S(1)} %bitcast.194), channel_id=1, replica_groups=mesh['rows'=16,'rep'=8] {'rows'}, dimensions={0} | all-to-all | bytes 1048576 | tf_op jit(solution)/shard_map/all_to_all | solution.py:208
  101.6 2.7 %collective-permute-start.13 = (bf16[128,16,128]{2,1,0:T(8,128)(2,1)S(1)}, bf16[128,16,128]{2,1,0:T(8,128)(2,1)S(1)}, u32[]{:S(2)}, u32[]{:S(2)}) collective-permute-start(bf16[128,16,128]{2,1,0:T(8,128)(2,1)S(1)} %bitcast.176), channel_id=1, source_target_pairs={{2,0},{3,1},{4,2},{5,3},{6,4},{7,5},{0,6},{1,7},{10,8},{11,9},{12,... | collective-permute-start | bytes 1572872 | tf_op jit(solution)/shard_map/ppermute | solution.py:136
  104.3 8.8 %collective-permute-done.11 = bf16[128,16,128]{2,1,0:T(8,128)(2,1)S(1)} collective-permute-done((bf16[128,16,128]{2,1,0:T(8,128)(2,1)S(1)}, bf16[128,16,128]{2,1,0:T(8,128)(2,1)S(1)}, u32[]{:S(2)}, u32[]{:S(2)}) %collective-permute-start.11) | collective-permute-done | bytes 524320 | tf_op jit(solution)/shard_map/ppermute | solution.py:136
  113.7 3.5 %load_live.4.vals = bf16[512,128,128]{2,1,0:T(8,128)(2,1)S(1)} custom-call(s32[11]{0:T(128)S(1)} %stack.50.scalar, bf16[512,128,128]{2,1,0:T(8,128)(2,1)} %bitcast.187, bf16[128,16,128]{2,1,0:T(8,128)(2,1)S(1)} %bitcast.179), custom_call_target="tpu_custom_call" | custom-call | tf_op jit(solution)/shard_map/load_live/pallas_call | solution.py:96
  117.4 3.3 %collective-permute-start.17 = (bf16[64,16,128]{2,1,0:T(8,128)(2,1)S(1)}, bf16[64,16,128]{2,1,0:T(8,128)(2,1)S(1)}, u32[]{:S(2)}, u32[]{:S(2)}) collective-permute-start(bf16[64,16,128]{2,1,0:T(8,128)(2,1)S(1)} %slice.150), channel_id=1, source_target_pairs={{2,0},{3,1},{4,2},{5,3},{6,4},{7,5},{0,6},{1,7},{10,8},{11,9},{12,... | collective-permute-start | bytes 786440 | tf_op jit(solution)/shard_map/ppermute | solution.py:136
  121.1 6.5 %collective-permute-done.15 = bf16[64,16,128]{2,1,0:T(8,128)(2,1)S(1)} collective-permute-done((bf16[64,16,128]{2,1,0:T(8,128)(2,1)S(1)}, bf16[64,16,128]{2,1,0:T(8,128)(2,1)S(1)}, u32[]{:S(2)}, u32[]{:S(2)}) %collective-permute-start.15) | collective-permute-done | bytes 262176 | tf_op jit(solution)/shard_map/ppermute | solution.py:136
  128.4 0.7 collective-permute-done.16
  129.5 3.9 %tile_sums.4 = (bf16[4,32,16,128]{3,2,1,0:T(8,128)(2,1)S(1)}, f32[4,32,16,128]{3,2,1,0:T(8,128)S(1)}) custom-call(s32[11]{0:T(128)S(1)} %stack.50.scalar, s32[512]{0:T(512)S(1)} %bitcast.181, s32[512]{0:T(512)S(1)} %bitcast.184, bf16[8,128,16,128]{3,2,1,0:T(8,128)(2,1)S(1)} %bitcast_dynamic-update-slice_fusion.22.fetched, ...), custom_call_target="tpu_custom_call" | custom-call | tf_op jit(solution)/shard_map/tile_sums/pallas_call | solution.py:57
  133.4 0.9 collective-permute-start.19
  134.3 1.5 collective-permute-done.19
  136.1 4.6 %collective-permute-start.21 = (bf16[32,16,128]{2,1,0:T(8,128)(2,1)S(1)}, bf16[32,16,128]{2,1,0:T(8,128)(2,1)S(1)}, u32[]{:S(2)}, u32[]{:S(2)}) collective-permute-start(bf16[32,16,128]{2,1,0:T(8,128)(2,1)S(1)} %get-tuple-element.29), channel_id=1, source_target_pairs={{4,0},{5,1},{6,2},{7,3},{0,4},{1,5},{2,6},{3,7},{12,8},{13,9},{14,... | collective-permute-start | bytes 393224 | tf_op jit(solution)/shard_map/ppermute | solution.py:136
  140.7 2.6 %collective-permute-done.20 = bf16[32,16,128]{2,1,0:T(8,128)(2,1)S(1)} collective-permute-done((bf16[32,16,128]{2,1,0:T(8,128)(2,1)S(1)}, bf16[32,16,128]{2,1,0:T(8,128)(2,1)S(1)}, u32[]{:S(2)}, u32[]{:S(2)}) %collective-permute-start.20) | collective-permute-done | bytes 131104 | tf_op jit(solution)/shard_map/ppermute | solution.py:136
  143.3 4.0 %collective-permute-done.21 = bf16[32,16,128]{2,1,0:T(8,128)(2,1)S(1)} collective-permute-done((bf16[32,16,128]{2,1,0:T(8,128)(2,1)S(1)}, bf16[32,16,128]{2,1,0:T(8,128)(2,1)S(1)}, u32[]{:S(2)}, u32[]{:S(2)}) %collective-permute-start.21) | collective-permute-done | bytes 131104 | tf_op jit(solution)/shard_map/ppermute | solution.py:136
  147.3 1.0 fusion.12
  149.0 18.5 %all_to_all.39 = bf16[16,8,16,128]{3,2,1,0:T(8,128)(2,1)S(1)} all-to-all(bf16[16,8,16,128]{3,2,1,0:T(8,128)(2,1)S(1)} %bitcast.193), channel_id=1, replica_groups=mesh['rows'=16,'rep'=8] {'rows'}, dimensions={0} | all-to-all | bytes 1048576 | tf_op jit(solution)/shard_map/all_to_all | solution.py:208
  167.8 3.0 %collective-permute-start.26 = (bf16[128,16,128]{2,1,0:T(8,128)(2,1)S(1)}, bf16[128,16,128]{2,1,0:T(8,128)(2,1)S(1)}, u32[]{:S(2)}, u32[]{:S(2)}) collective-permute-start(bf16[128,16,128]{2,1,0:T(8,128)(2,1)S(1)} %bitcast.171), channel_id=1, source_target_pairs={{2,0},{3,1},{4,2},{5,3},{6,4},{7,5},{0,6},{1,7},{10,8},{11,9},{12,... | collective-permute-start | bytes 1572872 | tf_op jit(solution)/shard_map/ppermute | solution.py:136
  170.7 9.9 %collective-permute-done.24 = bf16[128,16,128]{2,1,0:T(8,128)(2,1)S(1)} collective-permute-done((bf16[128,16,128]{2,1,0:T(8,128)(2,1)S(1)}, bf16[128,16,128]{2,1,0:T(8,128)(2,1)S(1)}, u32[]{:S(2)}, u32[]{:S(2)}) %collective-permute-start.24) | collective-permute-done | bytes 524320 | tf_op jit(solution)/shard_map/ppermute | solution.py:136
  181.3 3.5 %load_live.5.vals = bf16[512,128,128]{2,1,0:T(8,128)(2,1)S(1)} custom-call(s32[11]{0:T(128)S(1)} %stack.50.scalar, bf16[512,128,128]{2,1,0:T(8,128)(2,1)} %bitcast.188, bf16[128,16,128]{2,1,0:T(8,128)(2,1)S(1)} %bitcast.174), custom_call_target="tpu_custom_call" | custom-call | tf_op jit(solution)/shard_map/load_live/pallas_call | solution.py:96
  185.0 3.3 %collective-permute-start.30 = (bf16[64,16,128]{2,1,0:T(8,128)(2,1)S(1)}, bf16[64,16,128]{2,1,0:T(8,128)(2,1)S(1)}, u32[]{:S(2)}, u32[]{:S(2)}) collective-permute-start(bf16[64,16,128]{2,1,0:T(8,128)(2,1)S(1)} %slice.158), channel_id=1, source_target_pairs={{2,0},{3,1},{4,2},{5,3},{6,4},{7,5},{0,6},{1,7},{10,8},{11,9},{12,... | collective-permute-start | bytes 786440 | tf_op jit(solution)/shard_map/ppermute | solution.py:136
  188.7 6.5 %collective-permute-done.28 = bf16[64,16,128]{2,1,0:T(8,128)(2,1)S(1)} collective-permute-done((bf16[64,16,128]{2,1,0:T(8,128)(2,1)S(1)}, bf16[64,16,128]{2,1,0:T(8,128)(2,1)S(1)}, u32[]{:S(2)}, u32[]{:S(2)}) %collective-permute-start.28) | collective-permute-done | bytes 262176 | tf_op jit(solution)/shard_map/ppermute | solution.py:136
  196.0 0.7 collective-permute-done.29
  197.1 3.9 %tile_sums.5 = (bf16[4,32,16,128]{3,2,1,0:T(8,128)(2,1)S(1)}, f32[4,32,16,128]{3,2,1,0:T(8,128)S(1)}) custom-call(s32[11]{0:T(128)S(1)} %stack.50.scalar, s32[512]{0:T(512)S(1)} %bitcast.182, s32[512]{0:T(512)S(1)} %bitcast.185, bf16[8,128,16,128]{3,2,1,0:T(8,128)(2,1)S(1)} %bitcast_dynamic-update-slice_fusion.18.fetched, ...), custom_call_target="tpu_custom_call" | custom-call | tf_op jit(solution)/shard_map/tile_sums/pallas_call | solution.py:57
  201.7 0.7 pad_maximum_fusion
  202.4 4.4 %all-to-all-start.4 = ((bf16[8,4,2,16,128]{4,3,1,2,0:T(8,128)(2,1)}), bf16[8,4,2,16,128]{4,3,1,2,0:T(8,128)(2,1)S(1)}, u32[]{:S(2)}, u32[]{:S(2)}) async-start(bf16[8,4,2,16,128]{4,3,1,2,0:T(8,128)(2,1)} %pad_maximum_fusion), calls=%async_computation.4 | async-start | bytes 524288 | tf_op jit(solution)/shard_map/all_to_all | solution.py:205
  206.9 1.1 fusion.17
  208.0 6.4 %all-to-all-done.4 = bf16[8,4,2,16,128]{4,3,1,2,0:T(8,128)(2,1)S(1)} async-done(((bf16[8,4,2,16,128]{4,3,1,2,0:T(8,128)(2,1)}), bf16[8,4,2,16,128]{4,3,1,2,0:T(8,128)(2,1)S(1)}, u32[]{:S(2)}, u32[]{:S(2)}) %all-to-all-start.4) | async-done | bytes 262176 | tf_op jit(solution)/shard_map/all_to_all | solution.py:205
  215.3 2.7 %collective-permute-start.34 = (bf16[48,16,128]{2,1,0:T(8,128)(2,1)S(1)}, bf16[48,16,128]{2,1,0:T(8,128)(2,1)S(1)}, u32[]{:S(2)}, u32[]{:S(2)}) collective-permute-start(bf16[48,16,128]{2,1,0:T(8,128)(2,1)S(1)} %pad_maximum_fusion.2), channel_id=1, source_target_pairs={{2,0},{3,1},{4,2},{5,3},{6,4},{7,5},{0,6},{1,7},{10,8},{11,9},{12,... | collective-permute-start | bytes 589832 | tf_op jit(solution)/shard_map/ppermute | solution.py:136
  218.3 3.9 %collective-permute-done.33 = bf16[48,16,128]{2,1,0:T(8,128)(2,1)S(1)} collective-permute-done((bf16[48,16,128]{2,1,0:T(8,128)(2,1)S(1)}, bf16[48,16,128]{2,1,0:T(8,128)(2,1)S(1)}, u32[]{:S(2)}, u32[]{:S(2)}) %collective-permute-start.33) | collective-permute-done | bytes 196640 | tf_op jit(solution)/shard_map/ppermute | solution.py:136
  222.2 3.3 %collective-permute-start.36 = (bf16[16,16,128]{2,1,0:T(8,128)(2,1)S(1)}, bf16[16,16,128]{2,1,0:T(8,128)(2,1)S(1)}, u32[]{:S(2)}, u32[]{:S(2)}) collective-permute-start(bf16[16,16,128]{2,1,0:T(8,128)(2,1)S(1)} %slice.167), channel_id=1, source_target_pairs={{2,0},{3,1},{4,2},{5,3},{6,4},{7,5},{0,6},{1,7},{10,8},{11,9},{12,... | collective-permute-start | bytes 196616 | tf_op jit(solution)/shard_map/ppermute | solution.py:136
  225.7 1.9 collective-permute-done.35
  227.8 0.9 fusion
  (120 shorter events, 13.6 us)
Async XLA Ops:
  1.4 15.7 %all-to-all-start = ((s32[16,1,8]{2,1,0:T(1,128)}), s32[16,1,8]{2,1,0:T(1,128)S(1)}, u32[]{:S(2)}, u32[]{:S(2)}) async-start(s32[16,1,8]{2,1,0:T(1,128)} %copy.20), calls=%async_computation | async-start | bytes 16384 | tf_op jit(solution)/shard_map/all_to_all | solution.py:191
  31.1 12.3 %collective-permute-start.1 = (bf16[128,16,128]{2,1,0:T(8,128)(2,1)S(1)}, bf16[128,16,128]{2,1,0:T(8,128)(2,1)S(1)}, u32[]{:S(2)}, u32[]{:S(2)}) collective-permute-start(bf16[128,16,128]{2,1,0:T(8,128)(2,1)S(1)} %bitcast.165), channel_id=1, source_target_pairs={{6,0},{7,1},{0,2},{1,3},{2,4},{3,5},{4,6},{5,7},{14,8},{15,9},{8,1... | collective-permute-start | bytes 1572872 | tf_op jit(solution)/shard_map/ppermute | solution.py:136
  32.6 15.1 %collective-permute-start.3 = (bf16[128,16,128]{2,1,0:T(8,128)(2,1)S(1)}, bf16[128,16,128]{2,1,0:T(8,128)(2,1)S(1)}, u32[]{:S(2)}, u32[]{:S(2)}) collective-permute-start(bf16[128,16,128]{2,1,0:T(8,128)(2,1)S(1)} %bitcast.166), channel_id=1, source_target_pairs={{2,0},{3,1},{4,2},{5,3},{6,4},{7,5},{0,6},{1,7},{10,8},{11,9},{12,... | collective-permute-start | bytes 1572872 | tf_op jit(solution)/shard_map/ppermute | solution.py:136
  34.3 16.9 %collective-permute-start = (bf16[128,16,128]{2,1,0:T(8,128)(2,1)S(1)}, bf16[128,16,128]{2,1,0:T(8,128)(2,1)S(1)}, u32[]{:S(2)}, u32[]{:S(2)}) collective-permute-start(bf16[128,16,128]{2,1,0:T(8,128)(2,1)S(1)} %bitcast.167), channel_id=1, source_target_pairs={{0,1},{1,0},{2,3},{3,2},{4,5},{5,4},{6,7},{7,6},{8,9},{9,8},{10,11... | collective-permute-start | bytes 1572872 | tf_op jit(solution)/shard_map/ppermute | solution.py:139
  43.4 15.0 %collective-permute-start.2 = (bf16[128,16,128]{2,1,0:T(8,128)(2,1)S(1)}, bf16[128,16,128]{2,1,0:T(8,128)(2,1)S(1)}, u32[]{:S(2)}, u32[]{:S(2)}) collective-permute-start(bf16[128,16,128]{2,1,0:T(8,128)(2,1)S(1)} %collective-permute-done.1), channel_id=1, source_target_pairs={{0,1},{1,0},{2,3},{3,2},{4,5},{5,4},{6,7},{7,6},{8,9},{9,8},{10,11... | collective-permute-start | bytes 1572872 | tf_op jit(solution)/shard_map/ppermute | solution.py:139
  47.5 12.3 %copy-start = (s32[1,1,512]{2,1,0:T(1,128)S(1)}, s32[1,1,512]{2,1,0:T(1,128)}, u32[]{:S(2)}) copy-start(s32[1,1,512]{2,1,0:T(1,128)} %param.9) | copy-start | bytes 6148
  47.5 12.3 %copy-start.1 = (s32[1,1,512]{2,1,0:T(1,128)S(1)}, s32[1,1,512]{2,1,0:T(1,128)}, u32[]{:S(2)}) copy-start(s32[1,1,512]{2,1,0:T(1,128)} %param.10) | copy-start | bytes 6148
  47.6 10.3 %collective-permute-start.5 = (bf16[64,16,128]{2,1,0:T(8,128)(2,1)S(1)}, bf16[64,16,128]{2,1,0:T(8,128)(2,1)S(1)}, u32[]{:S(2)}, u32[]{:S(2)}) collective-permute-start(bf16[64,16,128]{2,1,0:T(8,128)(2,1)S(1)} %slice.142), channel_id=1, source_target_pairs={{6,0},{7,1},{0,2},{1,3},{2,4},{3,5},{4,6},{5,7},{14,8},{15,9},{8,1... | collective-permute-start | bytes 786440 | tf_op jit(solution)/shard_map/ppermute | solution.py:136
  47.7 10.2 %collective-permute-start.7 = (bf16[64,16,128]{2,1,0:T(8,128)(2,1)S(1)}, bf16[64,16,128]{2,1,0:T(8,128)(2,1)S(1)}, u32[]{:S(2)}, u32[]{:S(2)}) collective-permute-start(bf16[64,16,128]{2,1,0:T(8,128)(2,1)S(1)} %slice.143), channel_id=1, source_target_pairs={{2,0},{3,1},{4,2},{5,3},{6,4},{7,5},{0,6},{1,7},{10,8},{11,9},{12,... | collective-permute-start | bytes 786440 | tf_op jit(solution)/shard_map/ppermute | solution.py:136
  51.0 7.6 %collective-permute-start.4 = (bf16[128,16,128]{2,1,0:T(8,128)(2,1)S(1)}, bf16[128,16,128]{2,1,0:T(8,128)(2,1)S(1)}, u32[]{:S(2)}, u32[]{:S(2)}) collective-permute-start(bf16[128,16,128]{2,1,0:T(8,128)(2,1)S(1)} %collective-permute-done.3), channel_id=1, source_target_pairs={{0,1},{1,0},{2,3},{3,2},{4,5},{5,4},{6,7},{7,6},{8,9},{9,8},{10,11... | collective-permute-start | bytes 1572872 | tf_op jit(solution)/shard_map/ppermute | solution.py:139
  57.9 1.5 collective-permute-start.6
  57.9 1.9 collective-permute-start.8
  63.7 2.2 collective-permute-start.9
  67.5 14.4 %all-to-all-start.2 = ((bf16[4,32,16,128]{3,2,1,0:T(8,128)(2,1)}), bf16[4,32,16,128]{3,2,1,0:T(8,128)(2,1)S(1)}, u32[]{:S(2)}, u32[]{:S(2)}) async-start(bf16[4,32,16,128]{3,2,1,0:T(8,128)(2,1)} %gather_fusion.1), calls=%async_computation.2 | async-start | bytes 1048576 | tf_op jit(solution)/shard_map/all_to_all | solution.py:168
  101.0 12.1 %collective-permute-start.11 = (bf16[128,16,128]{2,1,0:T(8,128)(2,1)S(1)}, bf16[128,16,128]{2,1,0:T(8,128)(2,1)S(1)}, u32[]{:S(2)}, u32[]{:S(2)}) collective-permute-start(bf16[128,16,128]{2,1,0:T(8,128)(2,1)S(1)} %bitcast.175), channel_id=1, source_target_pairs={{6,0},{7,1},{0,2},{1,3},{2,4},{3,5},{4,6},{5,7},{14,8},{15,9},{8,1... | collective-permute-start | bytes 1572872 | tf_op jit(solution)/shard_map/ppermute | solution.py:136
  101.6 15.7 %collective-permute-start.13 = (bf16[128,16,128]{2,1,0:T(8,128)(2,1)S(1)}, bf16[128,16,128]{2,1,0:T(8,128)(2,1)S(1)}, u32[]{:S(2)}, u32[]{:S(2)}) collective-permute-start(bf16[128,16,128]{2,1,0:T(8,128)(2,1)S(1)} %bitcast.176), channel_id=1, source_target_pairs={{2,0},{3,1},{4,2},{5,3},{6,4},{7,5},{0,6},{1,7},{10,8},{11,9},{12,... | collective-permute-start | bytes 1572872 | tf_op jit(solution)/shard_map/ppermute | solution.py:136
  104.3 16.6 %collective-permute-start.10 = (bf16[128,16,128]{2,1,0:T(8,128)(2,1)S(1)}, bf16[128,16,128]{2,1,0:T(8,128)(2,1)S(1)}, u32[]{:S(2)}, u32[]{:S(2)}) collective-permute-start(bf16[128,16,128]{2,1,0:T(8,128)(2,1)S(1)} %bitcast.177), channel_id=1, source_target_pairs={{0,1},{1,0},{2,3},{3,2},{4,5},{5,4},{6,7},{7,6},{8,9},{9,8},{10,11... | collective-permute-start | bytes 1572872 | tf_op jit(solution)/shard_map/ppermute | solution.py:139
  113.1 15.0 %collective-permute-start.12 = (bf16[128,16,128]{2,1,0:T(8,128)(2,1)S(1)}, bf16[128,16,128]{2,1,0:T(8,128)(2,1)S(1)}, u32[]{:S(2)}, u32[]{:S(2)}) collective-permute-start(bf16[128,16,128]{2,1,0:T(8,128)(2,1)S(1)} %collective-permute-done.11), channel_id=1, source_target_pairs={{0,1},{1,0},{2,3},{3,2},{4,5},{5,4},{6,7},{7,6},{8,9},{9,8},{10,11... | collective-permute-start | bytes 1572872 | tf_op jit(solution)/shard_map/ppermute | solution.py:139
  117.2 10.3 %collective-permute-start.15 = (bf16[64,16,128]{2,1,0:T(8,128)(2,1)S(1)}, bf16[64,16,128]{2,1,0:T(8,128)(2,1)S(1)}, u32[]{:S(2)}, u32[]{:S(2)}) collective-permute-start(bf16[64,16,128]{2,1,0:T(8,128)(2,1)S(1)} %slice.149), channel_id=1, source_target_pairs={{6,0},{7,1},{0,2},{1,3},{2,4},{3,5},{4,6},{5,7},{14,8},{15,9},{8,1... | collective-permute-start | bytes 786440 | tf_op jit(solution)/shard_map/ppermute | solution.py:136
  117.4 10.2 %collective-permute-start.17 = (bf16[64,16,128]{2,1,0:T(8,128)(2,1)S(1)}, bf16[64,16,128]{2,1,0:T(8,128)(2,1)S(1)}, u32[]{:S(2)}, u32[]{:S(2)}) collective-permute-start(bf16[64,16,128]{2,1,0:T(8,128)(2,1)S(1)} %slice.150), channel_id=1, source_target_pairs={{2,0},{3,1},{4,2},{5,3},{6,4},{7,5},{0,6},{1,7},{10,8},{11,9},{12,... | collective-permute-start | bytes 786440 | tf_op jit(solution)/shard_map/ppermute | solution.py:136
  120.6 7.6 %collective-permute-start.14 = (bf16[128,16,128]{2,1,0:T(8,128)(2,1)S(1)}, bf16[128,16,128]{2,1,0:T(8,128)(2,1)S(1)}, u32[]{:S(2)}, u32[]{:S(2)}) collective-permute-start(bf16[128,16,128]{2,1,0:T(8,128)(2,1)S(1)} %collective-permute-done.13), channel_id=1, source_target_pairs={{0,1},{1,0},{2,3},{3,2},{4,5},{5,4},{6,7},{7,6},{8,9},{9,8},{10,11... | collective-permute-start | bytes 1572872 | tf_op jit(solution)/shard_map/ppermute | solution.py:139
  127.5 1.5 collective-permute-start.16
  127.6 1.9 collective-permute-start.18
  133.4 2.4 %collective-permute-start.19 = (bf16[4,32,16,128]{3,2,1,0:T(8,128)(2,1)S(1)}, bf16[4,32,16,128]{3,2,1,0:T(8,128)(2,1)S(1)}, u32[]{:S(2)}, u32[]{:S(2)}) collective-permute-start(bf16[4,32,16,128]{3,2,1,0:T(8,128)(2,1)S(1)} %get-tuple-element.14), channel_id=1, source_target_pairs={{0,1},{1,0},{2,3},{3,2},{4,5},{5,4},{6,7},{7,6},{8,9},{9,8},{10,11... | collective-permute-start | bytes 1572872 | tf_op jit(solution)/shard_map/ppermute | solution.py:139
  136.0 7.3 %collective-permute-start.20 = (bf16[32,16,128]{2,1,0:T(8,128)(2,1)S(1)}, bf16[32,16,128]{2,1,0:T(8,128)(2,1)S(1)}, u32[]{:S(2)}, u32[]{:S(2)}) collective-permute-start(bf16[32,16,128]{2,1,0:T(8,128)(2,1)S(1)} %get-tuple-element.27), channel_id=1, source_target_pairs={{6,0},{7,1},{0,2},{1,3},{2,4},{3,5},{4,6},{5,7},{14,8},{15,9},{8,1... | collective-permute-start | bytes 393224 | tf_op jit(solution)/shard_map/ppermute | solution.py:136
  136.1 11.2 %collective-permute-start.21 = (bf16[32,16,128]{2,1,0:T(8,128)(2,1)S(1)}, bf16[32,16,128]{2,1,0:T(8,128)(2,1)S(1)}, u32[]{:S(2)}, u32[]{:S(2)}) collective-permute-start(bf16[32,16,128]{2,1,0:T(8,128)(2,1)S(1)} %get-tuple-element.29), channel_id=1, source_target_pairs={{4,0},{5,1},{6,2},{7,3},{0,4},{1,5},{2,6},{3,7},{12,8},{13,9},{14,... | collective-permute-start | bytes 393224 | tf_op jit(solution)/shard_map/ppermute | solution.py:136
  140.7 6.6 %collective-permute-start.22 = (bf16[32,16,128]{2,1,0:T(8,128)(2,1)S(1)}, bf16[32,16,128]{2,1,0:T(8,128)(2,1)S(1)}, u32[]{:S(2)}, u32[]{:S(2)}) collective-permute-start(bf16[32,16,128]{2,1,0:T(8,128)(2,1)S(1)} %get-tuple-element.28), channel_id=1, source_target_pairs={{2,0},{3,1},{4,2},{5,3},{6,4},{7,5},{0,6},{1,7},{10,8},{11,9},{12,... | collective-permute-start | bytes 393224 | tf_op jit(solution)/shard_map/ppermute | solution.py:136
  167.5 13.2 %collective-permute-start.24 = (bf16[128,16,128]{2,1,0:T(8,128)(2,1)S(1)}, bf16[128,16,128]{2,1,0:T(8,128)(2,1)S(1)}, u32[]{:S(2)}, u32[]{:S(2)}) collective-permute-start(bf16[128,16,128]{2,1,0:T(8,128)(2,1)S(1)} %bitcast.170), channel_id=1, source_target_pairs={{6,0},{7,1},{0,2},{1,3},{2,4},{3,5},{4,6},{5,7},{14,8},{15,9},{8,1... | collective-permute-start | bytes 1572872 | tf_op jit(solution)/shard_map/ppermute | solution.py:136
  167.8 17.2 %collective-permute-start.26 = (bf16[128,16,128]{2,1,0:T(8,128)(2,1)S(1)}, bf16[128,16,128]{2,1,0:T(8,128)(2,1)S(1)}, u32[]{:S(2)}, u32[]{:S(2)}) collective-permute-start(bf16[128,16,128]{2,1,0:T(8,128)(2,1)S(1)} %bitcast.171), channel_id=1, source_target_pairs={{2,0},{3,1},{4,2},{5,3},{6,4},{7,5},{0,6},{1,7},{10,8},{11,9},{12,... | collective-permute-start | bytes 1572872 | tf_op jit(solution)/shard_map/ppermute | solution.py:136
  170.7 17.8 %collective-permute-start.23 = (bf16[128,16,128]{2,1,0:T(8,128)(2,1)S(1)}, bf16[128,16,128]{2,1,0:T(8,128)(2,1)S(1)}, u32[]{:S(2)}, u32[]{:S(2)}) collective-permute-start(bf16[128,16,128]{2,1,0:T(8,128)(2,1)S(1)} %bitcast.172), channel_id=1, source_target_pairs={{0,1},{1,0},{2,3},{3,2},{4,5},{5,4},{6,7},{7,6},{8,9},{9,8},{10,11... | collective-permute-start | bytes 1572872 | tf_op jit(solution)/shard_map/ppermute | solution.py:139
  180.7 15.0 %collective-permute-start.25 = (bf16[128,16,128]{2,1,0:T(8,128)(2,1)S(1)}, bf16[128,16,128]{2,1,0:T(8,128)(2,1)S(1)}, u32[]{:S(2)}, u32[]{:S(2)}) collective-permute-start(bf16[128,16,128]{2,1,0:T(8,128)(2,1)S(1)} %collective-permute-done.24), channel_id=1, source_target_pairs={{0,1},{1,0},{2,3},{3,2},{4,5},{5,4},{6,7},{7,6},{8,9},{9,8},{10,11... | collective-permute-start | bytes 1572872 | tf_op jit(solution)/shard_map/ppermute | solution.py:139
  184.9 10.3 %collective-permute-start.28 = (bf16[64,16,128]{2,1,0:T(8,128)(2,1)S(1)}, bf16[64,16,128]{2,1,0:T(8,128)(2,1)S(1)}, u32[]{:S(2)}, u32[]{:S(2)}) collective-permute-start(bf16[64,16,128]{2,1,0:T(8,128)(2,1)S(1)} %slice.157), channel_id=1, source_target_pairs={{6,0},{7,1},{0,2},{1,3},{2,4},{3,5},{4,6},{5,7},{14,8},{15,9},{8,1... | collective-permute-start | bytes 786440 | tf_op jit(solution)/shard_map/ppermute | solution.py:136
  185.0 10.2 %collective-permute-start.30 = (bf16[64,16,128]{2,1,0:T(8,128)(2,1)S(1)}, bf16[64,16,128]{2,1,0:T(8,128)(2,1)S(1)}, u32[]{:S(2)}, u32[]{:S(2)}) collective-permute-start(bf16[64,16,128]{2,1,0:T(8,128)(2,1)S(1)} %slice.158), channel_id=1, source_target_pairs={{2,0},{3,1},{4,2},{5,3},{6,4},{7,5},{0,6},{1,7},{10,8},{11,9},{12,... | collective-permute-start | bytes 786440 | tf_op jit(solution)/shard_map/ppermute | solution.py:136
  188.3 7.6 %collective-permute-start.27 = (bf16[128,16,128]{2,1,0:T(8,128)(2,1)S(1)}, bf16[128,16,128]{2,1,0:T(8,128)(2,1)S(1)}, u32[]{:S(2)}, u32[]{:S(2)}) collective-permute-start(bf16[128,16,128]{2,1,0:T(8,128)(2,1)S(1)} %collective-permute-done.26), channel_id=1, source_target_pairs={{0,1},{1,0},{2,3},{3,2},{4,5},{5,4},{6,7},{7,6},{8,9},{9,8},{10,11... | collective-permute-start | bytes 1572872 | tf_op jit(solution)/shard_map/ppermute | solution.py:139
  195.2 1.5 collective-permute-start.29
  195.2 1.9 collective-permute-start.31
  197.1 9.7 %copy-start.2 = (bf16[4,128,256]{2,1,0:T(8,128)(2,1)S(1)}, bf16[4,128,256]{2,1,0:T(8,128)(2,1)}, u32[]{:S(2)}) copy-start(bf16[4,128,256]{2,1,0:T(8,128)(2,1)} %param.13) | copy-start | bytes 786436
  201.0 13.4 %collective-permute-start.32 = (bf16[4,32,16,128]{3,2,1,0:T(8,128)(2,1)S(1)}, bf16[4,32,16,128]{3,2,1,0:T(8,128)(2,1)S(1)}, u32[]{:S(2)}, u32[]{:S(2)}) collective-permute-start(bf16[4,32,16,128]{3,2,1,0:T(8,128)(2,1)S(1)} %get-tuple-element.16), channel_id=1, source_target_pairs={{0,1},{1,0},{2,3},{3,2},{4,5},{5,4},{6,7},{7,6},{8,9},{9,8},{10,11... | collective-permute-start | bytes 1572872 | tf_op jit(solution)/shard_map/ppermute | solution.py:139
  202.4 11.9 %all-to-all-start.4 = ((bf16[8,4,2,16,128]{4,3,1,2,0:T(8,128)(2,1)}), bf16[8,4,2,16,128]{4,3,1,2,0:T(8,128)(2,1)S(1)}, u32[]{:S(2)}, u32[]{:S(2)}) async-start(bf16[8,4,2,16,128]{4,3,1,2,0:T(8,128)(2,1)} %pad_maximum_fusion), calls=%async_computation.4 | async-start | bytes 524288 | tf_op jit(solution)/shard_map/all_to_all | solution.py:205
  214.7 7.6 %collective-permute-start.33 = (bf16[48,16,128]{2,1,0:T(8,128)(2,1)S(1)}, bf16[48,16,128]{2,1,0:T(8,128)(2,1)S(1)}, u32[]{:S(2)}, u32[]{:S(2)}) collective-permute-start(bf16[48,16,128]{2,1,0:T(8,128)(2,1)S(1)} %pad_maximum_fusion.1), channel_id=1, source_target_pairs={{6,0},{7,1},{0,2},{1,3},{2,4},{3,5},{4,6},{5,7},{14,8},{15,9},{8,1... | collective-permute-start | bytes 589832 | tf_op jit(solution)/shard_map/ppermute | solution.py:136
  215.3 6.9 %collective-permute-start.34 = (bf16[48,16,128]{2,1,0:T(8,128)(2,1)S(1)}, bf16[48,16,128]{2,1,0:T(8,128)(2,1)S(1)}, u32[]{:S(2)}, u32[]{:S(2)}) collective-permute-start(bf16[48,16,128]{2,1,0:T(8,128)(2,1)S(1)} %pad_maximum_fusion.2), channel_id=1, source_target_pairs={{2,0},{3,1},{4,2},{5,3},{6,4},{7,5},{0,6},{1,7},{10,8},{11,9},{12,... | collective-permute-start | bytes 589832 | tf_op jit(solution)/shard_map/ppermute | solution.py:136
  222.2 5.5 %collective-permute-start.35 = (bf16[16,16,128]{2,1,0:T(8,128)(2,1)S(1)}, bf16[16,16,128]{2,1,0:T(8,128)(2,1)S(1)}, u32[]{:S(2)}, u32[]{:S(2)}) collective-permute-start(bf16[16,16,128]{2,1,0:T(8,128)(2,1)S(1)} %slice.166), channel_id=1, source_target_pairs={{6,0},{7,1},{0,2},{1,3},{2,4},{3,5},{4,6},{5,7},{14,8},{15,9},{8,1... | collective-permute-start | bytes 196616 | tf_op jit(solution)/shard_map/ppermute | solution.py:136
  222.2 5.4 %collective-permute-start.36 = (bf16[16,16,128]{2,1,0:T(8,128)(2,1)S(1)}, bf16[16,16,128]{2,1,0:T(8,128)(2,1)S(1)}, u32[]{:S(2)}, u32[]{:S(2)}) collective-permute-start(bf16[16,16,128]{2,1,0:T(8,128)(2,1)S(1)} %slice.167), channel_id=1, source_target_pairs={{2,0},{3,1},{4,2},{5,3},{6,4},{7,5},{0,6},{1,7},{10,8},{11,9},{12,... | collective-permute-start | bytes 196616 | tf_op jit(solution)/shard_map/ppermute | solution.py:136

commit v2 on v0

--- a/solution.py
+++ b/solution.py
@@ -138,17 +138,17 @@
     def partner(x):
         return lax.ppermute(x, "rep", [(i, i ^ 1) for i in range(replicas)])
 
-    def gather(sent):
+    def gather(sent, opposite=None):
         slots = sent.shape[0]
         half = slots // 2
-        low, high = sent[:half], sent[half:]
-        before_low, after_high = along(low, -1), along(high, 1)
-        before_high, after_low = along(high, -1), along(low, 1)
-        other = partner(sent)
+        before, after, other = along(sent, -1), along(sent, 1), partner(sent)
         live = load_live(values, scalars, sent)
-        before_low, live = lax.optimization_barrier((before_low, live))
-        far_low, far_high = along(before_low, -1), along(after_high, 1)
-        fetched = jnp.zeros((replicas, slots, sub, width), sent.dtype)
+        pieces = [(before, -1, 0), (after, 1, 0)]
+        if opposite is None:
+            first, second = along(before[:half], -1), along(after[half:], 1)
+            pieces += [(first, 2, 0), (second, 2, half)]
+        else:
+            pieces = [(opposite, 2, 0)] + pieces
 
         def put(fetched, array, hops, other_core, start):
             place = places[hops][other_core]
@@ -156,39 +156,25 @@
                 fetched, array[None], (place, start, 0, 0), allow_negative_indices=False
             )
 
+        fetched = jnp.zeros((replicas, slots, sub, width), sent.dtype)
         fetched = put(fetched, sent, 0, 0, 0)
         fetched = put(fetched, other, 0, 1, 0)
-        for array, hops, start in (
-            (before_low, -1, 0),
-            (after_high, 1, half),
-            (before_high, -1, half),
-            (after_low, 1, 0),
-            (far_low, 2, 0),
-            (far_high, 2, half),
-        ):
+        for array, hops, start in pieces:
             fetched = put(fetched, array, hops, 0, start)
-            crossed = partner(array)
-            fetched = put(fetched, crossed, hops, 1, start)
+            fetched = put(fetched, partner(array), hops, 1, start)
         return fetched, live
 
     def reduce(peer, mine):
         sums = mine + partner(peer).astype(jnp.float32)
-        sent = [sums[hops].astype(jnp.bfloat16) for hops in range(chips)]
-        half = row_blocks // 2
-        low, high = along(sent[2][:half], -1), along(sent[2][half:], 1)
-        parts = [along(sent[1], -1), along(sent[3], 1)]
-        parts.append(jnp.concatenate([along(low, -1), along(high, 1)], 0))
         total = sums[0]
-        for part in parts:
-            total = total + part.astype(jnp.float32)
+        for hops in range(1, chips):
+            total = total + along(sums[hops].astype(jnp.bfloat16), -hops).astype(jnp.float32)
         return total
 
     served = lax.all_to_all(wanted, "rows", split_axis=0, concat_axis=0, tiled=True)
-    terms = [
-        lax.dynamic_slice_in_dim(
-            features.reshape(row_blocks, tile, width), rank * sub, sub, 1
-        )
-    ]
+    blocks = features.reshape(row_blocks, tile, width)
+    terms = [lax.dynamic_slice_in_dim(blocks, rank * sub, sub, 1)]
+    opposite = lax.dynamic_slice_in_dim(blocks, places[2][0] * sub, sub, 1)
     own = [lax.dynamic_slice_in_dim(features, rank * share_rows, share_rows, 0)]
 
     def step(degree):
@@ -200,10 +186,16 @@
             swapped = lax.all_to_all(swapped, "rep", split_axis=0, concat_axis=0, tiled=True)
             swapped = swapped.transpose(2, 1, 0, 3, 4).reshape(degree_last - 1, share_rows, width)
             own.extend(swapped[k] for k in range(degree_last - 1))
-        sent = lax.all_to_all(
-            terms[-1][served], "rows", split_axis=0, concat_axis=0, tiled=True
-        ).reshape(-1, sub, width)
-        fetched, live = gather(sent)
+        if degree == 1:
+            both = jnp.concatenate([terms[0], opposite], 1)[served]
+            both = lax.all_to_all(both, "rows", split_axis=0, concat_axis=0, tiled=True)
+            both = both.reshape(-1, 2 * sub, width)
+            fetched, live = gather(both[:, :sub], both[:, sub:])
+        else:
+            sent = lax.all_to_all(
+                terms[-1][served], "rows", split_axis=0, concat_axis=0, tiled=True
+            ).reshape(-1, sub, width)
+            fetched, live = gather(sent)
         peer, mine = tile_sums(
             fetched, live, rows_of, slots_of, scalars, row_blocks, whole_blocks=last
         )

time: 207 us -> 209 us (level)
  starting transfers between devices: 76.9 us -> 46.5 us
  waiting for transfers between devices: 44.7 us -> 70.7 us
  blocking collectives: 48.1 us -> 55.4 us
    ppermute x36 -> x19, starting transfers between devices: 59.5 us -> 30.9 us  [along(): lax.ppermute(x, 'rep', [((i + step) % replicas, i) for i in range(replica...]
    ppermute x36 -> x19, waiting for transfers between devices: 32.1 us -> 57.4 us  [along(): lax.ppermute(x, 'rep', [((i + step) % replicas, i) for i in range(replica...]
    all_to_all x0 -> x1, blocking collectives: none -> 18.7 us  [step(): both = lax.all_to_all(both, 'rows', split_axis=0, concat_axis=0, tiled=True)]
    all_to_all x3 -> x2, blocking collectives: 48.1 us -> 36.7 us  [step(): lax.all_to_all(terms[-1][served], 'rows', split_axis=0, concat_axis=0, ti...]
    ppermute x24 -> x17, starting transfers between devices: 5.79 us -> 4 us  [partner(): return lax.ppermute(x, 'rep', [(i, i ^ 1) for i in range(replicas)])]
    ppermute x24 -> x17, waiting for transfers between devices: 5.95 us -> 6.82 us  [partner(): return lax.ppermute(x, 'rep', [(i, i ^ 1) for i in range(replicas)])]
  transfers between devices with their start and end apart: 62 -> 38, of which waited for: 23 -> 21; matrix products, arithmetic and copies ran while one was open for 3% -> 3% of each run, Pallas kernels for 7% -> 7%
where the time goes in v2:
time: 209 us
  waiting for transfers between devices  70.7 us (34%)
  blocking collectives  55.4 us (27%)
  starting transfers between devices  46.5 us (22%)
  Pallas kernels  22.1 us (11%)
  local copies, waits for them, and re-layouts  8.62 us (4%)
  matrix products  2.45 us (1%)
    ppermute x19, waiting for transfers between devices, along(): lax.ppermute(x, 'rep', [((i + step) % replicas, i) for i in range(replica...  57.4 us
    all_to_all x2, blocking collectives, step(): lax.all_to_all(terms[-1][served], 'rows', split_axis=0, concat_axis=0, ti...  36.7 us
    ppermute x19, starting transfers between devices, along(): lax.ppermute(x, 'rep', [((i + step) % replicas, i) for i in range(replica...  30.9 us
    all_to_all x1, blocking collectives, step(): both = lax.all_to_all(both, 'rows', split_axis=0, concat_axis=0, tiled=True)  18.7 us
    pallas_call x3, Pallas kernels, tile_sums(): pl.pallas_call(body, out_shape=(pltpu.VMEM(shape, jnp.bfloat16), pltpu.VM...  11.6 us
    pallas_call x3, Pallas kernels, load_live(): pl.pallas_call(body, out_shape=pltpu.VMEM(values.shape, values.dtype), in...  10.5 us
    all_to_all x1, starting transfers between devices, on_device(): lax.all_to_all(wanted, 'rows', split_axis=0, concat_axis=0, tiled=True)  8.16 us
    ppermute x17, waiting for transfers between devices, partner(): return lax.ppermute(x, 'rep', [(i, i ^ 1) for i in range(replicas)])  6.82 us
  transfers between devices with their start and end apart: 38, of which 21 were waited for; matrix products, arithmetic and copies ran while one was open for 3% of the time, Pallas kernels for 7%

profile of v2, /device:TPU:0, one launch (start us, length us, event | category | flops | bytes accessed | tf_op | source)
XLA Modules:
  0.0 208.5 jit_solution(15881486107541638780)
XLA Ops:
  0.0 1.4 copy.20
  1.4 8.2 %all-to-all-start = ((s32[16,1,8]{2,1,0:T(1,128)}), s32[16,1,8]{2,1,0:T(1,128)S(1)}, u32[]{:S(2)}, u32[]{:S(2)}) async-start(s32[16,1,8]{2,1,0:T(1,128)} %copy.20), calls=%async_computation | async-start | bytes 16384 | tf_op jit(solution)/shard_map/all_to_all | solution.py:174
  9.6 1.0 constant_dynamic-slice_fusion.1
  10.6 6.4 %all-to-all-done = s32[16,1,8]{2,1,0:T(1,128)S(1)} async-done(((s32[16,1,8]{2,1,0:T(1,128)}), s32[16,1,8]{2,1,0:T(1,128)S(1)}, u32[]{:S(2)}, u32[]{:S(2)}) %all-to-all-start) | async-done | bytes 544 | tf_op jit(solution)/shard_map/all_to_all | solution.py:174
  17.3 0.8 gather_fusion
  18.1 18.7 %all_to_all.32 = bf16[16,8,32,128]{3,2,1,0:T(8,128)(2,1)S(1)} all-to-all(bf16[16,8,32,128]{3,2,1,0:T(8,128)(2,1)S(1)} %bitcast.195), channel_id=1, replica_groups=mesh['rows'=16,'rep'=8] {'rows'}, dimensions={0} | all-to-all | bytes 2097152 | tf_op jit(solution)/shard_map/all_to_all | solution.py:191
  36.9 1.6 collective-permute-start.2
  39.2 1.8 collective-permute-start.4
  41.9 3.5 %load_live.3.vals = bf16[512,128,128]{2,1,0:T(8,128)(2,1)S(1)} custom-call(s32[11]{0:T(128)S(1)} %stack.52.scalar, bf16[512,128,128]{2,1,0:T(8,128)(2,1)} %bitcast.187, bf16[128,16,128]{2,1,0:T(8,128)(2,1)S(1)} %get-tuple-element.24.after), custom_call_target="tpu_custom_call" | custom-call | tf_op jit(solution)/shard_map/load_live/pallas_call | solution.py:96
  45.4 4.0 %collective-permute-done.2 = bf16[128,16,128]{2,1,0:T(8,128)(2,1)S(1)} collective-permute-done((bf16[128,16,128]{2,1,0:T(8,128)(2,1)S(1)}, bf16[128,16,128]{2,1,0:T(8,128)(2,1)S(1)}, u32[]{:S(2)}, u32[]{:S(2)}) %collective-permute-start.2) | collective-permute-done | bytes 524320 | tf_op jit(solution)/shard_map/ppermute | solution.py:136
  49.6 4.0 %collective-permute-done.4 = bf16[128,16,128]{2,1,0:T(8,128)(2,1)S(1)} collective-permute-done((bf16[128,16,128]{2,1,0:T(8,128)(2,1)S(1)}, bf16[128,16,128]{2,1,0:T(8,128)(2,1)S(1)}, u32[]{:S(2)}, u32[]{:S(2)}) %collective-permute-start.4) | collective-permute-done | bytes 524320 | tf_op jit(solution)/shard_map/ppermute | solution.py:136
  53.9 1.6 collective-permute-done.5
  55.6 3.9 %tile_sums.3 = (bf16[4,32,16,128]{3,2,1,0:T(8,128)(2,1)S(1)}, f32[4,32,16,128]{3,2,1,0:T(8,128)S(1)}) custom-call(s32[11]{0:T(128)S(1)} %stack.52.scalar, s32[512]{0:T(512)S(1)} %bitcast.181, s32[512]{0:T(512)S(1)} %bitcast.184, bf16[8,128,16,128]{3,2,1,0:T(8,128)(2,1)S(1)} %bitcast_dynamic-update-slice_fusion.12.fetched, ...), custom_call_target="tpu_custom_call" | custom-call | tf_op jit(solution)/shard_map/tile_sums/pallas_call | solution.py:57
  60.2 1.5 collective-permute-done.6
  62.5 4.4 %collective-permute-start.8 = (bf16[32,16,128]{2,1,0:T(8,128)(2,1)S(1)}, bf16[32,16,128]{2,1,0:T(8,128)(2,1)S(1)}, u32[]{:S(2)}, u32[]{:S(2)}) collective-permute-start(bf16[32,16,128]{2,1,0:T(8,128)(2,1)S(1)} %get-tuple-element.35), channel_id=1, source_target_pairs={{4,0},{5,1},{6,2},{7,3},{0,4},{1,5},{2,6},{3,7},{12,8},{13,9},{14,... | collective-permute-start | bytes 393224 | tf_op jit(solution)/shard_map/ppermute | solution.py:136
  66.9 2.6 %collective-permute-done.7 = bf16[32,16,128]{2,1,0:T(8,128)(2,1)S(1)} collective-permute-done((bf16[32,16,128]{2,1,0:T(8,128)(2,1)S(1)}, bf16[32,16,128]{2,1,0:T(8,128)(2,1)S(1)}, u32[]{:S(2)}, u32[]{:S(2)}) %collective-permute-start.7) | collective-permute-done | bytes 131104 | tf_op jit(solution)/shard_map/ppermute | solution.py:136
  69.5 4.0 %collective-permute-done.8 = bf16[32,16,128]{2,1,0:T(8,128)(2,1)S(1)} collective-permute-done((bf16[32,16,128]{2,1,0:T(8,128)(2,1)S(1)}, bf16[32,16,128]{2,1,0:T(8,128)(2,1)S(1)}, u32[]{:S(2)}, u32[]{:S(2)}) %collective-permute-start.8) | collective-permute-done | bytes 131104 | tf_op jit(solution)/shard_map/ppermute | solution.py:136
  73.5 0.7 gather_fusion.1
  74.2 17.8 %all_to_all.33 = bf16[16,8,16,128]{3,2,1,0:T(8,128)(2,1)S(1)} all-to-all(bf16[16,8,16,128]{3,2,1,0:T(8,128)(2,1)S(1)} %bitcast.197), channel_id=1, replica_groups=mesh['rows'=16,'rep'=8] {'rows'}, dimensions={0} | all-to-all | bytes 1048576 | tf_op jit(solution)/shard_map/all_to_all | solution.py:195
  92.4 3.0 %collective-permute-start.13 = (bf16[128,16,128]{2,1,0:T(8,128)(2,1)S(1)}, bf16[128,16,128]{2,1,0:T(8,128)(2,1)S(1)}, u32[]{:S(2)}, u32[]{:S(2)}) collective-permute-start(bf16[128,16,128]{2,1,0:T(8,128)(2,1)S(1)} %bitcast.177), channel_id=1, source_target_pairs={{2,0},{3,1},{4,2},{5,3},{6,4},{7,5},{0,6},{1,7},{10,8},{11,9},{12,... | collective-permute-start | bytes 1572872 | tf_op jit(solution)/shard_map/ppermute | solution.py:136
  95.3 9.9 %collective-permute-done.11 = bf16[128,16,128]{2,1,0:T(8,128)(2,1)S(1)} collective-permute-done((bf16[128,16,128]{2,1,0:T(8,128)(2,1)S(1)}, bf16[128,16,128]{2,1,0:T(8,128)(2,1)S(1)}, u32[]{:S(2)}, u32[]{:S(2)}) %collective-permute-start.11) | collective-permute-done | bytes 524320 | tf_op jit(solution)/shard_map/ppermute | solution.py:136
  105.9 3.5 %load_live.4.vals = bf16[512,128,128]{2,1,0:T(8,128)(2,1)S(1)} custom-call(s32[11]{0:T(128)S(1)} %stack.52.scalar, bf16[512,128,128]{2,1,0:T(8,128)(2,1)} %bitcast.188, bf16[128,16,128]{2,1,0:T(8,128)(2,1)S(1)} %bitcast.180), custom_call_target="tpu_custom_call" | custom-call | tf_op jit(solution)/shard_map/load_live/pallas_call | solution.py:96
  109.6 3.3 %collective-permute-start.17 = (bf16[64,16,128]{2,1,0:T(8,128)(2,1)S(1)}, bf16[64,16,128]{2,1,0:T(8,128)(2,1)S(1)}, u32[]{:S(2)}, u32[]{:S(2)}) collective-permute-start(bf16[64,16,128]{2,1,0:T(8,128)(2,1)S(1)} %slice.120), channel_id=1, source_target_pairs={{2,0},{3,1},{4,2},{5,3},{6,4},{7,5},{0,6},{1,7},{10,8},{11,9},{12,... | collective-permute-start | bytes 786440 | tf_op jit(solution)/shard_map/ppermute | solution.py:136
  113.2 6.5 %collective-permute-done.15 = bf16[64,16,128]{2,1,0:T(8,128)(2,1)S(1)} collective-permute-done((bf16[64,16,128]{2,1,0:T(8,128)(2,1)S(1)}, bf16[64,16,128]{2,1,0:T(8,128)(2,1)S(1)}, u32[]{:S(2)}, u32[]{:S(2)}) %collective-permute-start.15) | collective-permute-done | bytes 262176 | tf_op jit(solution)/shard_map/ppermute | solution.py:136
  120.5 0.7 collective-permute-done.16
  121.7 3.9 %tile_sums.4 = (bf16[4,32,16,128]{3,2,1,0:T(8,128)(2,1)S(1)}, f32[4,32,16,128]{3,2,1,0:T(8,128)S(1)}) custom-call(s32[11]{0:T(128)S(1)} %stack.52.scalar, s32[512]{0:T(512)S(1)} %bitcast.182, s32[512]{0:T(512)S(1)} %bitcast.185, bf16[8,128,16,128]{3,2,1,0:T(8,128)(2,1)S(1)} %bitcast_dynamic-update-slice_fusion.24.fetched, ...), custom_call_target="tpu_custom_call" | custom-call | tf_op jit(solution)/shard_map/tile_sums/pallas_call | solution.py:57
  125.6 0.9 collective-permute-start.19
  126.4 1.5 collective-permute-done.19
  128.3 4.6 %collective-permute-start.21 = (bf16[32,16,128]{2,1,0:T(8,128)(2,1)S(1)}, bf16[32,16,128]{2,1,0:T(8,128)(2,1)S(1)}, u32[]{:S(2)}, u32[]{:S(2)}) collective-permute-start(bf16[32,16,128]{2,1,0:T(8,128)(2,1)S(1)} %get-tuple-element.32), channel_id=1, source_target_pairs={{4,0},{5,1},{6,2},{7,3},{0,4},{1,5},{2,6},{3,7},{12,8},{13,9},{14,... | collective-permute-start | bytes 393224 | tf_op jit(solution)/shard_map/ppermute | solution.py:136
  132.9 2.6 %collective-permute-done.20 = bf16[32,16,128]{2,1,0:T(8,128)(2,1)S(1)} collective-permute-done((bf16[32,16,128]{2,1,0:T(8,128)(2,1)S(1)}, bf16[32,16,128]{2,1,0:T(8,128)(2,1)S(1)}, u32[]{:S(2)}, u32[]{:S(2)}) %collective-permute-start.20) | collective-permute-done | bytes 131104 | tf_op jit(solution)/shard_map/ppermute | solution.py:136
  135.5 4.0 %collective-permute-done.21 = bf16[32,16,128]{2,1,0:T(8,128)(2,1)S(1)} collective-permute-done((bf16[32,16,128]{2,1,0:T(8,128)(2,1)S(1)}, bf16[32,16,128]{2,1,0:T(8,128)(2,1)S(1)}, u32[]{:S(2)}, u32[]{:S(2)}) %collective-permute-start.21) | collective-permute-done | bytes 131104 | tf_op jit(solution)/shard_map/ppermute | solution.py:136
  139.5 0.7 gather_fusion.2
  140.3 18.9 %all_to_all.34 = bf16[16,8,16,128]{3,2,1,0:T(8,128)(2,1)S(1)} all-to-all(bf16[16,8,16,128]{3,2,1,0:T(8,128)(2,1)S(1)} %bitcast.196), channel_id=1, replica_groups=mesh['rows'=16,'rep'=8] {'rows'}, dimensions={0} | all-to-all | bytes 1048576 | tf_op jit(solution)/shard_map/all_to_all | solution.py:195
  159.4 3.0 %collective-permute-start.26 = (bf16[128,16,128]{2,1,0:T(8,128)(2,1)S(1)}, bf16[128,16,128]{2,1,0:T(8,128)(2,1)S(1)}, u32[]{:S(2)}, u32[]{:S(2)}) collective-permute-start(bf16[128,16,128]{2,1,0:T(8,128)(2,1)S(1)} %bitcast.172), channel_id=1, source_target_pairs={{2,0},{3,1},{4,2},{5,3},{6,4},{7,5},{0,6},{1,7},{10,8},{11,9},{12,... | collective-permute-start | bytes 1572872 | tf_op jit(solution)/shard_map/ppermute | solution.py:136
  162.4 0.7 pad_maximum_fusion.1
  163.1 3.4 %all-to-all-start.3 = ((bf16[8,4,2,16,128]{4,3,1,2,0:T(8,128)(2,1)}), bf16[8,4,2,16,128]{4,3,1,2,0:T(8,128)(2,1)S(1)}, u32[]{:S(2)}, u32[]{:S(2)}) async-start(bf16[8,4,2,16,128]{4,3,1,2,0:T(8,128)(2,1)} %pad_maximum_fusion.1), calls=%async_computation.3 | async-start | bytes 524288 | tf_op jit(solution)/shard_map/all_to_all | solution.py:186
  166.5 7.0 %collective-permute-done.24 = bf16[128,16,128]{2,1,0:T(8,128)(2,1)S(1)} collective-permute-done((bf16[128,16,128]{2,1,0:T(8,128)(2,1)S(1)}, bf16[128,16,128]{2,1,0:T(8,128)(2,1)S(1)}, u32[]{:S(2)}, u32[]{:S(2)}) %collective-permute-start.24) | collective-permute-done | bytes 524320 | tf_op jit(solution)/shard_map/ppermute | solution.py:136
  174.1 3.5 %load_live.5.vals = bf16[512,128,128]{2,1,0:T(8,128)(2,1)S(1)} custom-call(s32[11]{0:T(128)S(1)} %stack.52.scalar, bf16[512,128,128]{2,1,0:T(8,128)(2,1)} %bitcast.189, bf16[128,16,128]{2,1,0:T(8,128)(2,1)S(1)} %bitcast.175), custom_call_target="tpu_custom_call" | custom-call | tf_op jit(solution)/shard_map/load_live/pallas_call | solution.py:96
  177.8 3.3 %collective-permute-start.30 = (bf16[64,16,128]{2,1,0:T(8,128)(2,1)S(1)}, bf16[64,16,128]{2,1,0:T(8,128)(2,1)S(1)}, u32[]{:S(2)}, u32[]{:S(2)}) collective-permute-start(bf16[64,16,128]{2,1,0:T(8,128)(2,1)S(1)} %slice.128), channel_id=1, source_target_pairs={{2,0},{3,1},{4,2},{5,3},{6,4},{7,5},{0,6},{1,7},{10,8},{11,9},{12,... | collective-permute-start | bytes 786440 | tf_op jit(solution)/shard_map/ppermute | solution.py:136
  181.5 6.5 %collective-permute-done.28 = bf16[64,16,128]{2,1,0:T(8,128)(2,1)S(1)} collective-permute-done((bf16[64,16,128]{2,1,0:T(8,128)(2,1)S(1)}, bf16[64,16,128]{2,1,0:T(8,128)(2,1)S(1)}, u32[]{:S(2)}, u32[]{:S(2)}) %collective-permute-start.28) | collective-permute-done | bytes 262176 | tf_op jit(solution)/shard_map/ppermute | solution.py:136
  188.8 0.7 collective-permute-done.29
  190.0 3.9 %tile_sums.5 = (bf16[4,32,16,128]{3,2,1,0:T(8,128)(2,1)S(1)}, f32[4,32,16,128]{3,2,1,0:T(8,128)S(1)}) custom-call(s32[11]{0:T(128)S(1)} %stack.52.scalar, s32[512]{0:T(512)S(1)} %bitcast.183, s32[512]{0:T(512)S(1)} %bitcast.186, bf16[8,128,16,128]{3,2,1,0:T(8,128)(2,1)S(1)} %bitcast_dynamic-update-slice_fusion.20.fetched, ...), custom_call_target="tpu_custom_call" | custom-call | tf_op jit(solution)/shard_map/tile_sums/pallas_call | solution.py:57
  193.8 0.7 collective-permute-start.32
  194.5 1.1 fusion.17
  196.3 4.6 %collective-permute-start.34 = (bf16[32,16,128]{2,1,0:T(8,128)(2,1)S(1)}, bf16[32,16,128]{2,1,0:T(8,128)(2,1)S(1)}, u32[]{:S(2)}, u32[]{:S(2)}) collective-permute-start(bf16[32,16,128]{2,1,0:T(8,128)(2,1)S(1)} %get-tuple-element.29), channel_id=1, source_target_pairs={{4,0},{5,1},{6,2},{7,3},{0,4},{1,5},{2,6},{3,7},{12,8},{13,9},{14,... | collective-permute-start | bytes 393224 | tf_op jit(solution)/shard_map/ppermute | solution.py:136
  201.1 2.4 %collective-permute-done.33 = bf16[32,16,128]{2,1,0:T(8,128)(2,1)S(1)} collective-permute-done((bf16[32,16,128]{2,1,0:T(8,128)(2,1)S(1)}, bf16[32,16,128]{2,1,0:T(8,128)(2,1)S(1)}, u32[]{:S(2)}, u32[]{:S(2)}) %collective-permute-start.33) | collective-permute-done | bytes 131104 | tf_op jit(solution)/shard_map/ppermute | solution.py:136
  203.5 4.0 %collective-permute-done.34 = bf16[32,16,128]{2,1,0:T(8,128)(2,1)S(1)} collective-permute-done((bf16[32,16,128]{2,1,0:T(8,128)(2,1)S(1)}, bf16[32,16,128]{2,1,0:T(8,128)(2,1)S(1)}, u32[]{:S(2)}, u32[]{:S(2)}) %collective-permute-start.34) | collective-permute-done | bytes 131104 | tf_op jit(solution)/shard_map/ppermute | solution.py:136
  207.6 0.9 fusion
  (107 shorter events, 10.0 us)
Async XLA Ops:
  1.4 15.7 %all-to-all-start = ((s32[16,1,8]{2,1,0:T(1,128)}), s32[16,1,8]{2,1,0:T(1,128)S(1)}, u32[]{:S(2)}, u32[]{:S(2)}) async-start(s32[16,1,8]{2,1,0:T(1,128)} %copy.20), calls=%async_computation | async-start | bytes 16384 | tf_op jit(solution)/shard_map/all_to_all | solution.py:174
  36.9 12.5 %collective-permute-start.2 = (bf16[128,16,128]{2,1,0:T(8,128)(2,1)S(1)}, bf16[128,16,128]{2,1,0:T(8,128)(2,1)S(1)}, u32[]{:S(2)}, u32[]{:S(2)}) collective-permute-start(bf16[128,16,128]{2,1,0:T(8,128)(2,1)S(1)} %get-tuple-element.24.after), channel_id=1, source_target_pairs={{6,0},{7,1},{0,2},{1,3},{2,4},{3,5},{4,6},{5,7},{14,8},{15,9},{8,1... | collective-permute-start | bytes 1572872 | tf_op jit(solution)/shard_map/ppermute | solution.py:136
  38.5 11.0 %collective-permute-start = (bf16[128,16,128]{2,1,0:T(8,128)(2,1)S(1)}, bf16[128,16,128]{2,1,0:T(8,128)(2,1)S(1)}, u32[]{:S(2)}, u32[]{:S(2)}) collective-permute-start(bf16[128,16,128]{2,1,0:T(8,128)(2,1)S(1)} %get-tuple-element.24.after), channel_id=1, source_target_pairs={{0,1},{1,0},{2,3},{3,2},{4,5},{5,4},{6,7},{7,6},{8,9},{9,8},{10,11... | collective-permute-start | bytes 1572872 | tf_op jit(solution)/shard_map/ppermute | solution.py:139
  39.2 14.4 %collective-permute-start.4 = (bf16[128,16,128]{2,1,0:T(8,128)(2,1)S(1)}, bf16[128,16,128]{2,1,0:T(8,128)(2,1)S(1)}, u32[]{:S(2)}, u32[]{:S(2)}) collective-permute-start(bf16[128,16,128]{2,1,0:T(8,128)(2,1)S(1)} %get-tuple-element.24.after), channel_id=1, source_target_pairs={{2,0},{3,1},{4,2},{5,3},{6,4},{7,5},{0,6},{1,7},{10,8},{11,9},{12,... | collective-permute-start | bytes 1572872 | tf_op jit(solution)/shard_map/ppermute | solution.py:136
  41.0 12.6 %collective-permute-start.1 = (bf16[128,16,128]{2,1,0:T(8,128)(2,1)S(1)}, bf16[128,16,128]{2,1,0:T(8,128)(2,1)S(1)}, u32[]{:S(2)}, u32[]{:S(2)}) collective-permute-start(bf16[128,16,128]{2,1,0:T(8,128)(2,1)S(1)} %get-tuple-element.23), channel_id=1, source_target_pairs={{0,1},{1,0},{2,3},{3,2},{4,5},{5,4},{6,7},{7,6},{8,9},{9,8},{10,11... | collective-permute-start | bytes 1572872 | tf_op jit(solution)/shard_map/ppermute | solution.py:139
  45.4 10.2 %copy-start = (s32[1,1,512]{2,1,0:T(1,128)S(1)}, s32[1,1,512]{2,1,0:T(1,128)}, u32[]{:S(2)}) copy-start(s32[1,1,512]{2,1,0:T(1,128)} %param.9) | copy-start | bytes 6148
  45.4 10.2 %copy-start.1 = (s32[1,1,512]{2,1,0:T(1,128)S(1)}, s32[1,1,512]{2,1,0:T(1,128)}, u32[]{:S(2)}) copy-start(s32[1,1,512]{2,1,0:T(1,128)} %param.10) | copy-start | bytes 6148
  49.4 4.3 %collective-permute-start.3 = (bf16[128,16,128]{2,1,0:T(8,128)(2,1)S(1)}, bf16[128,16,128]{2,1,0:T(8,128)(2,1)S(1)}, u32[]{:S(2)}, u32[]{:S(2)}) collective-permute-start(bf16[128,16,128]{2,1,0:T(8,128)(2,1)S(1)} %collective-permute-done.2), channel_id=1, source_target_pairs={{0,1},{1,0},{2,3},{3,2},{4,5},{5,4},{6,7},{7,6},{8,9},{9,8},{10,11... | collective-permute-start | bytes 1572872 | tf_op jit(solution)/shard_map/ppermute | solution.py:139
  53.6 1.9 collective-permute-start.5
  59.5 2.2 %collective-permute-start.6 = (bf16[4,32,16,128]{3,2,1,0:T(8,128)(2,1)S(1)}, bf16[4,32,16,128]{3,2,1,0:T(8,128)(2,1)S(1)}, u32[]{:S(2)}, u32[]{:S(2)}) collective-permute-start(bf16[4,32,16,128]{3,2,1,0:T(8,128)(2,1)S(1)} %get-tuple-element.12), channel_id=1, source_target_pairs={{0,1},{1,0},{2,3},{3,2},{4,5},{5,4},{6,7},{7,6},{8,9},{9,8},{10,11... | collective-permute-start | bytes 1572872 | tf_op jit(solution)/shard_map/ppermute | solution.py:139
  61.9 7.6 %collective-permute-start.7 = (bf16[32,16,128]{2,1,0:T(8,128)(2,1)S(1)}, bf16[32,16,128]{2,1,0:T(8,128)(2,1)S(1)}, u32[]{:S(2)}, u32[]{:S(2)}) collective-permute-start(bf16[32,16,128]{2,1,0:T(8,128)(2,1)S(1)} %get-tuple-element.33), channel_id=1, source_target_pairs={{6,0},{7,1},{0,2},{1,3},{2,4},{3,5},{4,6},{5,7},{14,8},{15,9},{8,1... | collective-permute-start | bytes 393224 | tf_op jit(solution)/shard_map/ppermute | solution.py:136
  62.5 10.9 %collective-permute-start.8 = (bf16[32,16,128]{2,1,0:T(8,128)(2,1)S(1)}, bf16[32,16,128]{2,1,0:T(8,128)(2,1)S(1)}, u32[]{:S(2)}, u32[]{:S(2)}) collective-permute-start(bf16[32,16,128]{2,1,0:T(8,128)(2,1)S(1)} %get-tuple-element.35), channel_id=1, source_target_pairs={{4,0},{5,1},{6,2},{7,3},{0,4},{1,5},{2,6},{3,7},{12,8},{13,9},{14,... | collective-permute-start | bytes 393224 | tf_op jit(solution)/shard_map/ppermute | solution.py:136
  66.9 6.6 %collective-permute-start.9 = (bf16[32,16,128]{2,1,0:T(8,128)(2,1)S(1)}, bf16[32,16,128]{2,1,0:T(8,128)(2,1)S(1)}, u32[]{:S(2)}, u32[]{:S(2)}) collective-permute-start(bf16[32,16,128]{2,1,0:T(8,128)(2,1)S(1)} %get-tuple-element.34), channel_id=1, source_target_pairs={{2,0},{3,1},{4,2},{5,3},{6,4},{7,5},{0,6},{1,7},{10,8},{11,9},{12,... | collective-permute-start | bytes 393224 | tf_op jit(solution)/shard_map/ppermute | solution.py:136
  92.1 13.2 %collective-permute-start.11 = (bf16[128,16,128]{2,1,0:T(8,128)(2,1)S(1)}, bf16[128,16,128]{2,1,0:T(8,128)(2,1)S(1)}, u32[]{:S(2)}, u32[]{:S(2)}) collective-permute-start(bf16[128,16,128]{2,1,0:T(8,128)(2,1)S(1)} %bitcast.176), channel_id=1, source_target_pairs={{6,0},{7,1},{0,2},{1,3},{2,4},{3,5},{4,6},{5,7},{14,8},{15,9},{8,1... | collective-permute-start | bytes 1572872 | tf_op jit(solution)/shard_map/ppermute | solution.py:136
  92.4 17.2 %collective-permute-start.13 = (bf16[128,16,128]{2,1,0:T(8,128)(2,1)S(1)}, bf16[128,16,128]{2,1,0:T(8,128)(2,1)S(1)}, u32[]{:S(2)}, u32[]{:S(2)}) collective-permute-start(bf16[128,16,128]{2,1,0:T(8,128)(2,1)S(1)} %bitcast.177), channel_id=1, source_target_pairs={{2,0},{3,1},{4,2},{5,3},{6,4},{7,5},{0,6},{1,7},{10,8},{11,9},{12,... | collective-permute-start | bytes 1572872 | tf_op jit(solution)/shard_map/ppermute | solution.py:136
  95.3 17.8 %collective-permute-start.10 = (bf16[128,16,128]{2,1,0:T(8,128)(2,1)S(1)}, bf16[128,16,128]{2,1,0:T(8,128)(2,1)S(1)}, u32[]{:S(2)}, u32[]{:S(2)}) collective-permute-start(bf16[128,16,128]{2,1,0:T(8,128)(2,1)S(1)} %bitcast.178), channel_id=1, source_target_pairs={{0,1},{1,0},{2,3},{3,2},{4,5},{5,4},{6,7},{7,6},{8,9},{9,8},{10,11... | collective-permute-start | bytes 1572872 | tf_op jit(solution)/shard_map/ppermute | solution.py:139
  105.3 15.0 %collective-permute-start.12 = (bf16[128,16,128]{2,1,0:T(8,128)(2,1)S(1)}, bf16[128,16,128]{2,1,0:T(8,128)(2,1)S(1)}, u32[]{:S(2)}, u32[]{:S(2)}) collective-permute-start(bf16[128,16,128]{2,1,0:T(8,128)(2,1)S(1)} %collective-permute-done.11), channel_id=1, source_target_pairs={{0,1},{1,0},{2,3},{3,2},{4,5},{5,4},{6,7},{7,6},{8,9},{9,8},{10,11... | collective-permute-start | bytes 1572872 | tf_op jit(solution)/shard_map/ppermute | solution.py:139
  109.4 10.3 %collective-permute-start.15 = (bf16[64,16,128]{2,1,0:T(8,128)(2,1)S(1)}, bf16[64,16,128]{2,1,0:T(8,128)(2,1)S(1)}, u32[]{:S(2)}, u32[]{:S(2)}) collective-permute-start(bf16[64,16,128]{2,1,0:T(8,128)(2,1)S(1)} %slice.119), channel_id=1, source_target_pairs={{6,0},{7,1},{0,2},{1,3},{2,4},{3,5},{4,6},{5,7},{14,8},{15,9},{8,1... | collective-permute-start | bytes 786440 | tf_op jit(solution)/shard_map/ppermute | solution.py:136
  109.6 10.2 %collective-permute-start.17 = (bf16[64,16,128]{2,1,0:T(8,128)(2,1)S(1)}, bf16[64,16,128]{2,1,0:T(8,128)(2,1)S(1)}, u32[]{:S(2)}, u32[]{:S(2)}) collective-permute-start(bf16[64,16,128]{2,1,0:T(8,128)(2,1)S(1)} %slice.120), channel_id=1, source_target_pairs={{2,0},{3,1},{4,2},{5,3},{6,4},{7,5},{0,6},{1,7},{10,8},{11,9},{12,... | collective-permute-start | bytes 786440 | tf_op jit(solution)/shard_map/ppermute | solution.py:136
  112.8 7.6 %collective-permute-start.14 = (bf16[128,16,128]{2,1,0:T(8,128)(2,1)S(1)}, bf16[128,16,128]{2,1,0:T(8,128)(2,1)S(1)}, u32[]{:S(2)}, u32[]{:S(2)}) collective-permute-start(bf16[128,16,128]{2,1,0:T(8,128)(2,1)S(1)} %collective-permute-done.13), channel_id=1, source_target_pairs={{0,1},{1,0},{2,3},{3,2},{4,5},{5,4},{6,7},{7,6},{8,9},{9,8},{10,11... | collective-permute-start | bytes 1572872 | tf_op jit(solution)/shard_map/ppermute | solution.py:139
  119.7 1.5 collective-permute-start.16
  119.7 1.9 collective-permute-start.18
  125.6 2.4 %collective-permute-start.19 = (bf16[4,32,16,128]{3,2,1,0:T(8,128)(2,1)S(1)}, bf16[4,32,16,128]{3,2,1,0:T(8,128)(2,1)S(1)}, u32[]{:S(2)}, u32[]{:S(2)}) collective-permute-start(bf16[4,32,16,128]{3,2,1,0:T(8,128)(2,1)S(1)} %get-tuple-element.14), channel_id=1, source_target_pairs={{0,1},{1,0},{2,3},{3,2},{4,5},{5,4},{6,7},{7,6},{8,9},{9,8},{10,11... | collective-permute-start | bytes 1572872 | tf_op jit(solution)/shard_map/ppermute | solution.py:139
  128.2 7.3 %collective-permute-start.20 = (bf16[32,16,128]{2,1,0:T(8,128)(2,1)S(1)}, bf16[32,16,128]{2,1,0:T(8,128)(2,1)S(1)}, u32[]{:S(2)}, u32[]{:S(2)}) collective-permute-start(bf16[32,16,128]{2,1,0:T(8,128)(2,1)S(1)} %get-tuple-element.30), channel_id=1, source_target_pairs={{6,0},{7,1},{0,2},{1,3},{2,4},{3,5},{4,6},{5,7},{14,8},{15,9},{8,1... | collective-permute-start | bytes 393224 | tf_op jit(solution)/shard_map/ppermute | solution.py:136
  128.3 11.2 %collective-permute-start.21 = (bf16[32,16,128]{2,1,0:T(8,128)(2,1)S(1)}, bf16[32,16,128]{2,1,0:T(8,128)(2,1)S(1)}, u32[]{:S(2)}, u32[]{:S(2)}) collective-permute-start(bf16[32,16,128]{2,1,0:T(8,128)(2,1)S(1)} %get-tuple-element.32), channel_id=1, source_target_pairs={{4,0},{5,1},{6,2},{7,3},{0,4},{1,5},{2,6},{3,7},{12,8},{13,9},{14,... | collective-permute-start | bytes 393224 | tf_op jit(solution)/shard_map/ppermute | solution.py:136
  132.9 6.6 %collective-permute-start.22 = (bf16[32,16,128]{2,1,0:T(8,128)(2,1)S(1)}, bf16[32,16,128]{2,1,0:T(8,128)(2,1)S(1)}, u32[]{:S(2)}, u32[]{:S(2)}) collective-permute-start(bf16[32,16,128]{2,1,0:T(8,128)(2,1)S(1)} %get-tuple-element.31), channel_id=1, source_target_pairs={{2,0},{3,1},{4,2},{5,3},{6,4},{7,5},{0,6},{1,7},{10,8},{11,9},{12,... | collective-permute-start | bytes 393224 | tf_op jit(solution)/shard_map/ppermute | solution.py:136
  159.2 14.4 %collective-permute-start.24 = (bf16[128,16,128]{2,1,0:T(8,128)(2,1)S(1)}, bf16[128,16,128]{2,1,0:T(8,128)(2,1)S(1)}, u32[]{:S(2)}, u32[]{:S(2)}) collective-permute-start(bf16[128,16,128]{2,1,0:T(8,128)(2,1)S(1)} %bitcast.171), channel_id=1, source_target_pairs={{6,0},{7,1},{0,2},{1,3},{2,4},{3,5},{4,6},{5,7},{14,8},{15,9},{8,1... | collective-permute-start | bytes 1572872 | tf_op jit(solution)/shard_map/ppermute | solution.py:136
  159.4 18.3 %collective-permute-start.26 = (bf16[128,16,128]{2,1,0:T(8,128)(2,1)S(1)}, bf16[128,16,128]{2,1,0:T(8,128)(2,1)S(1)}, u32[]{:S(2)}, u32[]{:S(2)}) collective-permute-start(bf16[128,16,128]{2,1,0:T(8,128)(2,1)S(1)} %bitcast.172), channel_id=1, source_target_pairs={{2,0},{3,1},{4,2},{5,3},{6,4},{7,5},{0,6},{1,7},{10,8},{11,9},{12,... | collective-permute-start | bytes 1572872 | tf_op jit(solution)/shard_map/ppermute | solution.py:136
  162.4 19.0 %collective-permute-start.23 = (bf16[128,16,128]{2,1,0:T(8,128)(2,1)S(1)}, bf16[128,16,128]{2,1,0:T(8,128)(2,1)S(1)}, u32[]{:S(2)}, u32[]{:S(2)}) collective-permute-start(bf16[128,16,128]{2,1,0:T(8,128)(2,1)S(1)} %bitcast.173), channel_id=1, source_target_pairs={{0,1},{1,0},{2,3},{3,2},{4,5},{5,4},{6,7},{7,6},{8,9},{9,8},{10,11... | collective-permute-start | bytes 1572872 | tf_op jit(solution)/shard_map/ppermute | solution.py:139
  163.1 32.5 %all-to-all-start.3 = ((bf16[8,4,2,16,128]{4,3,1,2,0:T(8,128)(2,1)}), bf16[8,4,2,16,128]{4,3,1,2,0:T(8,128)(2,1)S(1)}, u32[]{:S(2)}, u32[]{:S(2)}) async-start(bf16[8,4,2,16,128]{4,3,1,2,0:T(8,128)(2,1)} %pad_maximum_fusion.1), calls=%async_computation.3 | async-start | bytes 524288 | tf_op jit(solution)/shard_map/all_to_all | solution.py:186
  173.5 15.0 %collective-permute-start.25 = (bf16[128,16,128]{2,1,0:T(8,128)(2,1)S(1)}, bf16[128,16,128]{2,1,0:T(8,128)(2,1)S(1)}, u32[]{:S(2)}, u32[]{:S(2)}) collective-permute-start(bf16[128,16,128]{2,1,0:T(8,128)(2,1)S(1)} %collective-permute-done.24), channel_id=1, source_target_pairs={{0,1},{1,0},{2,3},{3,2},{4,5},{5,4},{6,7},{7,6},{8,9},{9,8},{10,11... | collective-permute-start | bytes 1572872 | tf_op jit(solution)/shard_map/ppermute | solution.py:139
  177.7 10.3 %collective-permute-start.28 = (bf16[64,16,128]{2,1,0:T(8,128)(2,1)S(1)}, bf16[64,16,128]{2,1,0:T(8,128)(2,1)S(1)}, u32[]{:S(2)}, u32[]{:S(2)}) collective-permute-start(bf16[64,16,128]{2,1,0:T(8,128)(2,1)S(1)} %slice.127), channel_id=1, source_target_pairs={{6,0},{7,1},{0,2},{1,3},{2,4},{3,5},{4,6},{5,7},{14,8},{15,9},{8,1... | collective-permute-start | bytes 786440 | tf_op jit(solution)/shard_map/ppermute | solution.py:136
  177.8 10.2 %collective-permute-start.30 = (bf16[64,16,128]{2,1,0:T(8,128)(2,1)S(1)}, bf16[64,16,128]{2,1,0:T(8,128)(2,1)S(1)}, u32[]{:S(2)}, u32[]{:S(2)}) collective-permute-start(bf16[64,16,128]{2,1,0:T(8,128)(2,1)S(1)} %slice.128), channel_id=1, source_target_pairs={{2,0},{3,1},{4,2},{5,3},{6,4},{7,5},{0,6},{1,7},{10,8},{11,9},{12,... | collective-permute-start | bytes 786440 | tf_op jit(solution)/shard_map/ppermute | solution.py:136
  181.1 7.6 %collective-permute-start.27 = (bf16[128,16,128]{2,1,0:T(8,128)(2,1)S(1)}, bf16[128,16,128]{2,1,0:T(8,128)(2,1)S(1)}, u32[]{:S(2)}, u32[]{:S(2)}) collective-permute-start(bf16[128,16,128]{2,1,0:T(8,128)(2,1)S(1)} %collective-permute-done.26), channel_id=1, source_target_pairs={{0,1},{1,0},{2,3},{3,2},{4,5},{5,4},{6,7},{7,6},{8,9},{9,8},{10,11... | collective-permute-start | bytes 1572872 | tf_op jit(solution)/shard_map/ppermute | solution.py:139
  188.0 1.5 collective-permute-start.29
  188.0 1.9 collective-permute-start.31
  189.9 4.6 %copy-start.2 = (bf16[4,128,256]{2,1,0:T(8,128)(2,1)S(1)}, bf16[4,128,256]{2,1,0:T(8,128)(2,1)}, u32[]{:S(2)}) copy-start(bf16[4,128,256]{2,1,0:T(8,128)(2,1)} %param.13) | copy-start | bytes 786436
  193.8 2.2 %collective-permute-start.32 = (bf16[4,32,16,128]{3,2,1,0:T(8,128)(2,1)S(1)}, bf16[4,32,16,128]{3,2,1,0:T(8,128)(2,1)S(1)}, u32[]{:S(2)}, u32[]{:S(2)}) collective-permute-start(bf16[4,32,16,128]{3,2,1,0:T(8,128)(2,1)S(1)} %get-tuple-element.16), channel_id=1, source_target_pairs={{0,1},{1,0},{2,3},{3,2},{4,5},{5,4},{6,7},{7,6},{8,9},{9,8},{10,11... | collective-permute-start | bytes 1572872 | tf_op jit(solution)/shard_map/ppermute | solution.py:139
  196.2 7.3 %collective-permute-start.33 = (bf16[32,16,128]{2,1,0:T(8,128)(2,1)S(1)}, bf16[32,16,128]{2,1,0:T(8,128)(2,1)S(1)}, u32[]{:S(2)}, u32[]{:S(2)}) collective-permute-start(bf16[32,16,128]{2,1,0:T(8,128)(2,1)S(1)} %get-tuple-element.27), channel_id=1, source_target_pairs={{6,0},{7,1},{0,2},{1,3},{2,4},{3,5},{4,6},{5,7},{14,8},{15,9},{8,1... | collective-permute-start | bytes 393224 | tf_op jit(solution)/shard_map/ppermute | solution.py:136
  196.3 11.2 %collective-permute-start.34 = (bf16[32,16,128]{2,1,0:T(8,128)(2,1)S(1)}, bf16[32,16,128]{2,1,0:T(8,128)(2,1)S(1)}, u32[]{:S(2)}, u32[]{:S(2)}) collective-permute-start(bf16[32,16,128]{2,1,0:T(8,128)(2,1)S(1)} %get-tuple-element.29), channel_id=1, source_target_pairs={{4,0},{5,1},{6,2},{7,3},{0,4},{1,5},{2,6},{3,7},{12,8},{13,9},{14,... | collective-permute-start | bytes 393224 | tf_op jit(solution)/shard_map/ppermute | solution.py:136
  200.9 6.6 %collective-permute-start.35 = (bf16[32,16,128]{2,1,0:T(8,128)(2,1)S(1)}, bf16[32,16,128]{2,1,0:T(8,128)(2,1)S(1)}, u32[]{:S(2)}, u32[]{:S(2)}) collective-permute-start(bf16[32,16,128]{2,1,0:T(8,128)(2,1)S(1)} %get-tuple-element.28), channel_id=1, source_target_pairs={{2,0},{3,1},{4,2},{5,3},{6,4},{7,5},{0,6},{1,7},{10,8},{11,9},{12,... | collective-permute-start | bytes 393224 | tf_op jit(solution)/shard_map/ppermute | solution.py:136

commit v3 on v0

--- a/solution.py
+++ b/solution.py
@@ -74,13 +74,13 @@
     )
 
 
-def load_live(values, scalars, after):
-    def body(scalar, values, after, out, semaphore):
+def load_live(values, scalars, sent, replicas):
+    def body(scalar, values, sent, live, fetched, semaphore):
         groups = (scalar[0] + UNROLL - 1) // UNROLL
 
         def copy(step):
             part = pl.ds(step * UNROLL, UNROLL)
-            return pltpu.make_async_copy(values.at[part], out.at[part], semaphore.at[step])
+            return pltpu.make_async_copy(values.at[part], live.at[part], semaphore.at[step])
 
         def start(step, carry):
             copy(step).start()
@@ -91,21 +91,32 @@
             return carry
 
         lax.fori_loop(0, groups, start, 0)
+        fetched[pl.ds(scalar[3], 1)] = sent[...][None]
         lax.fori_loop(0, groups, wait, 0)
 
     return pl.pallas_call(
         body,
-        out_shape=pltpu.VMEM(values.shape, values.dtype),
+        out_shape=(
+            pltpu.VMEM(values.shape, values.dtype),
+            pltpu.VMEM((replicas, *sent.shape), sent.dtype),
+        ),
         in_specs=[
             pl.BlockSpec(memory_space=pltpu.SMEM),
             pl.BlockSpec(memory_space=pltpu.HBM),
-            pl.BlockSpec(memory_space=pl.ANY),
+            pl.BlockSpec(memory_space=pltpu.VMEM),
         ],
-        out_specs=pl.BlockSpec(memory_space=pltpu.VMEM),
+        out_specs=(
+            pl.BlockSpec(memory_space=pltpu.VMEM),
+            pl.BlockSpec(memory_space=pltpu.VMEM),
+        ),
         scratch_shapes=[pltpu.SemaphoreType.DMA((values.shape[0] // UNROLL,))],
         compiler_params=pltpu.CompilerParams(vmem_limit_bytes=2 * 2**20),
         name="load_live",
-    )(scalars, pltpu.with_memory_space_constraint(values, pltpu.HBM), after)
+    )(
+        scalars,
+        pltpu.with_memory_space_constraint(values, pltpu.HBM),
+        pltpu.with_memory_space_constraint(sent, pltpu.VMEM),
+    )
 
 
 def on_device(
@@ -139,16 +150,12 @@
         return lax.ppermute(x, "rep", [(i, i ^ 1) for i in range(replicas)])
 
     def gather(sent):
-        slots = sent.shape[0]
-        half = slots // 2
-        low, high = sent[:half], sent[half:]
-        before_low, after_high = along(low, -1), along(high, 1)
-        before_high, after_low = along(high, -1), along(low, 1)
-        other = partner(sent)
-        live = load_live(values, scalars, sent)
-        before_low, live = lax.optimization_barrier((before_low, live))
-        far_low, far_high = along(before_low, -1), along(after_high, 1)
-        fetched = jnp.zeros((replicas, slots, sub, width), sent.dtype)
+        half = sent.shape[0] // 2
+        before, after, other = along(sent, -1), along(sent, 1), partner(sent)
+        live, fetched = load_live(values, scalars, sent, replicas)
+        first, second = along(before[:half], -1), along(after[half:], 1)
+        crossed = [partner(before), partner(after)]
+        crossed += [partner(first), partner(second)]
 
         def put(fetched, array, hops, other_core, start):
             place = places[hops][other_core]
@@ -156,20 +163,19 @@
                 fetched, array[None], (place, start, 0, 0), allow_negative_indices=False
             )
 
-        fetched = put(fetched, sent, 0, 0, 0)
         fetched = put(fetched, other, 0, 1, 0)
-        for array, hops, start in (
-            (before_low, -1, 0),
-            (after_high, 1, half),
-            (before_high, -1, half),
-            (after_low, 1, 0),
-            (far_low, 2, 0),
-            (far_high, 2, half),
+        for array, across, hops, start in zip(
+            (before, after, first, second), crossed, (-1, 1, 2, 2), (0, 0, 0, half)
         ):
             fetched = put(fetched, array, hops, 0, start)
-            crossed = partner(array)
-            fetched = put(fetched, crossed, hops, 1, start)
+            fetched = put(fetched, across, hops, 1, start)
         return fetched, live
+
+    def swap(term):
+        parts = lax.all_to_all(
+            term.reshape(replicas, -1, sub, width), "rep", split_axis=0, concat_axis=0, tiled=True
+        )
+        return parts.transpose(1, 0, 2, 3).reshape(share_rows, width)
 
     def reduce(peer, mine):
         sums = mine + partner(peer).astype(jnp.float32)
@@ -184,22 +190,14 @@
         return total
 
     served = lax.all_to_all(wanted, "rows", split_axis=0, concat_axis=0, tiled=True)
-    terms = [
-        lax.dynamic_slice_in_dim(
-            features.reshape(row_blocks, tile, width), rank * sub, sub, 1
-        )
-    ]
+    blocks = features.reshape(row_blocks, tile, width)
+    terms = [lax.dynamic_slice_in_dim(blocks, rank * sub, sub, 1)]
     own = [lax.dynamic_slice_in_dim(features, rank * share_rows, share_rows, 0)]
 
     def step(degree):
         last = degree == degree_last
-        if last:
-            swapped = jnp.stack(terms[1:], 1).reshape(
-                replicas, row_blocks // replicas, degree_last - 1, sub, width
-            )
-            swapped = lax.all_to_all(swapped, "rep", split_axis=0, concat_axis=0, tiled=True)
-            swapped = swapped.transpose(2, 1, 0, 3, 4).reshape(degree_last - 1, share_rows, width)
-            own.extend(swapped[k] for k in range(degree_last - 1))
+        if degree > 1:
+            own.append(swap(terms[-1]))
         sent = lax.all_to_all(
             terms[-1][served], "rows", split_axis=0, concat_axis=0, tiled=True
         ).reshape(-1, sub, width)

time: 207 us -> 236 us (1.14)
  waiting for transfers between devices: 44.7 us -> 77.9 us
  starting transfers between devices: 76.9 us -> 69.5 us
  matrix products: 2.45 us -> 4.96 us
    ppermute x36 -> x30, waiting for transfers between devices: 32.1 us -> 55.3 us  [along(): lax.ppermute(x, 'rep', [((i + step) % replicas, i) for i in range(replica...]
    ppermute x36 -> x30, starting transfers between devices: 59.5 us -> 49.2 us  [along(): lax.ppermute(x, 'rep', [((i + step) % replicas, i) for i in range(replica...]
    all_to_all x1 -> x2, waiting for transfers between devices: 0.01 us -> 9.96 us  [swap(): lax.all_to_all(term.reshape(replicas, -1, sub, width), 'rep', split_axis=...]
    all_to_all x1 -> x2, starting transfers between devices: 3.41 us -> 7.82 us  [swap(): lax.all_to_all(term.reshape(replicas, -1, sub, width), 'rep', split_axis=...]
    dot_general x4, matrix products: 2.45 us -> 4.96 us  [on_device(): jnp.dot(own[degree], filter_weights[degree], preferred_element_type=jnp.f...]
    ppermute x24 -> x18, starting transfers between devices: 5.79 us -> 4.36 us  [partner(): return lax.ppermute(x, 'rep', [(i, i ^ 1) for i in range(replicas)])]
    ppermute x24 -> x18, waiting for transfers between devices: 5.95 us -> 6.13 us  [partner(): return lax.ppermute(x, 'rep', [(i, i ^ 1) for i in range(replicas)])]
  transfers between devices with their start and end apart: 62 -> 51, of which waited for: 23 -> 22; matrix products, arithmetic and copies ran while one was open for 3% -> 2% of each run, Pallas kernels for 7% -> 4%
where the time goes in v3:
time: 236 us; the launch traced here: 235 us
  waiting for transfers between devices  77.9 us (33%)
  starting transfers between devices  69.5 us (29%)
  blocking collectives  48.1 us (20%)
  Pallas kernels  22.1 us (9%)
  local copies, waits for them, and re-layouts  8.3 us (4%)
  matrix products  4.96 us (2%)
  other arithmetic  2.99 us (1%)
    ppermute x30, waiting for transfers between devices, along(): lax.ppermute(x, 'rep', [((i + step) % replicas, i) for i in range(replica...  55.3 us
    ppermute x30, starting transfers between devices, along(): lax.ppermute(x, 'rep', [((i + step) % replicas, i) for i in range(replica...  49.2 us
    all_to_all x3, blocking collectives, step(): lax.all_to_all(terms[-1][served], 'rows', split_axis=0, concat_axis=0, ti...  48.1 us
    pallas_call x3, Pallas kernels, tile_sums(): pl.pallas_call(body, out_shape=(pltpu.VMEM(shape, jnp.bfloat16), pltpu.VM...  11.6 us
    pallas_call x3, Pallas kernels, load_live(): pl.pallas_call(body, out_shape=(pltpu.VMEM(values.shape, values.dtype), p...  10.5 us
    all_to_all x2, waiting for transfers between devices, swap(): lax.all_to_all(term.reshape(replicas, -1, sub, width), 'rep', split_axis=...  9.96 us
    all_to_all x1, starting transfers between devices, on_device(): lax.all_to_all(wanted, 'rows', split_axis=0, concat_axis=0, tiled=True)  8.16 us
    all_to_all x2, starting transfers between devices, swap(): lax.all_to_all(term.reshape(replicas, -1, sub, width), 'rep', split_axis=...  7.82 us
  transfers between devices with their start and end apart: 51, of which 22 were waited for; matrix products, arithmetic and copies ran while one was open for 2% of the time, Pallas kernels for 4%

profile of v3, /device:TPU:0, one launch (start us, length us, event | category | flops | bytes accessed | tf_op | source)
XLA Modules:
  0.0 235.2 jit_solution(4037801670712754408)
XLA Ops:
  0.0 1.4 copy.18
  1.4 8.2 %all-to-all-start = ((s32[16,1,8]{2,1,0:T(1,128)}), s32[16,1,8]{2,1,0:T(1,128)S(1)}, u32[]{:S(2)}, u32[]{:S(2)}) async-start(s32[16,1,8]{2,1,0:T(1,128)} %copy.18), calls=%async_computation | async-start | bytes 16384 | tf_op jit(solution)/shard_map/all_to_all | solution.py:192
  10.5 6.6 %all-to-all-done = s32[16,1,8]{2,1,0:T(1,128)S(1)} async-done(((s32[16,1,8]{2,1,0:T(1,128)}), s32[16,1,8]{2,1,0:T(1,128)S(1)}, u32[]{:S(2)}, u32[]{:S(2)}) %all-to-all-start) | async-done | bytes 544 | tf_op jit(solution)/shard_map/all_to_all | solution.py:192
  18.0 13.1 %all_to_all.37 = bf16[16,8,16,128]{3,2,1,0:T(8,128)(2,1)S(1)} all-to-all(bf16[16,8,16,128]{3,2,1,0:T(8,128)(2,1)S(1)} %bitcast.192), channel_id=1, replica_groups=mesh['rows'=16,'rep'=8] {'rows'}, dimensions={0} | all-to-all | bytes 1048576 | tf_op jit(solution)/shard_map/all_to_all | solution.py:201
  31.1 1.5 collective-permute-start.1
  32.6 1.7 collective-permute-start.3
  34.3 9.1 %collective-permute-done.1 = bf16[128,16,128]{2,1,0:T(8,128)(2,1)S(1)} collective-permute-done((bf16[128,16,128]{2,1,0:T(8,128)(2,1)S(1)}, bf16[128,16,128]{2,1,0:T(8,128)(2,1)S(1)}, u32[]{:S(2)}, u32[]{:S(2)}) %collective-permute-start.1) | collective-permute-done | bytes 524320 | tf_op jit(solution)/shard_map/ppermute | solution.py:147
  44.1 3.5 %load_live.3 = (bf16[512,128,128]{2,1,0:T(8,128)(2,1)S(1)}, bf16[8,128,16,128]{3,2,1,0:T(8,128)(2,1)S(1)}) custom-call(s32[11]{0:T(128)S(1)} %stack.43.scalar, bf16[512,128,128]{2,1,0:T(8,128)(2,1)} %bitcast.189, bf16[128,16,128]{2,1,0:T(8,128)(2,1)S(1)} %bitcast.174), custom_call_target="tpu_custom_call" | custom-call | tf_op jit(solution)/shard_map/load_live/pallas_call | solution.py:97
  47.8 3.3 %collective-permute-start.7 = (bf16[64,16,128]{2,1,0:T(8,128)(2,1)S(1)}, bf16[64,16,128]{2,1,0:T(8,128)(2,1)S(1)}, u32[]{:S(2)}, u32[]{:S(2)}) collective-permute-start(bf16[64,16,128]{2,1,0:T(8,128)(2,1)S(1)} %slice.149), channel_id=1, source_target_pairs={{2,0},{3,1},{4,2},{5,3},{6,4},{7,5},{0,6},{1,7},{10,8},{11,9},{12,... | collective-permute-start | bytes 786440 | tf_op jit(solution)/shard_map/ppermute | solution.py:147
  51.5 6.5 %collective-permute-done.5 = bf16[64,16,128]{2,1,0:T(8,128)(2,1)S(1)} collective-permute-done((bf16[64,16,128]{2,1,0:T(8,128)(2,1)S(1)}, bf16[64,16,128]{2,1,0:T(8,128)(2,1)S(1)}, u32[]{:S(2)}, u32[]{:S(2)}) %collective-permute-start.5) | collective-permute-done | bytes 262176 | tf_op jit(solution)/shard_map/ppermute | solution.py:147
  60.0 3.9 %tile_sums.3 = (bf16[4,32,16,128]{3,2,1,0:T(8,128)(2,1)S(1)}, f32[4,32,16,128]{3,2,1,0:T(8,128)S(1)}) custom-call(s32[11]{0:T(128)S(1)} %stack.43.scalar, s32[512]{0:T(512)S(1)} %bitcast.183, s32[512]{0:T(512)S(1)} %bitcast.186, bf16[8,128,16,128]{3,2,1,0:T(8,128)(2,1)S(1)} %bitcast_dynamic-update-slice_fusion.23.fetched, ...), custom_call_target="tpu_custom_call" | custom-call | tf_op jit(solution)/shard_map/tile_sums/pallas_call | solution.py:57
  64.5 1.5 collective-permute-done.9
  66.4 3.2 %collective-permute-start.11 = (bf16[32,16,128]{2,1,0:T(8,128)(2,1)S(1)}, bf16[32,16,128]{2,1,0:T(8,128)(2,1)S(1)}, u32[]{:S(2)}, u32[]{:S(2)}) collective-permute-start(bf16[32,16,128]{2,1,0:T(8,128)(2,1)S(1)} %get-tuple-element.46), channel_id=1, source_target_pairs={{2,0},{3,1},{4,2},{5,3},{6,4},{7,5},{0,6},{1,7},{10,8},{11,9},{12,... | collective-permute-start | bytes 393224 | tf_op jit(solution)/shard_map/ppermute | solution.py:147
  69.6 3.2 %collective-permute-start.14 = (bf16[16,16,128]{2,1,0:T(8,128)(2,1)S(1)}, bf16[16,16,128]{2,1,0:T(8,128)(2,1)S(1)}, u32[]{:S(2)}, u32[]{:S(2)}) collective-permute-start(bf16[16,16,128]{2,1,0:T(8,128)(2,1)S(1)} %get-tuple-element.44), channel_id=1, source_target_pairs={{2,0},{3,1},{4,2},{5,3},{6,4},{7,5},{0,6},{1,7},{10,8},{11,9},{12,... | collective-permute-start | bytes 196616 | tf_op jit(solution)/shard_map/ppermute | solution.py:147
  72.9 2.2 collective-permute-done.12
  75.1 3.2 %collective-permute-start.15 = (bf16[16,16,128]{2,1,0:T(8,128)(2,1)S(1)}, bf16[16,16,128]{2,1,0:T(8,128)(2,1)S(1)}, u32[]{:S(2)}, u32[]{:S(2)}) collective-permute-start(bf16[16,16,128]{2,1,0:T(8,128)(2,1)S(1)} %collective-permute-done.14), channel_id=1, source_target_pairs={{2,0},{3,1},{4,2},{5,3},{6,4},{7,5},{0,6},{1,7},{10,8},{11,9},{12,... | collective-permute-start | bytes 196616 | tf_op jit(solution)/shard_map/ppermute | solution.py:147
  78.3 2.2 collective-permute-done.13
  81.3 1.6 gather_fusion.1
  82.9 17.4 %all_to_all.38 = bf16[16,8,16,128]{3,2,1,0:T(8,128)(2,1)S(1)} all-to-all(bf16[16,8,16,128]{3,2,1,0:T(8,128)(2,1)S(1)} %bitcast.194), channel_id=1, replica_groups=mesh['rows'=16,'rep'=8] {'rows'}, dimensions={0} | all-to-all | bytes 1048576 | tf_op jit(solution)/shard_map/all_to_all | solution.py:201
  100.3 3.2 %collective-permute-start.19 = (bf16[128,16,128]{2,1,0:T(8,128)(2,1)S(1)}, bf16[128,16,128]{2,1,0:T(8,128)(2,1)S(1)}, u32[]{:S(2)}, u32[]{:S(2)}) collective-permute-start(bf16[128,16,128]{2,1,0:T(8,128)(2,1)S(1)} %bitcast.176), channel_id=1, source_target_pairs={{2,0},{3,1},{4,2},{5,3},{6,4},{7,5},{0,6},{1,7},{10,8},{11,9},{12,... | collective-permute-start | bytes 1572872 | tf_op jit(solution)/shard_map/ppermute | solution.py:147
  103.6 8.3 %collective-permute-done.17 = bf16[128,16,128]{2,1,0:T(8,128)(2,1)S(1)} collective-permute-done((bf16[128,16,128]{2,1,0:T(8,128)(2,1)S(1)}, bf16[128,16,128]{2,1,0:T(8,128)(2,1)S(1)}, u32[]{:S(2)}, u32[]{:S(2)}) %collective-permute-start.17) | collective-permute-done | bytes 524320 | tf_op jit(solution)/shard_map/ppermute | solution.py:147
  111.9 3.5 %load_live.4 = (bf16[512,128,128]{2,1,0:T(8,128)(2,1)S(1)}, bf16[8,128,16,128]{3,2,1,0:T(8,128)(2,1)S(1)}) custom-call(s32[11]{0:T(128)S(1)} %stack.43.scalar, bf16[512,128,128]{2,1,0:T(8,128)(2,1)} %bitcast.190, bf16[128,16,128]{2,1,0:T(8,128)(2,1)S(1)} %bitcast.178), custom_call_target="tpu_custom_call" | custom-call | tf_op jit(solution)/shard_map/load_live/pallas_call | solution.py:97
  115.5 3.3 %collective-permute-start.23 = (bf16[64,16,128]{2,1,0:T(8,128)(2,1)S(1)}, bf16[64,16,128]{2,1,0:T(8,128)(2,1)S(1)}, u32[]{:S(2)}, u32[]{:S(2)}) collective-permute-start(bf16[64,16,128]{2,1,0:T(8,128)(2,1)S(1)} %slice.156), channel_id=1, source_target_pairs={{2,0},{3,1},{4,2},{5,3},{6,4},{7,5},{0,6},{1,7},{10,8},{11,9},{12,... | collective-permute-start | bytes 786440 | tf_op jit(solution)/shard_map/ppermute | solution.py:147
  119.2 6.5 %collective-permute-done.21 = bf16[64,16,128]{2,1,0:T(8,128)(2,1)S(1)} collective-permute-done((bf16[64,16,128]{2,1,0:T(8,128)(2,1)S(1)}, bf16[64,16,128]{2,1,0:T(8,128)(2,1)S(1)}, u32[]{:S(2)}, u32[]{:S(2)}) %collective-permute-start.21) | collective-permute-done | bytes 262176 | tf_op jit(solution)/shard_map/ppermute | solution.py:147
  127.6 3.9 %tile_sums.4 = (bf16[4,32,16,128]{3,2,1,0:T(8,128)(2,1)S(1)}, f32[4,32,16,128]{3,2,1,0:T(8,128)S(1)}) custom-call(s32[11]{0:T(128)S(1)} %stack.43.scalar, s32[512]{0:T(512)S(1)} %bitcast.184, s32[512]{0:T(512)S(1)} %bitcast.187, bf16[8,128,16,128]{3,2,1,0:T(8,128)(2,1)S(1)} %bitcast_dynamic-update-slice_fusion.19.fetched, ...), custom_call_target="tpu_custom_call" | custom-call | tf_op jit(solution)/shard_map/tile_sums/pallas_call | solution.py:57
  132.2 1.5 collective-permute-done.25
  134.1 3.2 %collective-permute-start.27 = (bf16[32,16,128]{2,1,0:T(8,128)(2,1)S(1)}, bf16[32,16,128]{2,1,0:T(8,128)(2,1)S(1)}, u32[]{:S(2)}, u32[]{:S(2)}) collective-permute-start(bf16[32,16,128]{2,1,0:T(8,128)(2,1)S(1)} %get-tuple-element.42), channel_id=1, source_target_pairs={{2,0},{3,1},{4,2},{5,3},{6,4},{7,5},{0,6},{1,7},{10,8},{11,9},{12,... | collective-permute-start | bytes 393224 | tf_op jit(solution)/shard_map/ppermute | solution.py:147
  137.3 3.2 %collective-permute-start.30 = (bf16[16,16,128]{2,1,0:T(8,128)(2,1)S(1)}, bf16[16,16,128]{2,1,0:T(8,128)(2,1)S(1)}, u32[]{:S(2)}, u32[]{:S(2)}) collective-permute-start(bf16[16,16,128]{2,1,0:T(8,128)(2,1)S(1)} %get-tuple-element.40), channel_id=1, source_target_pairs={{2,0},{3,1},{4,2},{5,3},{6,4},{7,5},{0,6},{1,7},{10,8},{11,9},{12,... | collective-permute-start | bytes 196616 | tf_op jit(solution)/shard_map/ppermute | solution.py:147
  140.5 2.2 collective-permute-done.28
  142.8 3.2 %collective-permute-start.31 = (bf16[16,16,128]{2,1,0:T(8,128)(2,1)S(1)}, bf16[16,16,128]{2,1,0:T(8,128)(2,1)S(1)}, u32[]{:S(2)}, u32[]{:S(2)}) collective-permute-start(bf16[16,16,128]{2,1,0:T(8,128)(2,1)S(1)} %collective-permute-done.30), channel_id=1, source_target_pairs={{2,0},{3,1},{4,2},{5,3},{6,4},{7,5},{0,6},{1,7},{10,8},{11,9},{12,... | collective-permute-start | bytes 196616 | tf_op jit(solution)/shard_map/ppermute | solution.py:147
  146.0 2.2 collective-permute-done.29
  148.3 1.7 fusion.12
  149.9 1.6 gather_fusion.2
  151.5 17.6 %all_to_all.39 = bf16[16,8,16,128]{3,2,1,0:T(8,128)(2,1)S(1)} all-to-all(bf16[16,8,16,128]{3,2,1,0:T(8,128)(2,1)S(1)} %bitcast.193), channel_id=1, replica_groups=mesh['rows'=16,'rep'=8] {'rows'}, dimensions={0} | all-to-all | bytes 1048576 | tf_op jit(solution)/shard_map/all_to_all | solution.py:201
  169.2 3.2 %collective-permute-start.35 = (bf16[128,16,128]{2,1,0:T(8,128)(2,1)S(1)}, bf16[128,16,128]{2,1,0:T(8,128)(2,1)S(1)}, u32[]{:S(2)}, u32[]{:S(2)}) collective-permute-start(bf16[128,16,128]{2,1,0:T(8,128)(2,1)S(1)} %bitcast.180), channel_id=1, source_target_pairs={{2,0},{3,1},{4,2},{5,3},{6,4},{7,5},{0,6},{1,7},{10,8},{11,9},{12,... | collective-permute-start | bytes 1572872 | tf_op jit(solution)/shard_map/ppermute | solution.py:147
  172.4 8.3 %collective-permute-done.33 = bf16[128,16,128]{2,1,0:T(8,128)(2,1)S(1)} collective-permute-done((bf16[128,16,128]{2,1,0:T(8,128)(2,1)S(1)}, bf16[128,16,128]{2,1,0:T(8,128)(2,1)S(1)}, u32[]{:S(2)}, u32[]{:S(2)}) %collective-permute-start.33) | collective-permute-done | bytes 524320 | tf_op jit(solution)/shard_map/ppermute | solution.py:147
  180.7 3.5 %load_live.5 = (bf16[512,128,128]{2,1,0:T(8,128)(2,1)S(1)}, bf16[8,128,16,128]{3,2,1,0:T(8,128)(2,1)S(1)}) custom-call(s32[11]{0:T(128)S(1)} %stack.43.scalar, bf16[512,128,128]{2,1,0:T(8,128)(2,1)} %bitcast.191, bf16[128,16,128]{2,1,0:T(8,128)(2,1)S(1)} %bitcast.182), custom_call_target="tpu_custom_call" | custom-call | tf_op jit(solution)/shard_map/load_live/pallas_call | solution.py:97
  184.4 3.3 %collective-permute-start.39 = (bf16[64,16,128]{2,1,0:T(8,128)(2,1)S(1)}, bf16[64,16,128]{2,1,0:T(8,128)(2,1)S(1)}, u32[]{:S(2)}, u32[]{:S(2)}) collective-permute-start(bf16[64,16,128]{2,1,0:T(8,128)(2,1)S(1)} %slice.163), channel_id=1, source_target_pairs={{2,0},{3,1},{4,2},{5,3},{6,4},{7,5},{0,6},{1,7},{10,8},{11,9},{12,... | collective-permute-start | bytes 786440 | tf_op jit(solution)/shard_map/ppermute | solution.py:147
  188.1 6.5 %collective-permute-done.37 = bf16[64,16,128]{2,1,0:T(8,128)(2,1)S(1)} collective-permute-done((bf16[64,16,128]{2,1,0:T(8,128)(2,1)S(1)}, bf16[64,16,128]{2,1,0:T(8,128)(2,1)S(1)}, u32[]{:S(2)}, u32[]{:S(2)}) %collective-permute-start.37) | collective-permute-done | bytes 262176 | tf_op jit(solution)/shard_map/ppermute | solution.py:147
  196.5 3.9 %tile_sums.5 = (bf16[4,32,16,128]{3,2,1,0:T(8,128)(2,1)S(1)}, f32[4,32,16,128]{3,2,1,0:T(8,128)S(1)}) custom-call(s32[11]{0:T(128)S(1)} %stack.43.scalar, s32[512]{0:T(512)S(1)} %bitcast.185, s32[512]{0:T(512)S(1)} %bitcast.188, bf16[8,128,16,128]{3,2,1,0:T(8,128)(2,1)S(1)} %bitcast_dynamic-update-slice_fusion.15.fetched, ...), custom_call_target="tpu_custom_call" | custom-call | tf_op jit(solution)/shard_map/tile_sums/pallas_call | solution.py:57
  201.1 4.4 %all-to-all-start.2 = ((bf16[8,4,16,128]{3,2,1,0:T(8,128)(2,1)}), bf16[8,4,16,128]{3,2,1,0:T(8,128)(2,1)S(1)}, u32[]{:S(2)}, u32[]{:S(2)}) async-start(bf16[8,4,16,128]{3,2,1,0:T(8,128)(2,1)} %bitcast.34), calls=%async_computation.2 | async-start | bytes 262144 | tf_op jit(solution)/shard_map/all_to_all | solution.py:175
  206.6 5.0 %all-to-all-done.2 = bf16[8,4,16,128]{3,2,1,0:T(8,128)(2,1)S(1)} async-done(((bf16[8,4,16,128]{3,2,1,0:T(8,128)(2,1)}), bf16[8,4,16,128]{3,2,1,0:T(8,128)(2,1)S(1)}, u32[]{:S(2)}, u32[]{:S(2)}) %all-to-all-start.2) | async-done | bytes 131104 | tf_op jit(solution)/shard_map/all_to_all | solution.py:175
  211.6 3.4 %all-to-all-start.4 = ((bf16[8,4,16,128]{3,2,1,0:T(8,128)(2,1)}), bf16[8,4,16,128]{3,2,1,0:T(8,128)(2,1)S(1)}, u32[]{:S(2)}, u32[]{:S(2)}) async-start(bf16[8,4,16,128]{3,2,1,0:T(8,128)(2,1)} %bitcast.54), calls=%async_computation.4 | async-start | bytes 262144 | tf_op jit(solution)/shard_map/all_to_all | solution.py:175
  216.1 5.0 %all-to-all-done.4 = bf16[8,4,16,128]{3,2,1,0:T(8,128)(2,1)S(1)} async-done(((bf16[8,4,16,128]{3,2,1,0:T(8,128)(2,1)}), bf16[8,4,16,128]{3,2,1,0:T(8,128)(2,1)S(1)}, u32[]{:S(2)}, u32[]{:S(2)}) %all-to-all-start.4) | async-done | bytes 131104 | tf_op jit(solution)/shard_map/all_to_all | solution.py:175
  221.9 2.7 %collective-permute-start.46 = (bf16[16,16,128]{2,1,0:T(8,128)(2,1)S(1)}, bf16[16,16,128]{2,1,0:T(8,128)(2,1)S(1)}, u32[]{:S(2)}, u32[]{:S(2)}) collective-permute-start(bf16[16,16,128]{2,1,0:T(8,128)(2,1)S(1)} %get-tuple-element.36), channel_id=1, source_target_pairs={{2,0},{3,1},{4,2},{5,3},{6,4},{7,5},{0,6},{1,7},{10,8},{11,9},{12,... | collective-permute-start | bytes 196616 | tf_op jit(solution)/shard_map/ppermute | solution.py:147
  224.7 3.2 %collective-permute-start.43 = (bf16[32,16,128]{2,1,0:T(8,128)(2,1)S(1)}, bf16[32,16,128]{2,1,0:T(8,128)(2,1)S(1)}, u32[]{:S(2)}, u32[]{:S(2)}) collective-permute-start(bf16[32,16,128]{2,1,0:T(8,128)(2,1)S(1)} %get-tuple-element.38), channel_id=1, source_target_pairs={{2,0},{3,1},{4,2},{5,3},{6,4},{7,5},{0,6},{1,7},{10,8},{11,9},{12,... | collective-permute-start | bytes 393224 | tf_op jit(solution)/shard_map/ppermute | solution.py:147
  227.9 3.2 %collective-permute-start.47 = (bf16[16,16,128]{2,1,0:T(8,128)(2,1)S(1)}, bf16[16,16,128]{2,1,0:T(8,128)(2,1)S(1)}, u32[]{:S(2)}, u32[]{:S(2)}) collective-permute-start(bf16[16,16,128]{2,1,0:T(8,128)(2,1)S(1)} %collective-permute-done.46), channel_id=1, source_target_pairs={{2,0},{3,1},{4,2},{5,3},{6,4},{7,5},{0,6},{1,7},{10,8},{11,9},{12,... | collective-permute-start | bytes 196616 | tf_op jit(solution)/shard_map/ppermute | solution.py:147
  233.5 1.8 fusion
  (129 shorter events, 18.1 us)
Async XLA Ops:
  1.4 15.7 %all-to-all-start = ((s32[16,1,8]{2,1,0:T(1,128)}), s32[16,1,8]{2,1,0:T(1,128)S(1)}, u32[]{:S(2)}, u32[]{:S(2)}) async-start(s32[16,1,8]{2,1,0:T(1,128)} %copy.18), calls=%async_computation | async-start | bytes 16384 | tf_op jit(solution)/shard_map/all_to_all | solution.py:192
  31.1 12.3 %collective-permute-start.1 = (bf16[128,16,128]{2,1,0:T(8,128)(2,1)S(1)}, bf16[128,16,128]{2,1,0:T(8,128)(2,1)S(1)}, u32[]{:S(2)}, u32[]{:S(2)}) collective-permute-start(bf16[128,16,128]{2,1,0:T(8,128)(2,1)S(1)} %bitcast.171), channel_id=1, source_target_pairs={{6,0},{7,1},{0,2},{1,3},{2,4},{3,5},{4,6},{5,7},{14,8},{15,9},{8,1... | collective-permute-start | bytes 1572872 | tf_op jit(solution)/shard_map/ppermute | solution.py:147
  32.6 15.2 %collective-permute-start.3 = (bf16[128,16,128]{2,1,0:T(8,128)(2,1)S(1)}, bf16[128,16,128]{2,1,0:T(8,128)(2,1)S(1)}, u32[]{:S(2)}, u32[]{:S(2)}) collective-permute-start(bf16[128,16,128]{2,1,0:T(8,128)(2,1)S(1)} %bitcast.172), channel_id=1, source_target_pairs={{2,0},{3,1},{4,2},{5,3},{6,4},{7,5},{0,6},{1,7},{10,8},{11,9},{12,... | collective-permute-start | bytes 1572872 | tf_op jit(solution)/shard_map/ppermute | solution.py:147
  34.3 17.0 %collective-permute-start = (bf16[128,16,128]{2,1,0:T(8,128)(2,1)S(1)}, bf16[128,16,128]{2,1,0:T(8,128)(2,1)S(1)}, u32[]{:S(2)}, u32[]{:S(2)}) collective-permute-start(bf16[128,16,128]{2,1,0:T(8,128)(2,1)S(1)} %bitcast.173), channel_id=1, source_target_pairs={{0,1},{1,0},{2,3},{3,2},{4,5},{5,4},{6,7},{7,6},{8,9},{9,8},{10,11... | collective-permute-start | bytes 1572872 | tf_op jit(solution)/shard_map/ppermute | solution.py:150
  43.4 15.1 %collective-permute-start.2 = (bf16[128,16,128]{2,1,0:T(8,128)(2,1)S(1)}, bf16[128,16,128]{2,1,0:T(8,128)(2,1)S(1)}, u32[]{:S(2)}, u32[]{:S(2)}) collective-permute-start(bf16[128,16,128]{2,1,0:T(8,128)(2,1)S(1)} %collective-permute-done.1), channel_id=1, source_target_pairs={{0,1},{1,0},{2,3},{3,2},{4,5},{5,4},{6,7},{7,6},{8,9},{9,8},{10,11... | collective-permute-start | bytes 1572872 | tf_op jit(solution)/shard_map/ppermute | solution.py:150
  47.7 10.3 %collective-permute-start.5 = (bf16[64,16,128]{2,1,0:T(8,128)(2,1)S(1)}, bf16[64,16,128]{2,1,0:T(8,128)(2,1)S(1)}, u32[]{:S(2)}, u32[]{:S(2)}) collective-permute-start(bf16[64,16,128]{2,1,0:T(8,128)(2,1)S(1)} %slice.148), channel_id=1, source_target_pairs={{6,0},{7,1},{0,2},{1,3},{2,4},{3,5},{4,6},{5,7},{14,8},{15,9},{8,1... | collective-permute-start | bytes 786440 | tf_op jit(solution)/shard_map/ppermute | solution.py:147
  47.8 10.2 %collective-permute-start.7 = (bf16[64,16,128]{2,1,0:T(8,128)(2,1)S(1)}, bf16[64,16,128]{2,1,0:T(8,128)(2,1)S(1)}, u32[]{:S(2)}, u32[]{:S(2)}) collective-permute-start(bf16[64,16,128]{2,1,0:T(8,128)(2,1)S(1)} %slice.149), channel_id=1, source_target_pairs={{2,0},{3,1},{4,2},{5,3},{6,4},{7,5},{0,6},{1,7},{10,8},{11,9},{12,... | collective-permute-start | bytes 786440 | tf_op jit(solution)/shard_map/ppermute | solution.py:147
  51.1 7.6 %collective-permute-start.4 = (bf16[128,16,128]{2,1,0:T(8,128)(2,1)S(1)}, bf16[128,16,128]{2,1,0:T(8,128)(2,1)S(1)}, u32[]{:S(2)}, u32[]{:S(2)}) collective-permute-start(bf16[128,16,128]{2,1,0:T(8,128)(2,1)S(1)} %collective-permute-done.3), channel_id=1, source_target_pairs={{0,1},{1,0},{2,3},{3,2},{4,5},{5,4},{6,7},{7,6},{8,9},{9,8},{10,11... | collective-permute-start | bytes 1572872 | tf_op jit(solution)/shard_map/ppermute | solution.py:150
  58.0 1.9 collective-permute-start.8
  63.9 2.2 collective-permute-start.9
  66.3 12.0 %collective-permute-start.10 = (bf16[32,16,128]{2,1,0:T(8,128)(2,1)S(1)}, bf16[32,16,128]{2,1,0:T(8,128)(2,1)S(1)}, u32[]{:S(2)}, u32[]{:S(2)}) collective-permute-start(bf16[32,16,128]{2,1,0:T(8,128)(2,1)S(1)} %get-tuple-element.45), channel_id=1, source_target_pairs={{6,0},{7,1},{0,2},{1,3},{2,4},{3,5},{4,6},{5,7},{14,8},{15,9},{8,1... | collective-permute-start | bytes 393224 | tf_op jit(solution)/shard_map/ppermute | solution.py:147
  66.4 12.0 %collective-permute-start.11 = (bf16[32,16,128]{2,1,0:T(8,128)(2,1)S(1)}, bf16[32,16,128]{2,1,0:T(8,128)(2,1)S(1)}, u32[]{:S(2)}, u32[]{:S(2)}) collective-permute-start(bf16[32,16,128]{2,1,0:T(8,128)(2,1)S(1)} %get-tuple-element.46), channel_id=1, source_target_pairs={{2,0},{3,1},{4,2},{5,3},{6,4},{7,5},{0,6},{1,7},{10,8},{11,9},{12,... | collective-permute-start | bytes 393224 | tf_op jit(solution)/shard_map/ppermute | solution.py:147
  69.6 5.5 %collective-permute-start.12 = (bf16[16,16,128]{2,1,0:T(8,128)(2,1)S(1)}, bf16[16,16,128]{2,1,0:T(8,128)(2,1)S(1)}, u32[]{:S(2)}, u32[]{:S(2)}) collective-permute-start(bf16[16,16,128]{2,1,0:T(8,128)(2,1)S(1)} %get-tuple-element.43), channel_id=1, source_target_pairs={{6,0},{7,1},{0,2},{1,3},{2,4},{3,5},{4,6},{5,7},{14,8},{15,9},{8,1... | collective-permute-start | bytes 196616 | tf_op jit(solution)/shard_map/ppermute | solution.py:147
  69.6 5.5 %collective-permute-start.14 = (bf16[16,16,128]{2,1,0:T(8,128)(2,1)S(1)}, bf16[16,16,128]{2,1,0:T(8,128)(2,1)S(1)}, u32[]{:S(2)}, u32[]{:S(2)}) collective-permute-start(bf16[16,16,128]{2,1,0:T(8,128)(2,1)S(1)} %get-tuple-element.44), channel_id=1, source_target_pairs={{2,0},{3,1},{4,2},{5,3},{6,4},{7,5},{0,6},{1,7},{10,8},{11,9},{12,... | collective-permute-start | bytes 196616 | tf_op jit(solution)/shard_map/ppermute | solution.py:147
  75.1 5.5 %collective-permute-start.13 = (bf16[16,16,128]{2,1,0:T(8,128)(2,1)S(1)}, bf16[16,16,128]{2,1,0:T(8,128)(2,1)S(1)}, u32[]{:S(2)}, u32[]{:S(2)}) collective-permute-start(bf16[16,16,128]{2,1,0:T(8,128)(2,1)S(1)} %collective-permute-done.12), channel_id=1, source_target_pairs={{6,0},{7,1},{0,2},{1,3},{2,4},{3,5},{4,6},{5,7},{14,8},{15,9},{8,1... | collective-permute-start | bytes 196616 | tf_op jit(solution)/shard_map/ppermute | solution.py:147
  75.1 5.5 %collective-permute-start.15 = (bf16[16,16,128]{2,1,0:T(8,128)(2,1)S(1)}, bf16[16,16,128]{2,1,0:T(8,128)(2,1)S(1)}, u32[]{:S(2)}, u32[]{:S(2)}) collective-permute-start(bf16[16,16,128]{2,1,0:T(8,128)(2,1)S(1)} %collective-permute-done.14), channel_id=1, source_target_pairs={{2,0},{3,1},{4,2},{5,3},{6,4},{7,5},{0,6},{1,7},{10,8},{11,9},{12,... | collective-permute-start | bytes 196616 | tf_op jit(solution)/shard_map/ppermute | solution.py:147
  100.3 11.5 %collective-permute-start.17 = (bf16[128,16,128]{2,1,0:T(8,128)(2,1)S(1)}, bf16[128,16,128]{2,1,0:T(8,128)(2,1)S(1)}, u32[]{:S(2)}, u32[]{:S(2)}) collective-permute-start(bf16[128,16,128]{2,1,0:T(8,128)(2,1)S(1)} %bitcast.175), channel_id=1, source_target_pairs={{6,0},{7,1},{0,2},{1,3},{2,4},{3,5},{4,6},{5,7},{14,8},{15,9},{8,1... | collective-permute-start | bytes 1572872 | tf_op jit(solution)/shard_map/ppermute | solution.py:147
  100.3 15.1 %collective-permute-start.19 = (bf16[128,16,128]{2,1,0:T(8,128)(2,1)S(1)}, bf16[128,16,128]{2,1,0:T(8,128)(2,1)S(1)}, u32[]{:S(2)}, u32[]{:S(2)}) collective-permute-start(bf16[128,16,128]{2,1,0:T(8,128)(2,1)S(1)} %bitcast.176), channel_id=1, source_target_pairs={{2,0},{3,1},{4,2},{5,3},{6,4},{7,5},{0,6},{1,7},{10,8},{11,9},{12,... | collective-permute-start | bytes 1572872 | tf_op jit(solution)/shard_map/ppermute | solution.py:147
  103.5 15.5 %collective-permute-start.16 = (bf16[128,16,128]{2,1,0:T(8,128)(2,1)S(1)}, bf16[128,16,128]{2,1,0:T(8,128)(2,1)S(1)}, u32[]{:S(2)}, u32[]{:S(2)}) collective-permute-start(bf16[128,16,128]{2,1,0:T(8,128)(2,1)S(1)} %bitcast.177), channel_id=1, source_target_pairs={{0,1},{1,0},{2,3},{3,2},{4,5},{5,4},{6,7},{7,6},{8,9},{9,8},{10,11... | collective-permute-start | bytes 1572872 | tf_op jit(solution)/shard_map/ppermute | solution.py:150
  111.8 14.4 %collective-permute-start.18 = (bf16[128,16,128]{2,1,0:T(8,128)(2,1)S(1)}, bf16[128,16,128]{2,1,0:T(8,128)(2,1)S(1)}, u32[]{:S(2)}, u32[]{:S(2)}) collective-permute-start(bf16[128,16,128]{2,1,0:T(8,128)(2,1)S(1)} %collective-permute-done.17), channel_id=1, source_target_pairs={{0,1},{1,0},{2,3},{3,2},{4,5},{5,4},{6,7},{7,6},{8,9},{9,8},{10,11... | collective-permute-start | bytes 1572872 | tf_op jit(solution)/shard_map/ppermute | solution.py:150
  115.4 10.3 %collective-permute-start.21 = (bf16[64,16,128]{2,1,0:T(8,128)(2,1)S(1)}, bf16[64,16,128]{2,1,0:T(8,128)(2,1)S(1)}, u32[]{:S(2)}, u32[]{:S(2)}) collective-permute-start(bf16[64,16,128]{2,1,0:T(8,128)(2,1)S(1)} %slice.155), channel_id=1, source_target_pairs={{6,0},{7,1},{0,2},{1,3},{2,4},{3,5},{4,6},{5,7},{14,8},{15,9},{8,1... | collective-permute-start | bytes 786440 | tf_op jit(solution)/shard_map/ppermute | solution.py:147
  115.5 10.2 %collective-permute-start.23 = (bf16[64,16,128]{2,1,0:T(8,128)(2,1)S(1)}, bf16[64,16,128]{2,1,0:T(8,128)(2,1)S(1)}, u32[]{:S(2)}, u32[]{:S(2)}) collective-permute-start(bf16[64,16,128]{2,1,0:T(8,128)(2,1)S(1)} %slice.156), channel_id=1, source_target_pairs={{2,0},{3,1},{4,2},{5,3},{6,4},{7,5},{0,6},{1,7},{10,8},{11,9},{12,... | collective-permute-start | bytes 786440 | tf_op jit(solution)/shard_map/ppermute | solution.py:147
  118.8 7.6 %collective-permute-start.20 = (bf16[128,16,128]{2,1,0:T(8,128)(2,1)S(1)}, bf16[128,16,128]{2,1,0:T(8,128)(2,1)S(1)}, u32[]{:S(2)}, u32[]{:S(2)}) collective-permute-start(bf16[128,16,128]{2,1,0:T(8,128)(2,1)S(1)} %collective-permute-done.19), channel_id=1, source_target_pairs={{0,1},{1,0},{2,3},{3,2},{4,5},{5,4},{6,7},{7,6},{8,9},{9,8},{10,11... | collective-permute-start | bytes 1572872 | tf_op jit(solution)/shard_map/ppermute | solution.py:150
  125.7 1.9 collective-permute-start.24
  131.5 2.2 collective-permute-start.25
  134.0 12.0 %collective-permute-start.26 = (bf16[32,16,128]{2,1,0:T(8,128)(2,1)S(1)}, bf16[32,16,128]{2,1,0:T(8,128)(2,1)S(1)}, u32[]{:S(2)}, u32[]{:S(2)}) collective-permute-start(bf16[32,16,128]{2,1,0:T(8,128)(2,1)S(1)} %get-tuple-element.41), channel_id=1, source_target_pairs={{6,0},{7,1},{0,2},{1,3},{2,4},{3,5},{4,6},{5,7},{14,8},{15,9},{8,1... | collective-permute-start | bytes 393224 | tf_op jit(solution)/shard_map/ppermute | solution.py:147
  134.1 12.0 %collective-permute-start.27 = (bf16[32,16,128]{2,1,0:T(8,128)(2,1)S(1)}, bf16[32,16,128]{2,1,0:T(8,128)(2,1)S(1)}, u32[]{:S(2)}, u32[]{:S(2)}) collective-permute-start(bf16[32,16,128]{2,1,0:T(8,128)(2,1)S(1)} %get-tuple-element.42), channel_id=1, source_target_pairs={{2,0},{3,1},{4,2},{5,3},{6,4},{7,5},{0,6},{1,7},{10,8},{11,9},{12,... | collective-permute-start | bytes 393224 | tf_op jit(solution)/shard_map/ppermute | solution.py:147
  137.3 5.5 %collective-permute-start.28 = (bf16[16,16,128]{2,1,0:T(8,128)(2,1)S(1)}, bf16[16,16,128]{2,1,0:T(8,128)(2,1)S(1)}, u32[]{:S(2)}, u32[]{:S(2)}) collective-permute-start(bf16[16,16,128]{2,1,0:T(8,128)(2,1)S(1)} %get-tuple-element.39), channel_id=1, source_target_pairs={{6,0},{7,1},{0,2},{1,3},{2,4},{3,5},{4,6},{5,7},{14,8},{15,9},{8,1... | collective-permute-start | bytes 196616 | tf_op jit(solution)/shard_map/ppermute | solution.py:147
  137.3 5.5 %collective-permute-start.30 = (bf16[16,16,128]{2,1,0:T(8,128)(2,1)S(1)}, bf16[16,16,128]{2,1,0:T(8,128)(2,1)S(1)}, u32[]{:S(2)}, u32[]{:S(2)}) collective-permute-start(bf16[16,16,128]{2,1,0:T(8,128)(2,1)S(1)} %get-tuple-element.40), channel_id=1, source_target_pairs={{2,0},{3,1},{4,2},{5,3},{6,4},{7,5},{0,6},{1,7},{10,8},{11,9},{12,... | collective-permute-start | bytes 196616 | tf_op jit(solution)/shard_map/ppermute | solution.py:147
  142.8 5.5 %collective-permute-start.29 = (bf16[16,16,128]{2,1,0:T(8,128)(2,1)S(1)}, bf16[16,16,128]{2,1,0:T(8,128)(2,1)S(1)}, u32[]{:S(2)}, u32[]{:S(2)}) collective-permute-start(bf16[16,16,128]{2,1,0:T(8,128)(2,1)S(1)} %collective-permute-done.28), channel_id=1, source_target_pairs={{6,0},{7,1},{0,2},{1,3},{2,4},{3,5},{4,6},{5,7},{14,8},{15,9},{8,1... | collective-permute-start | bytes 196616 | tf_op jit(solution)/shard_map/ppermute | solution.py:147
  142.8 5.5 %collective-permute-start.31 = (bf16[16,16,128]{2,1,0:T(8,128)(2,1)S(1)}, bf16[16,16,128]{2,1,0:T(8,128)(2,1)S(1)}, u32[]{:S(2)}, u32[]{:S(2)}) collective-permute-start(bf16[16,16,128]{2,1,0:T(8,128)(2,1)S(1)} %collective-permute-done.30), channel_id=1, source_target_pairs={{2,0},{3,1},{4,2},{5,3},{6,4},{7,5},{0,6},{1,7},{10,8},{11,9},{12,... | collective-permute-start | bytes 196616 | tf_op jit(solution)/shard_map/ppermute | solution.py:147
  169.2 11.5 %collective-permute-start.33 = (bf16[128,16,128]{2,1,0:T(8,128)(2,1)S(1)}, bf16[128,16,128]{2,1,0:T(8,128)(2,1)S(1)}, u32[]{:S(2)}, u32[]{:S(2)}) collective-permute-start(bf16[128,16,128]{2,1,0:T(8,128)(2,1)S(1)} %bitcast.179), channel_id=1, source_target_pairs={{6,0},{7,1},{0,2},{1,3},{2,4},{3,5},{4,6},{5,7},{14,8},{15,9},{8,1... | collective-permute-start | bytes 1572872 | tf_op jit(solution)/shard_map/ppermute | solution.py:147
  169.2 15.1 %collective-permute-start.35 = (bf16[128,16,128]{2,1,0:T(8,128)(2,1)S(1)}, bf16[128,16,128]{2,1,0:T(8,128)(2,1)S(1)}, u32[]{:S(2)}, u32[]{:S(2)}) collective-permute-start(bf16[128,16,128]{2,1,0:T(8,128)(2,1)S(1)} %bitcast.180), channel_id=1, source_target_pairs={{2,0},{3,1},{4,2},{5,3},{6,4},{7,5},{0,6},{1,7},{10,8},{11,9},{12,... | collective-permute-start | bytes 1572872 | tf_op jit(solution)/shard_map/ppermute | solution.py:147
  172.4 15.5 %collective-permute-start.32 = (bf16[128,16,128]{2,1,0:T(8,128)(2,1)S(1)}, bf16[128,16,128]{2,1,0:T(8,128)(2,1)S(1)}, u32[]{:S(2)}, u32[]{:S(2)}) collective-permute-start(bf16[128,16,128]{2,1,0:T(8,128)(2,1)S(1)} %bitcast.181), channel_id=1, source_target_pairs={{0,1},{1,0},{2,3},{3,2},{4,5},{5,4},{6,7},{7,6},{8,9},{9,8},{10,11... | collective-permute-start | bytes 1572872 | tf_op jit(solution)/shard_map/ppermute | solution.py:150
  180.7 14.4 %collective-permute-start.34 = (bf16[128,16,128]{2,1,0:T(8,128)(2,1)S(1)}, bf16[128,16,128]{2,1,0:T(8,128)(2,1)S(1)}, u32[]{:S(2)}, u32[]{:S(2)}) collective-permute-start(bf16[128,16,128]{2,1,0:T(8,128)(2,1)S(1)} %collective-permute-done.33), channel_id=1, source_target_pairs={{0,1},{1,0},{2,3},{3,2},{4,5},{5,4},{6,7},{7,6},{8,9},{9,8},{10,11... | collective-permute-start | bytes 1572872 | tf_op jit(solution)/shard_map/ppermute | solution.py:150
  184.3 10.3 %collective-permute-start.37 = (bf16[64,16,128]{2,1,0:T(8,128)(2,1)S(1)}, bf16[64,16,128]{2,1,0:T(8,128)(2,1)S(1)}, u32[]{:S(2)}, u32[]{:S(2)}) collective-permute-start(bf16[64,16,128]{2,1,0:T(8,128)(2,1)S(1)} %slice.162), channel_id=1, source_target_pairs={{6,0},{7,1},{0,2},{1,3},{2,4},{3,5},{4,6},{5,7},{14,8},{15,9},{8,1... | collective-permute-start | bytes 786440 | tf_op jit(solution)/shard_map/ppermute | solution.py:147
  184.4 10.2 %collective-permute-start.39 = (bf16[64,16,128]{2,1,0:T(8,128)(2,1)S(1)}, bf16[64,16,128]{2,1,0:T(8,128)(2,1)S(1)}, u32[]{:S(2)}, u32[]{:S(2)}) collective-permute-start(bf16[64,16,128]{2,1,0:T(8,128)(2,1)S(1)} %slice.163), channel_id=1, source_target_pairs={{2,0},{3,1},{4,2},{5,3},{6,4},{7,5},{0,6},{1,7},{10,8},{11,9},{12,... | collective-permute-start | bytes 786440 | tf_op jit(solution)/shard_map/ppermute | solution.py:147
  187.7 7.6 %collective-permute-start.36 = (bf16[128,16,128]{2,1,0:T(8,128)(2,1)S(1)}, bf16[128,16,128]{2,1,0:T(8,128)(2,1)S(1)}, u32[]{:S(2)}, u32[]{:S(2)}) collective-permute-start(bf16[128,16,128]{2,1,0:T(8,128)(2,1)S(1)} %collective-permute-done.35), channel_id=1, source_target_pairs={{0,1},{1,0},{2,3},{3,2},{4,5},{5,4},{6,7},{7,6},{8,9},{9,8},{10,11... | collective-permute-start | bytes 1572872 | tf_op jit(solution)/shard_map/ppermute | solution.py:150
  194.6 1.9 collective-permute-start.40
  200.4 20.7 %collective-permute-start.41 = (bf16[4,32,16,128]{3,2,1,0:T(8,128)(2,1)S(1)}, bf16[4,32,16,128]{3,2,1,0:T(8,128)(2,1)S(1)}, u32[]{:S(2)}, u32[]{:S(2)}) collective-permute-start(bf16[4,32,16,128]{3,2,1,0:T(8,128)(2,1)S(1)} %get-tuple-element.28), channel_id=1, source_target_pairs={{0,1},{1,0},{2,3},{3,2},{4,5},{5,4},{6,7},{7,6},{8,9},{9,8},{10,11... | collective-permute-start | bytes 1572872 | tf_op jit(solution)/shard_map/ppermute | solution.py:150
  201.1 10.5 %all-to-all-start.2 = ((bf16[8,4,16,128]{3,2,1,0:T(8,128)(2,1)}), bf16[8,4,16,128]{3,2,1,0:T(8,128)(2,1)S(1)}, u32[]{:S(2)}, u32[]{:S(2)}) async-start(bf16[8,4,16,128]{3,2,1,0:T(8,128)(2,1)} %bitcast.34), calls=%async_computation.2 | async-start | bytes 262144 | tf_op jit(solution)/shard_map/all_to_all | solution.py:175
  211.6 9.4 %all-to-all-start.4 = ((bf16[8,4,16,128]{3,2,1,0:T(8,128)(2,1)}), bf16[8,4,16,128]{3,2,1,0:T(8,128)(2,1)S(1)}, u32[]{:S(2)}, u32[]{:S(2)}) async-start(bf16[8,4,16,128]{3,2,1,0:T(8,128)(2,1)} %bitcast.54), calls=%async_computation.4 | async-start | bytes 262144 | tf_op jit(solution)/shard_map/all_to_all | solution.py:175
  221.2 6.6 %collective-permute-start.44 = (bf16[16,16,128]{2,1,0:T(8,128)(2,1)S(1)}, bf16[16,16,128]{2,1,0:T(8,128)(2,1)S(1)}, u32[]{:S(2)}, u32[]{:S(2)}) collective-permute-start(bf16[16,16,128]{2,1,0:T(8,128)(2,1)S(1)} %get-tuple-element.35), channel_id=1, source_target_pairs={{6,0},{7,1},{0,2},{1,3},{2,4},{3,5},{4,6},{5,7},{14,8},{15,9},{8,1... | collective-permute-start | bytes 196616 | tf_op jit(solution)/shard_map/ppermute | solution.py:147
  221.9 6.0 %collective-permute-start.46 = (bf16[16,16,128]{2,1,0:T(8,128)(2,1)S(1)}, bf16[16,16,128]{2,1,0:T(8,128)(2,1)S(1)}, u32[]{:S(2)}, u32[]{:S(2)}) collective-permute-start(bf16[16,16,128]{2,1,0:T(8,128)(2,1)S(1)} %get-tuple-element.36), channel_id=1, source_target_pairs={{2,0},{3,1},{4,2},{5,3},{6,4},{7,5},{0,6},{1,7},{10,8},{11,9},{12,... | collective-permute-start | bytes 196616 | tf_op jit(solution)/shard_map/ppermute | solution.py:147
  224.6 7.6 %collective-permute-start.42 = (bf16[32,16,128]{2,1,0:T(8,128)(2,1)S(1)}, bf16[32,16,128]{2,1,0:T(8,128)(2,1)S(1)}, u32[]{:S(2)}, u32[]{:S(2)}) collective-permute-start(bf16[32,16,128]{2,1,0:T(8,128)(2,1)S(1)} %get-tuple-element.37), channel_id=1, source_target_pairs={{6,0},{7,1},{0,2},{1,3},{2,4},{3,5},{4,6},{5,7},{14,8},{15,9},{8,1... | collective-permute-start | bytes 393224 | tf_op jit(solution)/shard_map/ppermute | solution.py:147
  224.7 7.5 %collective-permute-start.43 = (bf16[32,16,128]{2,1,0:T(8,128)(2,1)S(1)}, bf16[32,16,128]{2,1,0:T(8,128)(2,1)S(1)}, u32[]{:S(2)}, u32[]{:S(2)}) collective-permute-start(bf16[32,16,128]{2,1,0:T(8,128)(2,1)S(1)} %get-tuple-element.38), channel_id=1, source_target_pairs={{2,0},{3,1},{4,2},{5,3},{6,4},{7,5},{0,6},{1,7},{10,8},{11,9},{12,... | collective-permute-start | bytes 393224 | tf_op jit(solution)/shard_map/ppermute | solution.py:147
  227.9 5.5 %collective-permute-start.45 = (bf16[16,16,128]{2,1,0:T(8,128)(2,1)S(1)}, bf16[16,16,128]{2,1,0:T(8,128)(2,1)S(1)}, u32[]{:S(2)}, u32[]{:S(2)}) collective-permute-start(bf16[16,16,128]{2,1,0:T(8,128)(2,1)S(1)} %collective-permute-done.44), channel_id=1, source_target_pairs={{6,0},{7,1},{0,2},{1,3},{2,4},{3,5},{4,6},{5,7},{14,8},{15,9},{8,1... | collective-permute-start | bytes 196616 | tf_op jit(solution)/shard_map/ppermute | solution.py:147
  227.9 5.5 %collective-permute-start.47 = (bf16[16,16,128]{2,1,0:T(8,128)(2,1)S(1)}, bf16[16,16,128]{2,1,0:T(8,128)(2,1)S(1)}, u32[]{:S(2)}, u32[]{:S(2)}) collective-permute-start(bf16[16,16,128]{2,1,0:T(8,128)(2,1)S(1)} %collective-permute-done.46), channel_id=1, source_target_pairs={{2,0},{3,1},{4,2},{5,3},{6,4},{7,5},{0,6},{1,7},{10,8},{11,9},{12,... | collective-permute-start | bytes 196616 | tf_op jit(solution)/shard_map/ppermute | solution.py:147
  (5 other events, 29.2 us)

commit v4 on v3

--- a/solution.py
+++ b/solution.py
@@ -171,11 +171,11 @@
             fetched = put(fetched, across, hops, 1, start)
         return fetched, live
 
-    def swap(term):
-        parts = lax.all_to_all(
-            term.reshape(replicas, -1, sub, width), "rep", split_axis=0, concat_axis=0, tiled=True
-        )
-        return parts.transpose(1, 0, 2, 3).reshape(share_rows, width)
+    def swap(held):
+        parts = jnp.stack(held, 1).reshape(replicas, -1, len(held), sub, width)
+        parts = lax.all_to_all(parts, "rep", split_axis=0, concat_axis=0, tiled=True)
+        parts = parts.transpose(2, 1, 0, 3, 4).reshape(len(held), share_rows, width)
+        return [parts[k] for k in range(len(held))]
 
     def reduce(peer, mine):
         sums = mine + partner(peer).astype(jnp.float32)
@@ -196,8 +196,8 @@
 
     def step(degree):
         last = degree == degree_last
-        if degree > 1:
-            own.append(swap(terms[-1]))
+        if last:
+            own.extend(swap(terms[1:]))
         sent = lax.all_to_all(
             terms[-1][served], "rows", split_axis=0, concat_axis=0, tiled=True
         ).reshape(-1, sub, width)

time: 236 us -> 218 us (0.924)
  waiting for transfers between devices: 77.9 us -> 69 us
  starting transfers between devices: 69.5 us -> 65.4 us
  matrix products: 4.96 us -> 2.44 us
    all_to_all x2 -> x1, waiting for transfers between devices: 9.96 us -> 0.01 us  [swap(): lax.all_to_all(parts, 'rep', split_axis=0, concat_axis=0, tiled=True)]
    all_to_all x2 -> x1, starting transfers between devices: 7.82 us -> 3.41 us  [swap(): lax.all_to_all(parts, 'rep', split_axis=0, concat_axis=0, tiled=True)]
    dot_general x4, matrix products: 4.96 us -> 2.44 us  [on_device(): jnp.dot(own[degree], filter_weights[degree], preferred_element_type=jnp.f...]
  transfers between devices with their start and end apart: 51 -> 50, of which waited for: 22 -> 22; matrix products, arithmetic and copies ran while one was open for 2% -> 2% of each run, Pallas kernels for 4% -> 7%
where the time goes in v4:
time: 218 us; the launch traced here: 217 us
  waiting for transfers between devices  69 us (32%)
  starting transfers between devices  65.4 us (30%)
  blocking collectives  48.2 us (22%)
  Pallas kernels  22.2 us (10%)
  local copies, waits for them, and re-layouts  6.52 us (3%)
  matrix products  2.44 us (1%)
  other arithmetic  2.38 us (1%)
    ppermute x30, waiting for transfers between devices, along(): lax.ppermute(x, 'rep', [((i + step) % replicas, i) for i in range(replica...  56.1 us
    ppermute x30, starting transfers between devices, along(): lax.ppermute(x, 'rep', [((i + step) % replicas, i) for i in range(replica...  49.5 us
    all_to_all x3, blocking collectives, step(): lax.all_to_all(terms[-1][served], 'rows', split_axis=0, concat_axis=0, ti...  48.2 us
    pallas_call x3, Pallas kernels, tile_sums(): pl.pallas_call(body, out_shape=(pltpu.VMEM(shape, jnp.bfloat16), pltpu.VM...  11.6 us
    pallas_call x3, Pallas kernels, load_live(): pl.pallas_call(body, out_shape=(pltpu.VMEM(values.shape, values.dtype), p...  10.5 us
    all_to_all x1, starting transfers between devices, on_device(): lax.all_to_all(wanted, 'rows', split_axis=0, concat_axis=0, tiled=True)  8.16 us
    all_to_all x1, waiting for transfers between devices, on_device(): lax.all_to_all(wanted, 'rows', split_axis=0, concat_axis=0, tiled=True)  6.58 us
    ppermute x18, waiting for transfers between devices, partner(): return lax.ppermute(x, 'rep', [(i, i ^ 1) for i in range(replicas)])  6.26 us
  transfers between devices with their start and end apart: 50, of which 22 were waited for; matrix products, arithmetic and copies ran while one was open for 2% of the time, Pallas kernels for 7%

profile of v4, /device:TPU:0, one launch (start us, length us, event | category | flops | bytes accessed | tf_op | source)
XLA Modules:
  0.0 217.2 jit_solution(13450810098621591652)
XLA Ops:
  0.0 1.4 copy.20
  1.4 8.2 %all-to-all-start = ((s32[16,1,8]{2,1,0:T(1,128)}), s32[16,1,8]{2,1,0:T(1,128)S(1)}, u32[]{:S(2)}, u32[]{:S(2)}) async-start(s32[16,1,8]{2,1,0:T(1,128)} %copy.20), calls=%async_computation | async-start | bytes 16384 | tf_op jit(solution)/shard_map/all_to_all | solution.py:192
  9.5 0.9 constant_dynamic-slice_fusion
  10.5 6.6 %all-to-all-done = s32[16,1,8]{2,1,0:T(1,128)S(1)} async-done(((s32[16,1,8]{2,1,0:T(1,128)}), s32[16,1,8]{2,1,0:T(1,128)S(1)}, u32[]{:S(2)}, u32[]{:S(2)}) %all-to-all-start) | async-done | bytes 544 | tf_op jit(solution)/shard_map/all_to_all | solution.py:192
  18.0 13.1 %all_to_all.32 = bf16[16,8,16,128]{3,2,1,0:T(8,128)(2,1)S(1)} all-to-all(bf16[16,8,16,128]{3,2,1,0:T(8,128)(2,1)S(1)} %bitcast.196), channel_id=1, replica_groups=mesh['rows'=16,'rep'=8] {'rows'}, dimensions={0} | all-to-all | bytes 1048576 | tf_op jit(solution)/shard_map/all_to_all | solution.py:201
  31.1 1.5 collective-permute-start.1
  32.6 1.7 collective-permute-start.3
  34.3 9.1 %collective-permute-done.1 = bf16[128,16,128]{2,1,0:T(8,128)(2,1)S(1)} collective-permute-done((bf16[128,16,128]{2,1,0:T(8,128)(2,1)S(1)}, bf16[128,16,128]{2,1,0:T(8,128)(2,1)S(1)}, u32[]{:S(2)}, u32[]{:S(2)}) %collective-permute-start.1) | collective-permute-done | bytes 524320 | tf_op jit(solution)/shard_map/ppermute | solution.py:147
  44.1 3.5 %load_live.3 = (bf16[512,128,128]{2,1,0:T(8,128)(2,1)S(1)}, bf16[8,128,16,128]{3,2,1,0:T(8,128)(2,1)S(1)}) custom-call(s32[11]{0:T(128)S(1)} %stack.52.scalar, bf16[512,128,128]{2,1,0:T(8,128)(2,1)} %bitcast.191, bf16[128,16,128]{2,1,0:T(8,128)(2,1)S(1)} %bitcast.176), custom_call_target="tpu_custom_call" | custom-call | tf_op jit(solution)/shard_map/load_live/pallas_call | solution.py:97
  47.8 3.3 %collective-permute-start.7 = (bf16[64,16,128]{2,1,0:T(8,128)(2,1)S(1)}, bf16[64,16,128]{2,1,0:T(8,128)(2,1)S(1)}, u32[]{:S(2)}, u32[]{:S(2)}) collective-permute-start(bf16[64,16,128]{2,1,0:T(8,128)(2,1)S(1)} %slice.159), channel_id=1, source_target_pairs={{2,0},{3,1},{4,2},{5,3},{6,4},{7,5},{0,6},{1,7},{10,8},{11,9},{12,... | collective-permute-start | bytes 786440 | tf_op jit(solution)/shard_map/ppermute | solution.py:147
  51.5 6.5 %collective-permute-done.5 = bf16[64,16,128]{2,1,0:T(8,128)(2,1)S(1)} collective-permute-done((bf16[64,16,128]{2,1,0:T(8,128)(2,1)S(1)}, bf16[64,16,128]{2,1,0:T(8,128)(2,1)S(1)}, u32[]{:S(2)}, u32[]{:S(2)}) %collective-permute-start.5) | collective-permute-done | bytes 262176 | tf_op jit(solution)/shard_map/ppermute | solution.py:147
  60.0 3.9 %tile_sums.3 = (bf16[4,32,16,128]{3,2,1,0:T(8,128)(2,1)S(1)}, f32[4,32,16,128]{3,2,1,0:T(8,128)S(1)}) custom-call(s32[11]{0:T(128)S(1)} %stack.52.scalar, s32[512]{0:T(512)S(1)} %bitcast.185, s32[512]{0:T(512)S(1)} %bitcast.188, bf16[8,128,16,128]{3,2,1,0:T(8,128)(2,1)S(1)} %bitcast_dynamic-update-slice_fusion.23.fetched, ...), custom_call_target="tpu_custom_call" | custom-call | tf_op jit(solution)/shard_map/tile_sums/pallas_call | solution.py:57
  63.9 0.7 collective-permute-start.9
  64.6 1.5 collective-permute-done.9
  66.4 3.2 %collective-permute-start.11 = (bf16[32,16,128]{2,1,0:T(8,128)(2,1)S(1)}, bf16[32,16,128]{2,1,0:T(8,128)(2,1)S(1)}, u32[]{:S(2)}, u32[]{:S(2)}) collective-permute-start(bf16[32,16,128]{2,1,0:T(8,128)(2,1)S(1)} %get-tuple-element.46), channel_id=1, source_target_pairs={{2,0},{3,1},{4,2},{5,3},{6,4},{7,5},{0,6},{1,7},{10,8},{11,9},{12,... | collective-permute-start | bytes 393224 | tf_op jit(solution)/shard_map/ppermute | solution.py:147
  69.6 3.2 %collective-permute-start.14 = (bf16[16,16,128]{2,1,0:T(8,128)(2,1)S(1)}, bf16[16,16,128]{2,1,0:T(8,128)(2,1)S(1)}, u32[]{:S(2)}, u32[]{:S(2)}) collective-permute-start(bf16[16,16,128]{2,1,0:T(8,128)(2,1)S(1)} %get-tuple-element.44), channel_id=1, source_target_pairs={{2,0},{3,1},{4,2},{5,3},{6,4},{7,5},{0,6},{1,7},{10,8},{11,9},{12,... | collective-permute-start | bytes 196616 | tf_op jit(solution)/shard_map/ppermute | solution.py:147
  72.9 2.2 %collective-permute-done.12 = bf16[16,16,128]{2,1,0:T(8,128)(2,1)S(1)} collective-permute-done((bf16[16,16,128]{2,1,0:T(8,128)(2,1)S(1)}, bf16[16,16,128]{2,1,0:T(8,128)(2,1)S(1)}, u32[]{:S(2)}, u32[]{:S(2)}) %collective-permute-start.12) | collective-permute-done | bytes 65568 | tf_op jit(solution)/shard_map/ppermute | solution.py:147
  75.1 3.2 %collective-permute-start.15 = (bf16[16,16,128]{2,1,0:T(8,128)(2,1)S(1)}, bf16[16,16,128]{2,1,0:T(8,128)(2,1)S(1)}, u32[]{:S(2)}, u32[]{:S(2)}) collective-permute-start(bf16[16,16,128]{2,1,0:T(8,128)(2,1)S(1)} %collective-permute-done.14), channel_id=1, source_target_pairs={{2,0},{3,1},{4,2},{5,3},{6,4},{7,5},{0,6},{1,7},{10,8},{11,9},{12,... | collective-permute-start | bytes 196616 | tf_op jit(solution)/shard_map/ppermute | solution.py:147
  78.4 2.2 %collective-permute-done.13 = bf16[16,16,128]{2,1,0:T(8,128)(2,1)S(1)} collective-permute-done((bf16[16,16,128]{2,1,0:T(8,128)(2,1)S(1)}, bf16[16,16,128]{2,1,0:T(8,128)(2,1)S(1)}, u32[]{:S(2)}, u32[]{:S(2)}) %collective-permute-start.13) | collective-permute-done | bytes 65568 | tf_op jit(solution)/shard_map/ppermute | solution.py:147
  81.4 17.4 %all_to_all.33 = bf16[16,8,16,128]{3,2,1,0:T(8,128)(2,1)S(1)} all-to-all(bf16[16,8,16,128]{3,2,1,0:T(8,128)(2,1)S(1)} %bitcast.198), channel_id=1, replica_groups=mesh['rows'=16,'rep'=8] {'rows'}, dimensions={0} | all-to-all | bytes 1048576 | tf_op jit(solution)/shard_map/all_to_all | solution.py:201
  98.8 3.2 %collective-permute-start.19 = (bf16[128,16,128]{2,1,0:T(8,128)(2,1)S(1)}, bf16[128,16,128]{2,1,0:T(8,128)(2,1)S(1)}, u32[]{:S(2)}, u32[]{:S(2)}) collective-permute-start(bf16[128,16,128]{2,1,0:T(8,128)(2,1)S(1)} %bitcast.182), channel_id=1, source_target_pairs={{2,0},{3,1},{4,2},{5,3},{6,4},{7,5},{0,6},{1,7},{10,8},{11,9},{12,... | collective-permute-start | bytes 1572872 | tf_op jit(solution)/shard_map/ppermute | solution.py:147
  102.0 8.3 %collective-permute-done.17 = bf16[128,16,128]{2,1,0:T(8,128)(2,1)S(1)} collective-permute-done((bf16[128,16,128]{2,1,0:T(8,128)(2,1)S(1)}, bf16[128,16,128]{2,1,0:T(8,128)(2,1)S(1)}, u32[]{:S(2)}, u32[]{:S(2)}) %collective-permute-start.17) | collective-permute-done | bytes 524320 | tf_op jit(solution)/shard_map/ppermute | solution.py:147
  110.3 3.5 %load_live.4 = (bf16[512,128,128]{2,1,0:T(8,128)(2,1)S(1)}, bf16[8,128,16,128]{3,2,1,0:T(8,128)(2,1)S(1)}) custom-call(s32[11]{0:T(128)S(1)} %stack.52.scalar, bf16[512,128,128]{2,1,0:T(8,128)(2,1)} %bitcast.192, bf16[128,16,128]{2,1,0:T(8,128)(2,1)S(1)} %bitcast.184), custom_call_target="tpu_custom_call" | custom-call | tf_op jit(solution)/shard_map/load_live/pallas_call | solution.py:97
  114.0 3.3 %collective-permute-start.23 = (bf16[64,16,128]{2,1,0:T(8,128)(2,1)S(1)}, bf16[64,16,128]{2,1,0:T(8,128)(2,1)S(1)}, u32[]{:S(2)}, u32[]{:S(2)}) collective-permute-start(bf16[64,16,128]{2,1,0:T(8,128)(2,1)S(1)} %slice.166), channel_id=1, source_target_pairs={{2,0},{3,1},{4,2},{5,3},{6,4},{7,5},{0,6},{1,7},{10,8},{11,9},{12,... | collective-permute-start | bytes 786440 | tf_op jit(solution)/shard_map/ppermute | solution.py:147
  117.7 6.5 %collective-permute-done.21 = bf16[64,16,128]{2,1,0:T(8,128)(2,1)S(1)} collective-permute-done((bf16[64,16,128]{2,1,0:T(8,128)(2,1)S(1)}, bf16[64,16,128]{2,1,0:T(8,128)(2,1)S(1)}, u32[]{:S(2)}, u32[]{:S(2)}) %collective-permute-start.21) | collective-permute-done | bytes 262176 | tf_op jit(solution)/shard_map/ppermute | solution.py:147
  126.1 3.9 %tile_sums.4 = (bf16[4,32,16,128]{3,2,1,0:T(8,128)(2,1)S(1)}, f32[4,32,16,128]{3,2,1,0:T(8,128)S(1)}) custom-call(s32[11]{0:T(128)S(1)} %stack.52.scalar, s32[512]{0:T(512)S(1)} %bitcast.186, s32[512]{0:T(512)S(1)} %bitcast.189, bf16[8,128,16,128]{3,2,1,0:T(8,128)(2,1)S(1)} %bitcast_dynamic-update-slice_fusion.19.fetched, ...), custom_call_target="tpu_custom_call" | custom-call | tf_op jit(solution)/shard_map/tile_sums/pallas_call | solution.py:57
  130.7 1.5 collective-permute-done.25
  132.6 3.2 %collective-permute-start.27 = (bf16[32,16,128]{2,1,0:T(8,128)(2,1)S(1)}, bf16[32,16,128]{2,1,0:T(8,128)(2,1)S(1)}, u32[]{:S(2)}, u32[]{:S(2)}) collective-permute-start(bf16[32,16,128]{2,1,0:T(8,128)(2,1)S(1)} %get-tuple-element.42), channel_id=1, source_target_pairs={{2,0},{3,1},{4,2},{5,3},{6,4},{7,5},{0,6},{1,7},{10,8},{11,9},{12,... | collective-permute-start | bytes 393224 | tf_op jit(solution)/shard_map/ppermute | solution.py:147
  135.8 3.2 %collective-permute-start.30 = (bf16[16,16,128]{2,1,0:T(8,128)(2,1)S(1)}, bf16[16,16,128]{2,1,0:T(8,128)(2,1)S(1)}, u32[]{:S(2)}, u32[]{:S(2)}) collective-permute-start(bf16[16,16,128]{2,1,0:T(8,128)(2,1)S(1)} %get-tuple-element.40), channel_id=1, source_target_pairs={{2,0},{3,1},{4,2},{5,3},{6,4},{7,5},{0,6},{1,7},{10,8},{11,9},{12,... | collective-permute-start | bytes 196616 | tf_op jit(solution)/shard_map/ppermute | solution.py:147
  139.0 2.2 %collective-permute-done.28 = bf16[16,16,128]{2,1,0:T(8,128)(2,1)S(1)} collective-permute-done((bf16[16,16,128]{2,1,0:T(8,128)(2,1)S(1)}, bf16[16,16,128]{2,1,0:T(8,128)(2,1)S(1)}, u32[]{:S(2)}, u32[]{:S(2)}) %collective-permute-start.28) | collective-permute-done | bytes 65568 | tf_op jit(solution)/shard_map/ppermute | solution.py:147
  141.3 3.2 %collective-permute-start.31 = (bf16[16,16,128]{2,1,0:T(8,128)(2,1)S(1)}, bf16[16,16,128]{2,1,0:T(8,128)(2,1)S(1)}, u32[]{:S(2)}, u32[]{:S(2)}) collective-permute-start(bf16[16,16,128]{2,1,0:T(8,128)(2,1)S(1)} %collective-permute-done.30), channel_id=1, source_target_pairs={{2,0},{3,1},{4,2},{5,3},{6,4},{7,5},{0,6},{1,7},{10,8},{11,9},{12,... | collective-permute-start | bytes 196616 | tf_op jit(solution)/shard_map/ppermute | solution.py:147
  144.5 2.2 %collective-permute-done.29 = bf16[16,16,128]{2,1,0:T(8,128)(2,1)S(1)} collective-permute-done((bf16[16,16,128]{2,1,0:T(8,128)(2,1)S(1)}, bf16[16,16,128]{2,1,0:T(8,128)(2,1)S(1)}, u32[]{:S(2)}, u32[]{:S(2)}) %collective-permute-start.29) | collective-permute-done | bytes 65568 | tf_op jit(solution)/shard_map/ppermute | solution.py:147
  146.7 1.0 fusion.12
  148.5 17.7 %all_to_all.34 = bf16[16,8,16,128]{3,2,1,0:T(8,128)(2,1)S(1)} all-to-all(bf16[16,8,16,128]{3,2,1,0:T(8,128)(2,1)S(1)} %bitcast.197), channel_id=1, replica_groups=mesh['rows'=16,'rep'=8] {'rows'}, dimensions={0} | all-to-all | bytes 1048576 | tf_op jit(solution)/shard_map/all_to_all | solution.py:201
  166.2 3.2 %collective-permute-start.35 = (bf16[128,16,128]{2,1,0:T(8,128)(2,1)S(1)}, bf16[128,16,128]{2,1,0:T(8,128)(2,1)S(1)}, u32[]{:S(2)}, u32[]{:S(2)}) collective-permute-start(bf16[128,16,128]{2,1,0:T(8,128)(2,1)S(1)} %bitcast.178), channel_id=1, source_target_pairs={{2,0},{3,1},{4,2},{5,3},{6,4},{7,5},{0,6},{1,7},{10,8},{11,9},{12,... | collective-permute-start | bytes 1572872 | tf_op jit(solution)/shard_map/ppermute | solution.py:147
  169.4 8.3 %collective-permute-done.33 = bf16[128,16,128]{2,1,0:T(8,128)(2,1)S(1)} collective-permute-done((bf16[128,16,128]{2,1,0:T(8,128)(2,1)S(1)}, bf16[128,16,128]{2,1,0:T(8,128)(2,1)S(1)}, u32[]{:S(2)}, u32[]{:S(2)}) %collective-permute-start.33) | collective-permute-done | bytes 524320 | tf_op jit(solution)/shard_map/ppermute | solution.py:147
  178.4 3.4 %all-to-all-start.3 = ((bf16[8,4,2,16,128]{4,3,1,2,0:T(8,128)(2,1)}), bf16[8,4,2,16,128]{4,3,1,2,0:T(8,128)(2,1)S(1)}, u32[]{:S(2)}, u32[]{:S(2)}) async-start(bf16[8,4,2,16,128]{4,3,1,2,0:T(8,128)(2,1)} %pad_maximum_fusion), calls=%async_computation.3 | async-start | bytes 524288 | tf_op jit(solution)/shard_map/all_to_all | solution.py:176
  181.8 3.5 %load_live.5 = (bf16[512,128,128]{2,1,0:T(8,128)(2,1)S(1)}, bf16[8,128,16,128]{3,2,1,0:T(8,128)(2,1)S(1)}) custom-call(s32[11]{0:T(128)S(1)} %stack.52.scalar, bf16[512,128,128]{2,1,0:T(8,128)(2,1)} %bitcast.193, bf16[128,16,128]{2,1,0:T(8,128)(2,1)S(1)} %bitcast.180), custom_call_target="tpu_custom_call" | custom-call | tf_op jit(solution)/shard_map/load_live/pallas_call | solution.py:97
  185.4 1.0 collective-permute-start.37
  186.4 2.6 %collective-permute-start.39 = (bf16[64,16,128]{2,1,0:T(8,128)(2,1)S(1)}, bf16[64,16,128]{2,1,0:T(8,128)(2,1)S(1)}, u32[]{:S(2)}, u32[]{:S(2)}) collective-permute-start(bf16[64,16,128]{2,1,0:T(8,128)(2,1)S(1)} %slice.175), channel_id=1, source_target_pairs={{2,0},{3,1},{4,2},{5,3},{6,4},{7,5},{0,6},{1,7},{10,8},{11,9},{12,... | collective-permute-start | bytes 786440 | tf_op jit(solution)/shard_map/ppermute | solution.py:147
  189.3 6.5 %collective-permute-done.37 = bf16[64,16,128]{2,1,0:T(8,128)(2,1)S(1)} collective-permute-done((bf16[64,16,128]{2,1,0:T(8,128)(2,1)S(1)}, bf16[64,16,128]{2,1,0:T(8,128)(2,1)S(1)}, u32[]{:S(2)}, u32[]{:S(2)}) %collective-permute-start.37) | collective-permute-done | bytes 262176 | tf_op jit(solution)/shard_map/ppermute | solution.py:147
  197.8 3.9 %tile_sums.5 = (bf16[4,32,16,128]{3,2,1,0:T(8,128)(2,1)S(1)}, f32[4,32,16,128]{3,2,1,0:T(8,128)S(1)}) custom-call(s32[11]{0:T(128)S(1)} %stack.52.scalar, s32[512]{0:T(512)S(1)} %bitcast.187, s32[512]{0:T(512)S(1)} %bitcast.190, bf16[8,128,16,128]{3,2,1,0:T(8,128)(2,1)S(1)} %bitcast_dynamic-update-slice_fusion.15.fetched, ...), custom_call_target="tpu_custom_call" | custom-call | tf_op jit(solution)/shard_map/tile_sums/pallas_call | solution.py:57
  202.4 1.1 fusion.17
  204.2 3.2 %collective-permute-start.46 = (bf16[16,16,128]{2,1,0:T(8,128)(2,1)S(1)}, bf16[16,16,128]{2,1,0:T(8,128)(2,1)S(1)}, u32[]{:S(2)}, u32[]{:S(2)}) collective-permute-start(bf16[16,16,128]{2,1,0:T(8,128)(2,1)S(1)} %get-tuple-element.36), channel_id=1, source_target_pairs={{2,0},{3,1},{4,2},{5,3},{6,4},{7,5},{0,6},{1,7},{10,8},{11,9},{12,... | collective-permute-start | bytes 196616 | tf_op jit(solution)/shard_map/ppermute | solution.py:147
  207.5 3.2 %collective-permute-start.43 = (bf16[32,16,128]{2,1,0:T(8,128)(2,1)S(1)}, bf16[32,16,128]{2,1,0:T(8,128)(2,1)S(1)}, u32[]{:S(2)}, u32[]{:S(2)}) collective-permute-start(bf16[32,16,128]{2,1,0:T(8,128)(2,1)S(1)} %get-tuple-element.38), channel_id=1, source_target_pairs={{2,0},{3,1},{4,2},{5,3},{6,4},{7,5},{0,6},{1,7},{10,8},{11,9},{12,... | collective-permute-start | bytes 393224 | tf_op jit(solution)/shard_map/ppermute | solution.py:147
  210.8 3.2 %collective-permute-start.47 = (bf16[16,16,128]{2,1,0:T(8,128)(2,1)S(1)}, bf16[16,16,128]{2,1,0:T(8,128)(2,1)S(1)}, u32[]{:S(2)}, u32[]{:S(2)}) collective-permute-start(bf16[16,16,128]{2,1,0:T(8,128)(2,1)S(1)} %collective-permute-done.46), channel_id=1, source_target_pairs={{2,0},{3,1},{4,2},{5,3},{6,4},{7,5},{0,6},{1,7},{10,8},{11,9},{12,... | collective-permute-start | bytes 196616 | tf_op jit(solution)/shard_map/ppermute | solution.py:147
  214.3 1.9 collective-permute-done.45
  216.3 0.9 fusion
  (130 shorter events, 13.5 us)
Async XLA Ops:
  1.4 15.7 %all-to-all-start = ((s32[16,1,8]{2,1,0:T(1,128)}), s32[16,1,8]{2,1,0:T(1,128)S(1)}, u32[]{:S(2)}, u32[]{:S(2)}) async-start(s32[16,1,8]{2,1,0:T(1,128)} %copy.20), calls=%async_computation | async-start | bytes 16384 | tf_op jit(solution)/shard_map/all_to_all | solution.py:192
  31.1 12.3 %collective-permute-start.1 = (bf16[128,16,128]{2,1,0:T(8,128)(2,1)S(1)}, bf16[128,16,128]{2,1,0:T(8,128)(2,1)S(1)}, u32[]{:S(2)}, u32[]{:S(2)}) collective-permute-start(bf16[128,16,128]{2,1,0:T(8,128)(2,1)S(1)} %bitcast.173), channel_id=1, source_target_pairs={{6,0},{7,1},{0,2},{1,3},{2,4},{3,5},{4,6},{5,7},{14,8},{15,9},{8,1... | collective-permute-start | bytes 1572872 | tf_op jit(solution)/shard_map/ppermute | solution.py:147
  32.6 15.2 %collective-permute-start.3 = (bf16[128,16,128]{2,1,0:T(8,128)(2,1)S(1)}, bf16[128,16,128]{2,1,0:T(8,128)(2,1)S(1)}, u32[]{:S(2)}, u32[]{:S(2)}) collective-permute-start(bf16[128,16,128]{2,1,0:T(8,128)(2,1)S(1)} %bitcast.174), channel_id=1, source_target_pairs={{2,0},{3,1},{4,2},{5,3},{6,4},{7,5},{0,6},{1,7},{10,8},{11,9},{12,... | collective-permute-start | bytes 1572872 | tf_op jit(solution)/shard_map/ppermute | solution.py:147
  34.3 17.0 %collective-permute-start = (bf16[128,16,128]{2,1,0:T(8,128)(2,1)S(1)}, bf16[128,16,128]{2,1,0:T(8,128)(2,1)S(1)}, u32[]{:S(2)}, u32[]{:S(2)}) collective-permute-start(bf16[128,16,128]{2,1,0:T(8,128)(2,1)S(1)} %bitcast.175), channel_id=1, source_target_pairs={{0,1},{1,0},{2,3},{3,2},{4,5},{5,4},{6,7},{7,6},{8,9},{9,8},{10,11... | collective-permute-start | bytes 1572872 | tf_op jit(solution)/shard_map/ppermute | solution.py:150
  43.4 15.1 %collective-permute-start.2 = (bf16[128,16,128]{2,1,0:T(8,128)(2,1)S(1)}, bf16[128,16,128]{2,1,0:T(8,128)(2,1)S(1)}, u32[]{:S(2)}, u32[]{:S(2)}) collective-permute-start(bf16[128,16,128]{2,1,0:T(8,128)(2,1)S(1)} %collective-permute-done.1), channel_id=1, source_target_pairs={{0,1},{1,0},{2,3},{3,2},{4,5},{5,4},{6,7},{7,6},{8,9},{9,8},{10,11... | collective-permute-start | bytes 1572872 | tf_op jit(solution)/shard_map/ppermute | solution.py:150
  47.7 10.3 %collective-permute-start.5 = (bf16[64,16,128]{2,1,0:T(8,128)(2,1)S(1)}, bf16[64,16,128]{2,1,0:T(8,128)(2,1)S(1)}, u32[]{:S(2)}, u32[]{:S(2)}) collective-permute-start(bf16[64,16,128]{2,1,0:T(8,128)(2,1)S(1)} %slice.158), channel_id=1, source_target_pairs={{6,0},{7,1},{0,2},{1,3},{2,4},{3,5},{4,6},{5,7},{14,8},{15,9},{8,1... | collective-permute-start | bytes 786440 | tf_op jit(solution)/shard_map/ppermute | solution.py:147
  47.8 10.2 %collective-permute-start.7 = (bf16[64,16,128]{2,1,0:T(8,128)(2,1)S(1)}, bf16[64,16,128]{2,1,0:T(8,128)(2,1)S(1)}, u32[]{:S(2)}, u32[]{:S(2)}) collective-permute-start(bf16[64,16,128]{2,1,0:T(8,128)(2,1)S(1)} %slice.159), channel_id=1, source_target_pairs={{2,0},{3,1},{4,2},{5,3},{6,4},{7,5},{0,6},{1,7},{10,8},{11,9},{12,... | collective-permute-start | bytes 786440 | tf_op jit(solution)/shard_map/ppermute | solution.py:147
  51.1 7.6 %collective-permute-start.4 = (bf16[128,16,128]{2,1,0:T(8,128)(2,1)S(1)}, bf16[128,16,128]{2,1,0:T(8,128)(2,1)S(1)}, u32[]{:S(2)}, u32[]{:S(2)}) collective-permute-start(bf16[128,16,128]{2,1,0:T(8,128)(2,1)S(1)} %collective-permute-done.3), channel_id=1, source_target_pairs={{0,1},{1,0},{2,3},{3,2},{4,5},{5,4},{6,7},{7,6},{8,9},{9,8},{10,11... | collective-permute-start | bytes 1572872 | tf_op jit(solution)/shard_map/ppermute | solution.py:150
  58.0 1.5 collective-permute-start.6
  58.0 1.9 collective-permute-start.8
  63.9 2.3 %collective-permute-start.9 = (bf16[4,32,16,128]{3,2,1,0:T(8,128)(2,1)S(1)}, bf16[4,32,16,128]{3,2,1,0:T(8,128)(2,1)S(1)}, u32[]{:S(2)}, u32[]{:S(2)}) collective-permute-start(bf16[4,32,16,128]{3,2,1,0:T(8,128)(2,1)S(1)} %get-tuple-element.20), channel_id=1, source_target_pairs={{0,1},{1,0},{2,3},{3,2},{4,5},{5,4},{6,7},{7,6},{8,9},{9,8},{10,11... | collective-permute-start | bytes 1572872 | tf_op jit(solution)/shard_map/ppermute | solution.py:150
  66.3 12.0 %collective-permute-start.10 = (bf16[32,16,128]{2,1,0:T(8,128)(2,1)S(1)}, bf16[32,16,128]{2,1,0:T(8,128)(2,1)S(1)}, u32[]{:S(2)}, u32[]{:S(2)}) collective-permute-start(bf16[32,16,128]{2,1,0:T(8,128)(2,1)S(1)} %get-tuple-element.45), channel_id=1, source_target_pairs={{6,0},{7,1},{0,2},{1,3},{2,4},{3,5},{4,6},{5,7},{14,8},{15,9},{8,1... | collective-permute-start | bytes 393224 | tf_op jit(solution)/shard_map/ppermute | solution.py:147
  66.4 11.9 %collective-permute-start.11 = (bf16[32,16,128]{2,1,0:T(8,128)(2,1)S(1)}, bf16[32,16,128]{2,1,0:T(8,128)(2,1)S(1)}, u32[]{:S(2)}, u32[]{:S(2)}) collective-permute-start(bf16[32,16,128]{2,1,0:T(8,128)(2,1)S(1)} %get-tuple-element.46), channel_id=1, source_target_pairs={{2,0},{3,1},{4,2},{5,3},{6,4},{7,5},{0,6},{1,7},{10,8},{11,9},{12,... | collective-permute-start | bytes 393224 | tf_op jit(solution)/shard_map/ppermute | solution.py:147
  69.6 5.5 %collective-permute-start.12 = (bf16[16,16,128]{2,1,0:T(8,128)(2,1)S(1)}, bf16[16,16,128]{2,1,0:T(8,128)(2,1)S(1)}, u32[]{:S(2)}, u32[]{:S(2)}) collective-permute-start(bf16[16,16,128]{2,1,0:T(8,128)(2,1)S(1)} %get-tuple-element.43), channel_id=1, source_target_pairs={{6,0},{7,1},{0,2},{1,3},{2,4},{3,5},{4,6},{5,7},{14,8},{15,9},{8,1... | collective-permute-start | bytes 196616 | tf_op jit(solution)/shard_map/ppermute | solution.py:147
  69.6 5.5 %collective-permute-start.14 = (bf16[16,16,128]{2,1,0:T(8,128)(2,1)S(1)}, bf16[16,16,128]{2,1,0:T(8,128)(2,1)S(1)}, u32[]{:S(2)}, u32[]{:S(2)}) collective-permute-start(bf16[16,16,128]{2,1,0:T(8,128)(2,1)S(1)} %get-tuple-element.44), channel_id=1, source_target_pairs={{2,0},{3,1},{4,2},{5,3},{6,4},{7,5},{0,6},{1,7},{10,8},{11,9},{12,... | collective-permute-start | bytes 196616 | tf_op jit(solution)/shard_map/ppermute | solution.py:147
  75.1 5.5 %collective-permute-start.13 = (bf16[16,16,128]{2,1,0:T(8,128)(2,1)S(1)}, bf16[16,16,128]{2,1,0:T(8,128)(2,1)S(1)}, u32[]{:S(2)}, u32[]{:S(2)}) collective-permute-start(bf16[16,16,128]{2,1,0:T(8,128)(2,1)S(1)} %collective-permute-done.12), channel_id=1, source_target_pairs={{6,0},{7,1},{0,2},{1,3},{2,4},{3,5},{4,6},{5,7},{14,8},{15,9},{8,1... | collective-permute-start | bytes 196616 | tf_op jit(solution)/shard_map/ppermute | solution.py:147
  75.1 5.5 %collective-permute-start.15 = (bf16[16,16,128]{2,1,0:T(8,128)(2,1)S(1)}, bf16[16,16,128]{2,1,0:T(8,128)(2,1)S(1)}, u32[]{:S(2)}, u32[]{:S(2)}) collective-permute-start(bf16[16,16,128]{2,1,0:T(8,128)(2,1)S(1)} %collective-permute-done.14), channel_id=1, source_target_pairs={{2,0},{3,1},{4,2},{5,3},{6,4},{7,5},{0,6},{1,7},{10,8},{11,9},{12,... | collective-permute-start | bytes 196616 | tf_op jit(solution)/shard_map/ppermute | solution.py:147
  98.8 11.5 %collective-permute-start.17 = (bf16[128,16,128]{2,1,0:T(8,128)(2,1)S(1)}, bf16[128,16,128]{2,1,0:T(8,128)(2,1)S(1)}, u32[]{:S(2)}, u32[]{:S(2)}) collective-permute-start(bf16[128,16,128]{2,1,0:T(8,128)(2,1)S(1)} %bitcast.181), channel_id=1, source_target_pairs={{6,0},{7,1},{0,2},{1,3},{2,4},{3,5},{4,6},{5,7},{14,8},{15,9},{8,1... | collective-permute-start | bytes 1572872 | tf_op jit(solution)/shard_map/ppermute | solution.py:147
  98.8 15.1 %collective-permute-start.19 = (bf16[128,16,128]{2,1,0:T(8,128)(2,1)S(1)}, bf16[128,16,128]{2,1,0:T(8,128)(2,1)S(1)}, u32[]{:S(2)}, u32[]{:S(2)}) collective-permute-start(bf16[128,16,128]{2,1,0:T(8,128)(2,1)S(1)} %bitcast.182), channel_id=1, source_target_pairs={{2,0},{3,1},{4,2},{5,3},{6,4},{7,5},{0,6},{1,7},{10,8},{11,9},{12,... | collective-permute-start | bytes 1572872 | tf_op jit(solution)/shard_map/ppermute | solution.py:147
  102.0 15.5 %collective-permute-start.16 = (bf16[128,16,128]{2,1,0:T(8,128)(2,1)S(1)}, bf16[128,16,128]{2,1,0:T(8,128)(2,1)S(1)}, u32[]{:S(2)}, u32[]{:S(2)}) collective-permute-start(bf16[128,16,128]{2,1,0:T(8,128)(2,1)S(1)} %bitcast.183), channel_id=1, source_target_pairs={{0,1},{1,0},{2,3},{3,2},{4,5},{5,4},{6,7},{7,6},{8,9},{9,8},{10,11... | collective-permute-start | bytes 1572872 | tf_op jit(solution)/shard_map/ppermute | solution.py:150
  110.3 14.4 %collective-permute-start.18 = (bf16[128,16,128]{2,1,0:T(8,128)(2,1)S(1)}, bf16[128,16,128]{2,1,0:T(8,128)(2,1)S(1)}, u32[]{:S(2)}, u32[]{:S(2)}) collective-permute-start(bf16[128,16,128]{2,1,0:T(8,128)(2,1)S(1)} %collective-permute-done.17), channel_id=1, source_target_pairs={{0,1},{1,0},{2,3},{3,2},{4,5},{5,4},{6,7},{7,6},{8,9},{9,8},{10,11... | collective-permute-start | bytes 1572872 | tf_op jit(solution)/shard_map/ppermute | solution.py:150
  113.9 10.3 %collective-permute-start.21 = (bf16[64,16,128]{2,1,0:T(8,128)(2,1)S(1)}, bf16[64,16,128]{2,1,0:T(8,128)(2,1)S(1)}, u32[]{:S(2)}, u32[]{:S(2)}) collective-permute-start(bf16[64,16,128]{2,1,0:T(8,128)(2,1)S(1)} %slice.165), channel_id=1, source_target_pairs={{6,0},{7,1},{0,2},{1,3},{2,4},{3,5},{4,6},{5,7},{14,8},{15,9},{8,1... | collective-permute-start | bytes 786440 | tf_op jit(solution)/shard_map/ppermute | solution.py:147
  114.0 10.2 %collective-permute-start.23 = (bf16[64,16,128]{2,1,0:T(8,128)(2,1)S(1)}, bf16[64,16,128]{2,1,0:T(8,128)(2,1)S(1)}, u32[]{:S(2)}, u32[]{:S(2)}) collective-permute-start(bf16[64,16,128]{2,1,0:T(8,128)(2,1)S(1)} %slice.166), channel_id=1, source_target_pairs={{2,0},{3,1},{4,2},{5,3},{6,4},{7,5},{0,6},{1,7},{10,8},{11,9},{12,... | collective-permute-start | bytes 786440 | tf_op jit(solution)/shard_map/ppermute | solution.py:147
  117.3 7.6 %collective-permute-start.20 = (bf16[128,16,128]{2,1,0:T(8,128)(2,1)S(1)}, bf16[128,16,128]{2,1,0:T(8,128)(2,1)S(1)}, u32[]{:S(2)}, u32[]{:S(2)}) collective-permute-start(bf16[128,16,128]{2,1,0:T(8,128)(2,1)S(1)} %collective-permute-done.19), channel_id=1, source_target_pairs={{0,1},{1,0},{2,3},{3,2},{4,5},{5,4},{6,7},{7,6},{8,9},{9,8},{10,11... | collective-permute-start | bytes 1572872 | tf_op jit(solution)/shard_map/ppermute | solution.py:150
  124.2 1.9 collective-permute-start.24
  130.0 2.2 %collective-permute-start.25 = (bf16[4,32,16,128]{3,2,1,0:T(8,128)(2,1)S(1)}, bf16[4,32,16,128]{3,2,1,0:T(8,128)(2,1)S(1)}, u32[]{:S(2)}, u32[]{:S(2)}) collective-permute-start(bf16[4,32,16,128]{3,2,1,0:T(8,128)(2,1)S(1)} %get-tuple-element.24), channel_id=1, source_target_pairs={{0,1},{1,0},{2,3},{3,2},{4,5},{5,4},{6,7},{7,6},{8,9},{9,8},{10,11... | collective-permute-start | bytes 1572872 | tf_op jit(solution)/shard_map/ppermute | solution.py:150
  132.5 12.0 %collective-permute-start.26 = (bf16[32,16,128]{2,1,0:T(8,128)(2,1)S(1)}, bf16[32,16,128]{2,1,0:T(8,128)(2,1)S(1)}, u32[]{:S(2)}, u32[]{:S(2)}) collective-permute-start(bf16[32,16,128]{2,1,0:T(8,128)(2,1)S(1)} %get-tuple-element.41), channel_id=1, source_target_pairs={{6,0},{7,1},{0,2},{1,3},{2,4},{3,5},{4,6},{5,7},{14,8},{15,9},{8,1... | collective-permute-start | bytes 393224 | tf_op jit(solution)/shard_map/ppermute | solution.py:147
  132.6 11.9 %collective-permute-start.27 = (bf16[32,16,128]{2,1,0:T(8,128)(2,1)S(1)}, bf16[32,16,128]{2,1,0:T(8,128)(2,1)S(1)}, u32[]{:S(2)}, u32[]{:S(2)}) collective-permute-start(bf16[32,16,128]{2,1,0:T(8,128)(2,1)S(1)} %get-tuple-element.42), channel_id=1, source_target_pairs={{2,0},{3,1},{4,2},{5,3},{6,4},{7,5},{0,6},{1,7},{10,8},{11,9},{12,... | collective-permute-start | bytes 393224 | tf_op jit(solution)/shard_map/ppermute | solution.py:147
  135.8 5.5 %collective-permute-start.28 = (bf16[16,16,128]{2,1,0:T(8,128)(2,1)S(1)}, bf16[16,16,128]{2,1,0:T(8,128)(2,1)S(1)}, u32[]{:S(2)}, u32[]{:S(2)}) collective-permute-start(bf16[16,16,128]{2,1,0:T(8,128)(2,1)S(1)} %get-tuple-element.39), channel_id=1, source_target_pairs={{6,0},{7,1},{0,2},{1,3},{2,4},{3,5},{4,6},{5,7},{14,8},{15,9},{8,1... | collective-permute-start | bytes 196616 | tf_op jit(solution)/shard_map/ppermute | solution.py:147
  135.8 5.5 %collective-permute-start.30 = (bf16[16,16,128]{2,1,0:T(8,128)(2,1)S(1)}, bf16[16,16,128]{2,1,0:T(8,128)(2,1)S(1)}, u32[]{:S(2)}, u32[]{:S(2)}) collective-permute-start(bf16[16,16,128]{2,1,0:T(8,128)(2,1)S(1)} %get-tuple-element.40), channel_id=1, source_target_pairs={{2,0},{3,1},{4,2},{5,3},{6,4},{7,5},{0,6},{1,7},{10,8},{11,9},{12,... | collective-permute-start | bytes 196616 | tf_op jit(solution)/shard_map/ppermute | solution.py:147
  141.3 5.5 %collective-permute-start.29 = (bf16[16,16,128]{2,1,0:T(8,128)(2,1)S(1)}, bf16[16,16,128]{2,1,0:T(8,128)(2,1)S(1)}, u32[]{:S(2)}, u32[]{:S(2)}) collective-permute-start(bf16[16,16,128]{2,1,0:T(8,128)(2,1)S(1)} %collective-permute-done.28), channel_id=1, source_target_pairs={{6,0},{7,1},{0,2},{1,3},{2,4},{3,5},{4,6},{5,7},{14,8},{15,9},{8,1... | collective-permute-start | bytes 196616 | tf_op jit(solution)/shard_map/ppermute | solution.py:147
  141.3 5.5 %collective-permute-start.31 = (bf16[16,16,128]{2,1,0:T(8,128)(2,1)S(1)}, bf16[16,16,128]{2,1,0:T(8,128)(2,1)S(1)}, u32[]{:S(2)}, u32[]{:S(2)}) collective-permute-start(bf16[16,16,128]{2,1,0:T(8,128)(2,1)S(1)} %collective-permute-done.30), channel_id=1, source_target_pairs={{2,0},{3,1},{4,2},{5,3},{6,4},{7,5},{0,6},{1,7},{10,8},{11,9},{12,... | collective-permute-start | bytes 196616 | tf_op jit(solution)/shard_map/ppermute | solution.py:147
  166.1 11.5 %collective-permute-start.33 = (bf16[128,16,128]{2,1,0:T(8,128)(2,1)S(1)}, bf16[128,16,128]{2,1,0:T(8,128)(2,1)S(1)}, u32[]{:S(2)}, u32[]{:S(2)}) collective-permute-start(bf16[128,16,128]{2,1,0:T(8,128)(2,1)S(1)} %bitcast.177), channel_id=1, source_target_pairs={{6,0},{7,1},{0,2},{1,3},{2,4},{3,5},{4,6},{5,7},{14,8},{15,9},{8,1... | collective-permute-start | bytes 1572872 | tf_op jit(solution)/shard_map/ppermute | solution.py:147
  166.2 20.2 %collective-permute-start.35 = (bf16[128,16,128]{2,1,0:T(8,128)(2,1)S(1)}, bf16[128,16,128]{2,1,0:T(8,128)(2,1)S(1)}, u32[]{:S(2)}, u32[]{:S(2)}) collective-permute-start(bf16[128,16,128]{2,1,0:T(8,128)(2,1)S(1)} %bitcast.178), channel_id=1, source_target_pairs={{2,0},{3,1},{4,2},{5,3},{6,4},{7,5},{0,6},{1,7},{10,8},{11,9},{12,... | collective-permute-start | bytes 1572872 | tf_op jit(solution)/shard_map/ppermute | solution.py:147
  169.4 19.8 %collective-permute-start.32 = (bf16[128,16,128]{2,1,0:T(8,128)(2,1)S(1)}, bf16[128,16,128]{2,1,0:T(8,128)(2,1)S(1)}, u32[]{:S(2)}, u32[]{:S(2)}) collective-permute-start(bf16[128,16,128]{2,1,0:T(8,128)(2,1)S(1)} %bitcast.179), channel_id=1, source_target_pairs={{0,1},{1,0},{2,3},{3,2},{4,5},{5,4},{6,7},{7,6},{8,9},{9,8},{10,11... | collective-permute-start | bytes 1572872 | tf_op jit(solution)/shard_map/ppermute | solution.py:150
  177.7 18.6 %collective-permute-start.34 = (bf16[128,16,128]{2,1,0:T(8,128)(2,1)S(1)}, bf16[128,16,128]{2,1,0:T(8,128)(2,1)S(1)}, u32[]{:S(2)}, u32[]{:S(2)}) collective-permute-start(bf16[128,16,128]{2,1,0:T(8,128)(2,1)S(1)} %collective-permute-done.33), channel_id=1, source_target_pairs={{0,1},{1,0},{2,3},{3,2},{4,5},{5,4},{6,7},{7,6},{8,9},{9,8},{10,11... | collective-permute-start | bytes 1572872 | tf_op jit(solution)/shard_map/ppermute | solution.py:150
  178.4 25.1 %all-to-all-start.3 = ((bf16[8,4,2,16,128]{4,3,1,2,0:T(8,128)(2,1)}), bf16[8,4,2,16,128]{4,3,1,2,0:T(8,128)(2,1)S(1)}, u32[]{:S(2)}, u32[]{:S(2)}) async-start(bf16[8,4,2,16,128]{4,3,1,2,0:T(8,128)(2,1)} %pad_maximum_fusion), calls=%async_computation.3 | async-start | bytes 524288 | tf_op jit(solution)/shard_map/all_to_all | solution.py:176
  185.4 10.4 %collective-permute-start.37 = (bf16[64,16,128]{2,1,0:T(8,128)(2,1)S(1)}, bf16[64,16,128]{2,1,0:T(8,128)(2,1)S(1)}, u32[]{:S(2)}, u32[]{:S(2)}) collective-permute-start(bf16[64,16,128]{2,1,0:T(8,128)(2,1)S(1)} %slice.174), channel_id=1, source_target_pairs={{6,0},{7,1},{0,2},{1,3},{2,4},{3,5},{4,6},{5,7},{14,8},{15,9},{8,1... | collective-permute-start | bytes 786440 | tf_op jit(solution)/shard_map/ppermute | solution.py:147
  186.4 9.4 %collective-permute-start.39 = (bf16[64,16,128]{2,1,0:T(8,128)(2,1)S(1)}, bf16[64,16,128]{2,1,0:T(8,128)(2,1)S(1)}, u32[]{:S(2)}, u32[]{:S(2)}) collective-permute-start(bf16[64,16,128]{2,1,0:T(8,128)(2,1)S(1)} %slice.175), channel_id=1, source_target_pairs={{2,0},{3,1},{4,2},{5,3},{6,4},{7,5},{0,6},{1,7},{10,8},{11,9},{12,... | collective-permute-start | bytes 786440 | tf_op jit(solution)/shard_map/ppermute | solution.py:147
  189.0 7.4 %collective-permute-start.36 = (bf16[128,16,128]{2,1,0:T(8,128)(2,1)S(1)}, bf16[128,16,128]{2,1,0:T(8,128)(2,1)S(1)}, u32[]{:S(2)}, u32[]{:S(2)}) collective-permute-start(bf16[128,16,128]{2,1,0:T(8,128)(2,1)S(1)} %collective-permute-done.35), channel_id=1, source_target_pairs={{0,1},{1,0},{2,3},{3,2},{4,5},{5,4},{6,7},{7,6},{8,9},{9,8},{10,11... | collective-permute-start | bytes 1572872 | tf_op jit(solution)/shard_map/ppermute | solution.py:150
  195.8 1.9 collective-permute-start.40
  201.7 2.2 %collective-permute-start.41 = (bf16[4,32,16,128]{3,2,1,0:T(8,128)(2,1)S(1)}, bf16[4,32,16,128]{3,2,1,0:T(8,128)(2,1)S(1)}, u32[]{:S(2)}, u32[]{:S(2)}) collective-permute-start(bf16[4,32,16,128]{3,2,1,0:T(8,128)(2,1)S(1)} %get-tuple-element.28), channel_id=1, source_target_pairs={{0,1},{1,0},{2,3},{3,2},{4,5},{5,4},{6,7},{7,6},{8,9},{9,8},{10,11... | collective-permute-start | bytes 1572872 | tf_op jit(solution)/shard_map/ppermute | solution.py:150
  204.1 6.7 %collective-permute-start.44 = (bf16[16,16,128]{2,1,0:T(8,128)(2,1)S(1)}, bf16[16,16,128]{2,1,0:T(8,128)(2,1)S(1)}, u32[]{:S(2)}, u32[]{:S(2)}) collective-permute-start(bf16[16,16,128]{2,1,0:T(8,128)(2,1)S(1)} %get-tuple-element.35), channel_id=1, source_target_pairs={{6,0},{7,1},{0,2},{1,3},{2,4},{3,5},{4,6},{5,7},{14,8},{15,9},{8,1... | collective-permute-start | bytes 196616 | tf_op jit(solution)/shard_map/ppermute | solution.py:147
  204.2 6.6 %collective-permute-start.46 = (bf16[16,16,128]{2,1,0:T(8,128)(2,1)S(1)}, bf16[16,16,128]{2,1,0:T(8,128)(2,1)S(1)}, u32[]{:S(2)}, u32[]{:S(2)}) collective-permute-start(bf16[16,16,128]{2,1,0:T(8,128)(2,1)S(1)} %get-tuple-element.36), channel_id=1, source_target_pairs={{2,0},{3,1},{4,2},{5,3},{6,4},{7,5},{0,6},{1,7},{10,8},{11,9},{12,... | collective-permute-start | bytes 196616 | tf_op jit(solution)/shard_map/ppermute | solution.py:147
  207.4 6.9 %collective-permute-start.42 = (bf16[32,16,128]{2,1,0:T(8,128)(2,1)S(1)}, bf16[32,16,128]{2,1,0:T(8,128)(2,1)S(1)}, u32[]{:S(2)}, u32[]{:S(2)}) collective-permute-start(bf16[32,16,128]{2,1,0:T(8,128)(2,1)S(1)} %get-tuple-element.37), channel_id=1, source_target_pairs={{6,0},{7,1},{0,2},{1,3},{2,4},{3,5},{4,6},{5,7},{14,8},{15,9},{8,1... | collective-permute-start | bytes 393224 | tf_op jit(solution)/shard_map/ppermute | solution.py:147
  207.5 6.8 %collective-permute-start.43 = (bf16[32,16,128]{2,1,0:T(8,128)(2,1)S(1)}, bf16[32,16,128]{2,1,0:T(8,128)(2,1)S(1)}, u32[]{:S(2)}, u32[]{:S(2)}) collective-permute-start(bf16[32,16,128]{2,1,0:T(8,128)(2,1)S(1)} %get-tuple-element.38), channel_id=1, source_target_pairs={{2,0},{3,1},{4,2},{5,3},{6,4},{7,5},{0,6},{1,7},{10,8},{11,9},{12,... | collective-permute-start | bytes 393224 | tf_op jit(solution)/shard_map/ppermute | solution.py:147
  210.7 5.5 %collective-permute-start.45 = (bf16[16,16,128]{2,1,0:T(8,128)(2,1)S(1)}, bf16[16,16,128]{2,1,0:T(8,128)(2,1)S(1)}, u32[]{:S(2)}, u32[]{:S(2)}) collective-permute-start(bf16[16,16,128]{2,1,0:T(8,128)(2,1)S(1)} %collective-permute-done.44), channel_id=1, source_target_pairs={{6,0},{7,1},{0,2},{1,3},{2,4},{3,5},{4,6},{5,7},{14,8},{15,9},{8,1... | collective-permute-start | bytes 196616 | tf_op jit(solution)/shard_map/ppermute | solution.py:147
  210.8 5.5 %collective-permute-start.47 = (bf16[16,16,128]{2,1,0:T(8,128)(2,1)S(1)}, bf16[16,16,128]{2,1,0:T(8,128)(2,1)S(1)}, u32[]{:S(2)}, u32[]{:S(2)}) collective-permute-start(bf16[16,16,128]{2,1,0:T(8,128)(2,1)S(1)} %collective-permute-done.46), channel_id=1, source_target_pairs={{2,0},{3,1},{4,2},{5,3},{6,4},{7,5},{0,6},{1,7},{10,8},{11,9},{12,... | collective-permute-start | bytes 196616 | tf_op jit(solution)/shard_map/ppermute | solution.py:147
  (5 other events, 32.3 us)

commit v5 on v4

--- a/solution.py
+++ b/solution.py
@@ -8,6 +8,7 @@
 
 UNROLL = 32
 CORES = 2
+KEPT = 352
 
 
 def tile_sums(fetched, values, rows_of, slots_of, scalars, row_blocks, whole_blocks):
@@ -17,7 +18,6 @@
     per = row_blocks // replicas
 
     def body(scalar, rows, slot, fetched, vals, peer, mine, acc):
-        count = scalar[0]
         chip = scalar[1]
         core = scalar[2]
 
@@ -27,20 +27,24 @@
 
         lax.fori_loop(0, row_blocks + 1, clear, 0)
 
-        def group(step, carry):
-            products = []
-            for unit in range(UNROLL):
-                t = step * UNROLL + unit
-                block = fetched[:, slot[t]].reshape(tile, width)
-                target = jnp.where(t < count, rows[t], row_blocks)
-                products.append(
-                    (target, jnp.dot(vals[t], block, preferred_element_type=jnp.float32))
-                )
-            for target, product in products:
-                acc[target] += product
-            return carry
-
-        lax.fori_loop(0, (count + UNROLL - 1) // UNROLL, group, 0)
+        def groups(first, count):
+            def group(step, carry):
+                products = []
+                for unit in range(UNROLL):
+                    t = step * UNROLL + unit
+                    block = fetched[:, slot[t]].reshape(tile, width)
+                    target = jnp.where(t < count, rows[t], row_blocks)
+                    products.append(
+                        (target, jnp.dot(vals[t], block, preferred_element_type=jnp.float32))
+                    )
+                for target, product in products:
+                    acc[target] += product
+                return carry
+
+            lax.fori_loop(first // UNROLL, (count + UNROLL - 1) // UNROLL, group, 0)
+
+        groups(0, jnp.minimum(scalar[0], KEPT))
+        groups(KEPT, scalar[-1 + scalar.shape[0]])
 
         for hops in range(chips):
             for out, from_core in ((peer, 1 - core), (mine, core)):
@@ -74,25 +78,40 @@
     )
 
 
-def load_live(values, scalars, sent, replicas):
-    def body(scalar, values, sent, live, fetched, semaphore):
-        groups = (scalar[0] + UNROLL - 1) // UNROLL
-
-        def copy(step):
-            part = pl.ds(step * UNROLL, UNROLL)
-            return pltpu.make_async_copy(values.at[part], live.at[part], semaphore.at[step])
-
-        def start(step, carry):
-            copy(step).start()
-            return carry
-
-        def wait(step, carry):
-            copy(step).wait()
-            return carry
-
-        lax.fori_loop(0, groups, start, 0)
+def load_live(values, tail, scalars, sent, replicas):
+    def body(scalar, values, tail, sent, live, fetched, semaphore):
+        own = (jnp.minimum(scalar[0], KEPT) + UNROLL - 1) // UNROLL
+        kept = KEPT // UNROLL
+        end = (scalar[-1 + scalar.shape[0]] + UNROLL - 1) // UNROLL
+
+        def copy(source, step, skipped):
+            return pltpu.make_async_copy(
+                source.at[pl.ds((step - skipped) * UNROLL, UNROLL)],
+                live.at[pl.ds(step * UNROLL, UNROLL)],
+                semaphore.at[step],
+            )
+
+        def start_own(step, carry):
+            copy(values, step, 0).start()
+            return carry
+
+        def start_tail(step, carry):
+            copy(tail, step, kept).start()
+            return carry
+
+        def wait_own(step, carry):
+            copy(values, step, 0).wait()
+            return carry
+
+        def wait_tail(step, carry):
+            copy(tail, step, kept).wait()
+            return carry
+
+        lax.fori_loop(0, own, start_own, 0)
+        lax.fori_loop(kept, end, start_tail, 0)
         fetched[pl.ds(scalar[3], 1)] = sent[...][None]
-        lax.fori_loop(0, groups, wait, 0)
+        lax.fori_loop(0, own, wait_own, 0)
+        lax.fori_loop(kept, end, wait_tail, 0)
 
     return pl.pallas_call(
         body,
@@ -102,6 +121,7 @@
         ),
         in_specs=[
             pl.BlockSpec(memory_space=pltpu.SMEM),
+            pl.BlockSpec(memory_space=pltpu.HBM),
             pl.BlockSpec(memory_space=pltpu.HBM),
             pl.BlockSpec(memory_space=pltpu.VMEM),
         ],
@@ -115,6 +135,7 @@
     )(
         scalars,
         pltpu.with_memory_space_constraint(values, pltpu.HBM),
+        pltpu.with_memory_space_constraint(tail, pltpu.HBM),
         pltpu.with_memory_space_constraint(sent, pltpu.VMEM),
     )
 
@@ -140,7 +161,6 @@
         ((chip + hops) % chips * CORES + core, (chip + hops) % chips * CORES + 1 - core)
         for hops in range(chips)
     ]
-    scalars = jnp.stack([tile_counts[0, 0], chip, core, *sum(places, ())]).astype(jnp.int32)
 
     def along(x, hops):
         step = CORES * hops
@@ -149,10 +169,19 @@
     def partner(x):
         return lax.ppermute(x, "rep", [(i, i ^ 1) for i in range(replicas)])
 
+    count = tile_counts[0, 0]
+    tail = partner(values[KEPT:])
+    given = jnp.concatenate([rows_of[KEPT:], slots_of[KEPT:], tile_counts[0]])
+    taken = partner(given)
+    past = values.shape[0] - KEPT
+    rows_of = jnp.concatenate([rows_of[:KEPT], taken[:past]])
+    slots_of = jnp.concatenate([slots_of[:KEPT], taken[past : 2 * past]])
+    scalars = jnp.stack([count, chip, core, *sum(places, ()), taken[2 * past]]).astype(jnp.int32)
+
     def gather(sent):
         half = sent.shape[0] // 2
         before, after, other = along(sent, -1), along(sent, 1), partner(sent)
-        live, fetched = load_live(values, scalars, sent, replicas)
+        live, fetched = load_live(values, tail, scalars, sent, replicas)
         first, second = along(before[:half], -1), along(after[half:], 1)
         crossed = [partner(before), partner(after)]
         crossed += [partner(first), partner(second)]
@@ -179,14 +208,9 @@
 
     def reduce(peer, mine):
         sums = mine + partner(peer).astype(jnp.float32)
-        sent = [sums[hops].astype(jnp.bfloat16) for hops in range(chips)]
-        half = row_blocks // 2
-        low, high = along(sent[2][:half], -1), along(sent[2][half:], 1)
-        parts = [along(sent[1], -1), along(sent[3], 1)]
-        parts.append(jnp.concatenate([along(low, -1), along(high, 1)], 0))
         total = sums[0]
-        for part in parts:
-            total = total + part.astype(jnp.float32)
+        for hops in range(1, chips):
+            total = total + along(sums[hops].astype(jnp.bfloat16), -hops).astype(jnp.float32)
         return total
 
     served = lax.all_to_all(wanted, "rows", split_axis=0, concat_axis=0, tiled=True)

time: 218 us -> 217 us (level)
  starting transfers between devices: 65.4 us -> 51.2 us
  local copies, waits for them, and re-layouts: 6.52 us -> 14.9 us
  waiting for transfers between devices: 69 us -> 75.3 us
  blocking collectives: 48.2 us -> 46 us
    ppermute x30 -> x21, starting transfers between devices: 49.5 us -> 34.9 us  [along(): lax.ppermute(x, 'rep', [((i + step) % replicas, i) for i in range(replica...]
    slice x3 -> x7, local copies, waits for them, and re-layouts: 0.03 us -> 7.79 us  [the longest x1 6.98 us: on_device(): tail = partner(values[KEPT:])]
    ppermute x30 -> x21, waiting for transfers between devices: 56.1 us -> 63.5 us  [along(): lax.ppermute(x, 'rep', [((i + step) % replicas, i) for i in range(replica...]
    ppermute x18 -> x20, waiting for transfers between devices: 6.26 us -> 5.27 us  [partner(): return lax.ppermute(x, 'rep', [(i, i ^ 1) for i in range(replicas)])]
    ppermute x18 -> x20, starting transfers between devices: 4.35 us -> 4.73 us  [partner(): return lax.ppermute(x, 'rep', [(i, i ^ 1) for i in range(replicas)])]
  transfers between devices with their start and end apart: 50 -> 43, of which waited for: 22 -> 21; matrix products, arithmetic and copies ran while one was open for 2% -> 4% of each run, Pallas kernels for 7% -> 7%
where the time goes in v5:
time: 217 us; the launch traced here: 216 us
  waiting for transfers between devices  75.3 us (35%)
  starting transfers between devices  51.2 us (24%)
  blocking collectives  46 us (21%)
  Pallas kernels  22.2 us (10%)
  local copies, waits for them, and re-layouts  14.9 us (7%)
  other arithmetic  2.54 us (1%)
  matrix products  2.44 us (1%)
    ppermute x21, waiting for transfers between devices, along(): lax.ppermute(x, 'rep', [((i + step) % replicas, i) for i in range(replica...  63.5 us
    all_to_all x3, blocking collectives, step(): lax.all_to_all(terms[-1][served], 'rows', split_axis=0, concat_axis=0, ti...  46 us
    ppermute x21, starting transfers between devices, along(): lax.ppermute(x, 'rep', [((i + step) % replicas, i) for i in range(replica...  34.9 us
    pallas_call x3, Pallas kernels, tile_sums(): pl.pallas_call(body, out_shape=(pltpu.VMEM(shape, jnp.bfloat16), pltpu.VM...  11.7 us
    pallas_call x3, Pallas kernels, load_live(): pl.pallas_call(body, out_shape=(pltpu.VMEM(values.shape, values.dtype), p...  10.5 us
    all_to_all x1, starting transfers between devices, on_device(): lax.all_to_all(wanted, 'rows', split_axis=0, concat_axis=0, tiled=True)  8.16 us
    slice x1, local copies, waits for them, and re-layouts, on_device(): tail = partner(values[KEPT:])  6.98 us
    all_to_all x1, waiting for transfers between devices, on_device(): lax.all_to_all(wanted, 'rows', split_axis=0, concat_axis=0, tiled=True)  6.58 us
  transfers between devices with their start and end apart: 43, of which 21 were waited for; matrix products, arithmetic and copies ran while one was open for 4% of the time, Pallas kernels for 7%

profile of v5, /device:TPU:0, one launch (start us, length us, event | category | flops | bytes accessed | tf_op | source)
XLA Modules:
  0.0 216.0 jit_solution(13830292503512752928)
XLA Ops:
  0.0 7.0 %slice_bitcast_fusion = bf16[160,128,128]{2,1,0:T(8,128)(2,1)} fusion(bf16[1,1,512,128,128]{4,3,2,1,0:T(8,128)(2,1)} %param.8), kind=kLoop, calls=%fused_computation.3 | loop fusion | bytes 10485760 | tf_op jit(solution)/shard_map/slice | solution.py:173
  7.7 8.2 %all-to-all-start = ((s32[16,1,8]{2,1,0:T(1,128)}), s32[16,1,8]{2,1,0:T(1,128)S(1)}, u32[]{:S(2)}, u32[]{:S(2)}) async-start(s32[16,1,8]{2,1,0:T(1,128)} %copy.20), calls=%async_computation | async-start | bytes 16384 | tf_op jit(solution)/shard_map/all_to_all | solution.py:216
  15.8 0.9 constant_dynamic-slice_fusion
  16.8 6.6 %all-to-all-done = s32[16,1,8]{2,1,0:T(1,128)S(1)} async-done(((s32[16,1,8]{2,1,0:T(1,128)}), s32[16,1,8]{2,1,0:T(1,128)S(1)}, u32[]{:S(2)}, u32[]{:S(2)}) %all-to-all-start) | async-done | bytes 544 | tf_op jit(solution)/shard_map/all_to_all | solution.py:216
  24.3 13.7 %all_to_all.32 = bf16[16,8,16,128]{3,2,1,0:T(8,128)(2,1)S(1)} all-to-all(bf16[16,8,16,128]{3,2,1,0:T(8,128)(2,1)S(1)} %bitcast.187), channel_id=1, replica_groups=mesh['rows'=16,'rep'=8] {'rows'}, dimensions={0} | all-to-all | bytes 1048576 | tf_op jit(solution)/shard_map/all_to_all | solution.py:225
  38.0 1.5 collective-permute-start.3
  39.5 1.7 collective-permute-start.5
  42.8 7.5 %collective-permute-done.3 = bf16[128,16,128]{2,1,0:T(8,128)(2,1)S(1)} collective-permute-done((bf16[128,16,128]{2,1,0:T(8,128)(2,1)S(1)}, bf16[128,16,128]{2,1,0:T(8,128)(2,1)S(1)}, u32[]{:S(2)}, u32[]{:S(2)}) %collective-permute-start.3) | collective-permute-done | bytes 524320 | tf_op jit(solution)/shard_map/ppermute | solution.py:167
  50.3 1.3 collective-permute-start.7
  52.3 2.0 collective-permute-start.9
  55.7 2.2 %collective-permute-done.7 = bf16[64,16,128]{2,1,0:T(8,128)(2,1)S(1)} collective-permute-done((bf16[64,16,128]{2,1,0:T(8,128)(2,1)S(1)}, bf16[64,16,128]{2,1,0:T(8,128)(2,1)S(1)}, u32[]{:S(2)}, u32[]{:S(2)}) %collective-permute-start.7) | collective-permute-done | bytes 262176 | tf_op jit(solution)/shard_map/ppermute | solution.py:167
  57.9 1.0 collective-permute-done.9
  59.4 3.5 %load_live.3 = (bf16[512,128,128]{2,1,0:T(8,128)(2,1)S(1)}, bf16[8,128,16,128]{3,2,1,0:T(8,128)(2,1)S(1)}) custom-call(s32[12]{0:T(128)S(1)} %stack.52.scalar, bf16[512,128,128]{2,1,0:T(8,128)(2,1)} %bitcast.182, bf16[160,128,128]{2,1,0:T(8,128)(2,1)} %collective-permute-done.1.tail, bf16[128,16,128]{2,1,0:T(8,128)(2,1)S(1)} %bitcast.173), custom_call_target="tpu_custom_call" | custom-call | tf_op jit(solution)/shard_map/load_live/pallas_call | solution.py:116
  63.6 3.9 %tile_sums.3 = (bf16[4,32,16,128]{3,2,1,0:T(8,128)(2,1)S(1)}, f32[4,32,16,128]{3,2,1,0:T(8,128)S(1)}) custom-call(s32[12]{0:T(128)S(1)} %stack.52.scalar, s32[512]{0:T(512)S(1)} %get-tuple-element.48.rows, s32[512]{0:T(512)S(1)} %get-tuple-element.49.slot, bf16[8,128,16,128]{3,2,1,0:T(8,128)(2,1)S(1)} %bitcast_dynamic-update-slice_fusion.23.fetched, ...), custom_call_target="tpu_custom_call" | custom-call | tf_op jit(solution)/shard_map/tile_sums/pallas_call | solution.py:61
  67.5 0.9 collective-permute-start.11
  68.4 1.5 collective-permute-done.11
  70.2 5.4 %collective-permute-start.13 = (bf16[32,16,128]{2,1,0:T(8,128)(2,1)S(1)}, bf16[32,16,128]{2,1,0:T(8,128)(2,1)S(1)}, u32[]{:S(2)}, u32[]{:S(2)}) collective-permute-start(bf16[32,16,128]{2,1,0:T(8,128)(2,1)S(1)} %get-tuple-element.43), channel_id=1, source_target_pairs={{4,0},{5,1},{6,2},{7,3},{0,4},{1,5},{2,6},{3,7},{12,8},{13,9},{14,... | collective-permute-start | bytes 393224 | tf_op jit(solution)/shard_map/ppermute | solution.py:167
  75.6 2.6 %collective-permute-done.12 = bf16[32,16,128]{2,1,0:T(8,128)(2,1)S(1)} collective-permute-done((bf16[32,16,128]{2,1,0:T(8,128)(2,1)S(1)}, bf16[32,16,128]{2,1,0:T(8,128)(2,1)S(1)}, u32[]{:S(2)}, u32[]{:S(2)}) %collective-permute-start.12) | collective-permute-done | bytes 131104 | tf_op jit(solution)/shard_map/ppermute | solution.py:167
  78.2 4.0 %collective-permute-done.13 = bf16[32,16,128]{2,1,0:T(8,128)(2,1)S(1)} collective-permute-done((bf16[32,16,128]{2,1,0:T(8,128)(2,1)S(1)}, bf16[32,16,128]{2,1,0:T(8,128)(2,1)S(1)}, u32[]{:S(2)}, u32[]{:S(2)}) %collective-permute-start.13) | collective-permute-done | bytes 131104 | tf_op jit(solution)/shard_map/ppermute | solution.py:167
  83.0 16.8 %all_to_all.33 = bf16[16,8,16,128]{3,2,1,0:T(8,128)(2,1)S(1)} all-to-all(bf16[16,8,16,128]{3,2,1,0:T(8,128)(2,1)S(1)} %bitcast.189), channel_id=1, replica_groups=mesh['rows'=16,'rep'=8] {'rows'}, dimensions={0} | all-to-all | bytes 1048576 | tf_op jit(solution)/shard_map/all_to_all | solution.py:225
  100.2 2.8 %collective-permute-start.18 = (bf16[128,16,128]{2,1,0:T(8,128)(2,1)S(1)}, bf16[128,16,128]{2,1,0:T(8,128)(2,1)S(1)}, u32[]{:S(2)}, u32[]{:S(2)}) collective-permute-start(bf16[128,16,128]{2,1,0:T(8,128)(2,1)S(1)} %bitcast.179), channel_id=1, source_target_pairs={{2,0},{3,1},{4,2},{5,3},{6,4},{7,5},{0,6},{1,7},{10,8},{11,9},{12,... | collective-permute-start | bytes 1572872 | tf_op jit(solution)/shard_map/ppermute | solution.py:167
  103.0 10.2 %collective-permute-done.16 = bf16[128,16,128]{2,1,0:T(8,128)(2,1)S(1)} collective-permute-done((bf16[128,16,128]{2,1,0:T(8,128)(2,1)S(1)}, bf16[128,16,128]{2,1,0:T(8,128)(2,1)S(1)}, u32[]{:S(2)}, u32[]{:S(2)}) %collective-permute-start.16) | collective-permute-done | bytes 524320 | tf_op jit(solution)/shard_map/ppermute | solution.py:167
  113.2 3.5 %load_live.4 = (bf16[512,128,128]{2,1,0:T(8,128)(2,1)S(1)}, bf16[8,128,16,128]{3,2,1,0:T(8,128)(2,1)S(1)}) custom-call(s32[12]{0:T(128)S(1)} %stack.52.scalar, bf16[512,128,128]{2,1,0:T(8,128)(2,1)} %bitcast.183, bf16[160,128,128]{2,1,0:T(8,128)(2,1)} %collective-permute-done.1.tail, bf16[128,16,128]{2,1,0:T(8,128)(2,1)S(1)} %bitcast.181), custom_call_target="tpu_custom_call" | custom-call | tf_op jit(solution)/shard_map/load_live/pallas_call | solution.py:116
  116.9 3.3 %collective-permute-start.22 = (bf16[64,16,128]{2,1,0:T(8,128)(2,1)S(1)}, bf16[64,16,128]{2,1,0:T(8,128)(2,1)S(1)}, u32[]{:S(2)}, u32[]{:S(2)}) collective-permute-start(bf16[64,16,128]{2,1,0:T(8,128)(2,1)S(1)} %slice.172), channel_id=1, source_target_pairs={{2,0},{3,1},{4,2},{5,3},{6,4},{7,5},{0,6},{1,7},{10,8},{11,9},{12,... | collective-permute-start | bytes 786440 | tf_op jit(solution)/shard_map/ppermute | solution.py:167
  120.6 6.5 %collective-permute-done.20 = bf16[64,16,128]{2,1,0:T(8,128)(2,1)S(1)} collective-permute-done((bf16[64,16,128]{2,1,0:T(8,128)(2,1)S(1)}, bf16[64,16,128]{2,1,0:T(8,128)(2,1)S(1)}, u32[]{:S(2)}, u32[]{:S(2)}) %collective-permute-start.20) | collective-permute-done | bytes 262176 | tf_op jit(solution)/shard_map/ppermute | solution.py:167
  127.9 0.7 collective-permute-done.21
  129.0 3.9 %tile_sums.4 = (bf16[4,32,16,128]{3,2,1,0:T(8,128)(2,1)S(1)}, f32[4,32,16,128]{3,2,1,0:T(8,128)S(1)}) custom-call(s32[12]{0:T(128)S(1)} %stack.52.scalar, s32[512]{0:T(512)S(1)} %get-tuple-element.48.rows, s32[512]{0:T(512)S(1)} %get-tuple-element.49.slot, bf16[8,128,16,128]{3,2,1,0:T(8,128)(2,1)S(1)} %bitcast_dynamic-update-slice_fusion.19.fetched, ...), custom_call_target="tpu_custom_call" | custom-call | tf_op jit(solution)/shard_map/tile_sums/pallas_call | solution.py:61
  133.6 1.5 collective-permute-done.24
  135.4 4.6 %collective-permute-start.26 = (bf16[32,16,128]{2,1,0:T(8,128)(2,1)S(1)}, bf16[32,16,128]{2,1,0:T(8,128)(2,1)S(1)}, u32[]{:S(2)}, u32[]{:S(2)}) collective-permute-start(bf16[32,16,128]{2,1,0:T(8,128)(2,1)S(1)} %get-tuple-element.40), channel_id=1, source_target_pairs={{4,0},{5,1},{6,2},{7,3},{0,4},{1,5},{2,6},{3,7},{12,8},{13,9},{14,... | collective-permute-start | bytes 393224 | tf_op jit(solution)/shard_map/ppermute | solution.py:167
  140.0 2.6 %collective-permute-done.25 = bf16[32,16,128]{2,1,0:T(8,128)(2,1)S(1)} collective-permute-done((bf16[32,16,128]{2,1,0:T(8,128)(2,1)S(1)}, bf16[32,16,128]{2,1,0:T(8,128)(2,1)S(1)}, u32[]{:S(2)}, u32[]{:S(2)}) %collective-permute-start.25) | collective-permute-done | bytes 131104 | tf_op jit(solution)/shard_map/ppermute | solution.py:167
  142.6 4.0 %collective-permute-done.26 = bf16[32,16,128]{2,1,0:T(8,128)(2,1)S(1)} collective-permute-done((bf16[32,16,128]{2,1,0:T(8,128)(2,1)S(1)}, bf16[32,16,128]{2,1,0:T(8,128)(2,1)S(1)}, u32[]{:S(2)}, u32[]{:S(2)}) %collective-permute-start.26) | collective-permute-done | bytes 131104 | tf_op jit(solution)/shard_map/ppermute | solution.py:167
  146.6 1.0 fusion.12
  148.3 15.5 %all_to_all.34 = bf16[16,8,16,128]{3,2,1,0:T(8,128)(2,1)S(1)} all-to-all(bf16[16,8,16,128]{3,2,1,0:T(8,128)(2,1)S(1)} %bitcast.188), channel_id=1, replica_groups=mesh['rows'=16,'rep'=8] {'rows'}, dimensions={0} | all-to-all | bytes 1048576 | tf_op jit(solution)/shard_map/all_to_all | solution.py:225
  164.3 2.8 %collective-permute-start.31 = (bf16[128,16,128]{2,1,0:T(8,128)(2,1)S(1)}, bf16[128,16,128]{2,1,0:T(8,128)(2,1)S(1)}, u32[]{:S(2)}, u32[]{:S(2)}) collective-permute-start(bf16[128,16,128]{2,1,0:T(8,128)(2,1)S(1)} %bitcast.175), channel_id=1, source_target_pairs={{2,0},{3,1},{4,2},{5,3},{6,4},{7,5},{0,6},{1,7},{10,8},{11,9},{12,... | collective-permute-start | bytes 1572872 | tf_op jit(solution)/shard_map/ppermute | solution.py:167
  167.1 10.2 %collective-permute-done.29 = bf16[128,16,128]{2,1,0:T(8,128)(2,1)S(1)} collective-permute-done((bf16[128,16,128]{2,1,0:T(8,128)(2,1)S(1)}, bf16[128,16,128]{2,1,0:T(8,128)(2,1)S(1)}, u32[]{:S(2)}, u32[]{:S(2)}) %collective-permute-start.29) | collective-permute-done | bytes 524320 | tf_op jit(solution)/shard_map/ppermute | solution.py:167
  177.2 0.7 pad_maximum_fusion
  178.0 3.4 %all-to-all-start.3 = ((bf16[8,4,2,16,128]{4,3,1,2,0:T(8,128)(2,1)}), bf16[8,4,2,16,128]{4,3,1,2,0:T(8,128)(2,1)S(1)}, u32[]{:S(2)}, u32[]{:S(2)}) async-start(bf16[8,4,2,16,128]{4,3,1,2,0:T(8,128)(2,1)} %pad_maximum_fusion), calls=%async_computation.3 | async-start | bytes 524288 | tf_op jit(solution)/shard_map/all_to_all | solution.py:205
  181.4 3.5 %load_live.5 = (bf16[512,128,128]{2,1,0:T(8,128)(2,1)S(1)}, bf16[8,128,16,128]{3,2,1,0:T(8,128)(2,1)S(1)}) custom-call(s32[12]{0:T(128)S(1)} %stack.52.scalar, bf16[512,128,128]{2,1,0:T(8,128)(2,1)} %bitcast.184, bf16[160,128,128]{2,1,0:T(8,128)(2,1)} %collective-permute-done.1.tail, bf16[128,16,128]{2,1,0:T(8,128)(2,1)S(1)} %bitcast.177), custom_call_target="tpu_custom_call" | custom-call | tf_op jit(solution)/shard_map/load_live/pallas_call | solution.py:116
  184.9 1.0 collective-permute-start.33
  186.0 2.6 %collective-permute-start.35 = (bf16[64,16,128]{2,1,0:T(8,128)(2,1)S(1)}, bf16[64,16,128]{2,1,0:T(8,128)(2,1)S(1)}, u32[]{:S(2)}, u32[]{:S(2)}) collective-permute-start(bf16[64,16,128]{2,1,0:T(8,128)(2,1)S(1)} %slice.180), channel_id=1, source_target_pairs={{2,0},{3,1},{4,2},{5,3},{6,4},{7,5},{0,6},{1,7},{10,8},{11,9},{12,... | collective-permute-start | bytes 786440 | tf_op jit(solution)/shard_map/ppermute | solution.py:167
  188.9 6.5 %collective-permute-done.33 = bf16[64,16,128]{2,1,0:T(8,128)(2,1)S(1)} collective-permute-done((bf16[64,16,128]{2,1,0:T(8,128)(2,1)S(1)}, bf16[64,16,128]{2,1,0:T(8,128)(2,1)S(1)}, u32[]{:S(2)}, u32[]{:S(2)}) %collective-permute-start.33) | collective-permute-done | bytes 262176 | tf_op jit(solution)/shard_map/ppermute | solution.py:167
  196.2 0.7 collective-permute-done.34
  197.3 3.9 %tile_sums.5 = (bf16[4,32,16,128]{3,2,1,0:T(8,128)(2,1)S(1)}, f32[4,32,16,128]{3,2,1,0:T(8,128)S(1)}) custom-call(s32[12]{0:T(128)S(1)} %stack.52.scalar, s32[512]{0:T(512)S(1)} %get-tuple-element.48.rows, s32[512]{0:T(512)S(1)} %get-tuple-element.49.slot, bf16[8,128,16,128]{3,2,1,0:T(8,128)(2,1)S(1)} %bitcast_dynamic-update-slice_fusion.15.fetched, ...), custom_call_target="tpu_custom_call" | custom-call | tf_op jit(solution)/shard_map/tile_sums/pallas_call | solution.py:61
  201.9 1.1 fusion.17
  203.8 4.6 %collective-permute-start.39 = (bf16[32,16,128]{2,1,0:T(8,128)(2,1)S(1)}, bf16[32,16,128]{2,1,0:T(8,128)(2,1)S(1)}, u32[]{:S(2)}, u32[]{:S(2)}) collective-permute-start(bf16[32,16,128]{2,1,0:T(8,128)(2,1)S(1)} %get-tuple-element.37), channel_id=1, source_target_pairs={{4,0},{5,1},{6,2},{7,3},{0,4},{1,5},{2,6},{3,7},{12,8},{13,9},{14,... | collective-permute-start | bytes 393224 | tf_op jit(solution)/shard_map/ppermute | solution.py:167
  208.6 2.4 %collective-permute-done.38 = bf16[32,16,128]{2,1,0:T(8,128)(2,1)S(1)} collective-permute-done((bf16[32,16,128]{2,1,0:T(8,128)(2,1)S(1)}, bf16[32,16,128]{2,1,0:T(8,128)(2,1)S(1)}, u32[]{:S(2)}, u32[]{:S(2)}) %collective-permute-start.38) | collective-permute-done | bytes 131104 | tf_op jit(solution)/shard_map/ppermute | solution.py:167
  211.0 4.0 %collective-permute-done.39 = bf16[32,16,128]{2,1,0:T(8,128)(2,1)S(1)} collective-permute-done((bf16[32,16,128]{2,1,0:T(8,128)(2,1)S(1)}, bf16[32,16,128]{2,1,0:T(8,128)(2,1)S(1)}, u32[]{:S(2)}, u32[]{:S(2)}) %collective-permute-start.39) | collective-permute-done | bytes 131104 | tf_op jit(solution)/shard_map/ppermute | solution.py:167
  215.1 0.9 fusion
  (124 shorter events, 14.0 us)
Async XLA Ops:
  0.0 7.0 %copy-start.1 = (s32[1,16,8]{1,2,0:T(8,128)S(1)}, s32[1,16,8]{1,2,0:T(8,128)}, u32[]{:S(2)}) copy-start(s32[1,16,8]{1,2,0:T(8,128)} %param.12) | copy-start | bytes 1540
  0.0 41.9 %copy-start.3 = (s32[1,1,512]{2,1,0:T(1,128)S(1)}, s32[1,1,512]{2,1,0:T(1,128)}, u32[]{:S(2)}) copy-start(s32[1,1,512]{2,1,0:T(1,128)} %param.9) | copy-start | bytes 6148
  0.0 42.0 %copy-start.2 = (s32[1,1,512]{2,1,0:T(1,128)S(1)}, s32[1,1,512]{2,1,0:T(1,128)}, u32[]{:S(2)}) copy-start(s32[1,1,512]{2,1,0:T(1,128)} %param.10) | copy-start | bytes 6148
  7.0 51.9 %collective-permute-start.1 = (bf16[160,128,128]{2,1,0:T(8,128)(2,1)}, bf16[160,128,128]{2,1,0:T(8,128)(2,1)}, u32[]{:S(2)}, u32[]{:S(2)}) collective-permute-start(bf16[160,128,128]{2,1,0:T(8,128)(2,1)} %slice_bitcast_fusion), channel_id=1, source_target_pairs={{0,1},{1,0},{2,3},{3,2},{4,5},{5,4},{6,7},{7,6},{8,9},{9,8},{10,11... | collective-permute-start | bytes 15728648 | tf_op jit(solution)/shard_map/ppermute | solution.py:170
  7.7 15.7 %all-to-all-start = ((s32[16,1,8]{2,1,0:T(1,128)}), s32[16,1,8]{2,1,0:T(1,128)S(1)}, u32[]{:S(2)}, u32[]{:S(2)}) async-start(s32[16,1,8]{2,1,0:T(1,128)} %copy.20), calls=%async_computation | async-start | bytes 16384 | tf_op jit(solution)/shard_map/all_to_all | solution.py:216
  38.0 12.2 %collective-permute-start.3 = (bf16[128,16,128]{2,1,0:T(8,128)(2,1)S(1)}, bf16[128,16,128]{2,1,0:T(8,128)(2,1)S(1)}, u32[]{:S(2)}, u32[]{:S(2)}) collective-permute-start(bf16[128,16,128]{2,1,0:T(8,128)(2,1)S(1)} %bitcast.170), channel_id=1, source_target_pairs={{6,0},{7,1},{0,2},{1,3},{2,4},{3,5},{4,6},{5,7},{14,8},{15,9},{8,1... | collective-permute-start | bytes 1572872 | tf_op jit(solution)/shard_map/ppermute | solution.py:167
  39.5 12.1 %collective-permute-start.5 = (bf16[128,16,128]{2,1,0:T(8,128)(2,1)S(1)}, bf16[128,16,128]{2,1,0:T(8,128)(2,1)S(1)}, u32[]{:S(2)}, u32[]{:S(2)}) collective-permute-start(bf16[128,16,128]{2,1,0:T(8,128)(2,1)S(1)} %bitcast.171), channel_id=1, source_target_pairs={{2,0},{3,1},{4,2},{5,3},{6,4},{7,5},{0,6},{1,7},{10,8},{11,9},{12,... | collective-permute-start | bytes 1572872 | tf_op jit(solution)/shard_map/ppermute | solution.py:167
  42.2 12.2 %collective-permute-start = (s32[321]{0:T(512)S(1)}, s32[321]{0:T(512)S(1)}, u32[]{:S(2)}, u32[]{:S(2)}) collective-permute-start(s32[321]{0:T(512)S(1)} %pad_add_fusion), channel_id=1, source_target_pairs={{0,1},{1,0},{2,3},{3,2},{4,5},{5,4},{6,7},{7,6},{8,9},{9,8},{10,11... | collective-permute-start | bytes 3860 | tf_op jit(solution)/shard_map/ppermute | solution.py:170
  42.3 20.7 %collective-permute-start.2 = (bf16[128,16,128]{2,1,0:T(8,128)(2,1)S(1)}, bf16[128,16,128]{2,1,0:T(8,128)(2,1)S(1)}, u32[]{:S(2)}, u32[]{:S(2)}) collective-permute-start(bf16[128,16,128]{2,1,0:T(8,128)(2,1)S(1)} %bitcast.172), channel_id=1, source_target_pairs={{0,1},{1,0},{2,3},{3,2},{4,5},{5,4},{6,7},{7,6},{8,9},{9,8},{10,11... | collective-permute-start | bytes 1572872 | tf_op jit(solution)/shard_map/ppermute | solution.py:170
  50.3 7.7 %collective-permute-start.7 = (bf16[64,16,128]{2,1,0:T(8,128)(2,1)S(1)}, bf16[64,16,128]{2,1,0:T(8,128)(2,1)S(1)}, u32[]{:S(2)}, u32[]{:S(2)}) collective-permute-start(bf16[64,16,128]{2,1,0:T(8,128)(2,1)S(1)} %slice.165), channel_id=1, source_target_pairs={{6,0},{7,1},{0,2},{1,3},{2,4},{3,5},{4,6},{5,7},{14,8},{15,9},{8,1... | collective-permute-start | bytes 786440 | tf_op jit(solution)/shard_map/ppermute | solution.py:167
  52.3 6.6 %collective-permute-start.9 = (bf16[64,16,128]{2,1,0:T(8,128)(2,1)}, bf16[64,16,128]{2,1,0:T(8,128)(2,1)S(1)}, u32[]{:S(2)}, u32[]{:S(2)}) collective-permute-start(bf16[64,16,128]{2,1,0:T(8,128)(2,1)} %slice.166), channel_id=1, source_target_pairs={{2,0},{3,1},{4,2},{5,3},{6,4},{7,5},{0,6},{1,7},{10,8},{11,9},{12,... | collective-permute-start | bytes 786440 | tf_op jit(solution)/shard_map/ppermute | solution.py:167
  54.4 8.7 %collective-permute-start.4 = (bf16[128,16,128]{2,1,0:T(8,128)(2,1)S(1)}, bf16[128,16,128]{2,1,0:T(8,128)(2,1)S(1)}, u32[]{:S(2)}, u32[]{:S(2)}) collective-permute-start(bf16[128,16,128]{2,1,0:T(8,128)(2,1)S(1)} %collective-permute-done.3), channel_id=1, source_target_pairs={{0,1},{1,0},{2,3},{3,2},{4,5},{5,4},{6,7},{7,6},{8,9},{9,8},{10,11... | collective-permute-start | bytes 1572872 | tf_op jit(solution)/shard_map/ppermute | solution.py:170
  57.9 5.4 %collective-permute-start.6 = (bf16[128,16,128]{2,1,0:T(8,128)(2,1)S(1)}, bf16[128,16,128]{2,1,0:T(8,128)(2,1)S(1)}, u32[]{:S(2)}, u32[]{:S(2)}) collective-permute-start(bf16[128,16,128]{2,1,0:T(8,128)(2,1)S(1)} %collective-permute-done.5), channel_id=1, source_target_pairs={{0,1},{1,0},{2,3},{3,2},{4,5},{5,4},{6,7},{7,6},{8,9},{9,8},{10,11... | collective-permute-start | bytes 1572872 | tf_op jit(solution)/shard_map/ppermute | solution.py:170
  58.9 4.5 %collective-permute-start.8 = (bf16[64,16,128]{2,1,0:T(8,128)(2,1)S(1)}, bf16[64,16,128]{2,1,0:T(8,128)(2,1)S(1)}, u32[]{:S(2)}, u32[]{:S(2)}) collective-permute-start(bf16[64,16,128]{2,1,0:T(8,128)(2,1)S(1)} %collective-permute-done.7), channel_id=1, source_target_pairs={{0,1},{1,0},{2,3},{3,2},{4,5},{5,4},{6,7},{7,6},{8,9},{9,8},{10,11... | collective-permute-start | bytes 786440 | tf_op jit(solution)/shard_map/ppermute | solution.py:170
  58.9 4.6 %collective-permute-start.10 = (bf16[64,16,128]{2,1,0:T(8,128)(2,1)S(1)}, bf16[64,16,128]{2,1,0:T(8,128)(2,1)S(1)}, u32[]{:S(2)}, u32[]{:S(2)}) collective-permute-start(bf16[64,16,128]{2,1,0:T(8,128)(2,1)S(1)} %collective-permute-done.9), channel_id=1, source_target_pairs={{0,1},{1,0},{2,3},{3,2},{4,5},{5,4},{6,7},{7,6},{8,9},{9,8},{10,11... | collective-permute-start | bytes 786440 | tf_op jit(solution)/shard_map/ppermute | solution.py:170
  67.5 2.4 %collective-permute-start.11 = (bf16[4,32,16,128]{3,2,1,0:T(8,128)(2,1)S(1)}, bf16[4,32,16,128]{3,2,1,0:T(8,128)(2,1)S(1)}, u32[]{:S(2)}, u32[]{:S(2)}) collective-permute-start(bf16[4,32,16,128]{3,2,1,0:T(8,128)(2,1)S(1)} %get-tuple-element.20), channel_id=1, source_target_pairs={{0,1},{1,0},{2,3},{3,2},{4,5},{5,4},{6,7},{7,6},{8,9},{9,8},{10,11... | collective-permute-start | bytes 1572872 | tf_op jit(solution)/shard_map/ppermute | solution.py:170
  70.1 8.1 %collective-permute-start.12 = (bf16[32,16,128]{2,1,0:T(8,128)(2,1)S(1)}, bf16[32,16,128]{2,1,0:T(8,128)(2,1)S(1)}, u32[]{:S(2)}, u32[]{:S(2)}) collective-permute-start(bf16[32,16,128]{2,1,0:T(8,128)(2,1)S(1)} %get-tuple-element.41), channel_id=1, source_target_pairs={{6,0},{7,1},{0,2},{1,3},{2,4},{3,5},{4,6},{5,7},{14,8},{15,9},{8,1... | collective-permute-start | bytes 393224 | tf_op jit(solution)/shard_map/ppermute | solution.py:167
  70.2 12.0 %collective-permute-start.13 = (bf16[32,16,128]{2,1,0:T(8,128)(2,1)S(1)}, bf16[32,16,128]{2,1,0:T(8,128)(2,1)S(1)}, u32[]{:S(2)}, u32[]{:S(2)}) collective-permute-start(bf16[32,16,128]{2,1,0:T(8,128)(2,1)S(1)} %get-tuple-element.43), channel_id=1, source_target_pairs={{4,0},{5,1},{6,2},{7,3},{0,4},{1,5},{2,6},{3,7},{12,8},{13,9},{14,... | collective-permute-start | bytes 393224 | tf_op jit(solution)/shard_map/ppermute | solution.py:167
  75.6 6.6 %collective-permute-start.14 = (bf16[32,16,128]{2,1,0:T(8,128)(2,1)S(1)}, bf16[32,16,128]{2,1,0:T(8,128)(2,1)S(1)}, u32[]{:S(2)}, u32[]{:S(2)}) collective-permute-start(bf16[32,16,128]{2,1,0:T(8,128)(2,1)S(1)} %get-tuple-element.42), channel_id=1, source_target_pairs={{2,0},{3,1},{4,2},{5,3},{6,4},{7,5},{0,6},{1,7},{10,8},{11,9},{12,... | collective-permute-start | bytes 393224 | tf_op jit(solution)/shard_map/ppermute | solution.py:167
  99.8 13.4 %collective-permute-start.16 = (bf16[128,16,128]{2,1,0:T(8,128)(2,1)S(1)}, bf16[128,16,128]{2,1,0:T(8,128)(2,1)S(1)}, u32[]{:S(2)}, u32[]{:S(2)}) collective-permute-start(bf16[128,16,128]{2,1,0:T(8,128)(2,1)S(1)} %bitcast.178), channel_id=1, source_target_pairs={{6,0},{7,1},{0,2},{1,3},{2,4},{3,5},{4,6},{5,7},{14,8},{15,9},{8,1... | collective-permute-start | bytes 1572872 | tf_op jit(solution)/shard_map/ppermute | solution.py:167
  100.2 16.6 %collective-permute-start.18 = (bf16[128,16,128]{2,1,0:T(8,128)(2,1)S(1)}, bf16[128,16,128]{2,1,0:T(8,128)(2,1)S(1)}, u32[]{:S(2)}, u32[]{:S(2)}) collective-permute-start(bf16[128,16,128]{2,1,0:T(8,128)(2,1)S(1)} %bitcast.179), channel_id=1, source_target_pairs={{2,0},{3,1},{4,2},{5,3},{6,4},{7,5},{0,6},{1,7},{10,8},{11,9},{12,... | collective-permute-start | bytes 1572872 | tf_op jit(solution)/shard_map/ppermute | solution.py:167
  103.0 17.4 %collective-permute-start.15 = (bf16[128,16,128]{2,1,0:T(8,128)(2,1)S(1)}, bf16[128,16,128]{2,1,0:T(8,128)(2,1)S(1)}, u32[]{:S(2)}, u32[]{:S(2)}) collective-permute-start(bf16[128,16,128]{2,1,0:T(8,128)(2,1)S(1)} %bitcast.180), channel_id=1, source_target_pairs={{0,1},{1,0},{2,3},{3,2},{4,5},{5,4},{6,7},{7,6},{8,9},{9,8},{10,11... | collective-permute-start | bytes 1572872 | tf_op jit(solution)/shard_map/ppermute | solution.py:170
  113.2 14.4 %collective-permute-start.17 = (bf16[128,16,128]{2,1,0:T(8,128)(2,1)S(1)}, bf16[128,16,128]{2,1,0:T(8,128)(2,1)S(1)}, u32[]{:S(2)}, u32[]{:S(2)}) collective-permute-start(bf16[128,16,128]{2,1,0:T(8,128)(2,1)S(1)} %collective-permute-done.16), channel_id=1, source_target_pairs={{0,1},{1,0},{2,3},{3,2},{4,5},{5,4},{6,7},{7,6},{8,9},{9,8},{10,11... | collective-permute-start | bytes 1572872 | tf_op jit(solution)/shard_map/ppermute | solution.py:170
  116.7 10.3 %collective-permute-start.20 = (bf16[64,16,128]{2,1,0:T(8,128)(2,1)S(1)}, bf16[64,16,128]{2,1,0:T(8,128)(2,1)S(1)}, u32[]{:S(2)}, u32[]{:S(2)}) collective-permute-start(bf16[64,16,128]{2,1,0:T(8,128)(2,1)S(1)} %slice.171), channel_id=1, source_target_pairs={{6,0},{7,1},{0,2},{1,3},{2,4},{3,5},{4,6},{5,7},{14,8},{15,9},{8,1... | collective-permute-start | bytes 786440 | tf_op jit(solution)/shard_map/ppermute | solution.py:167
  116.9 10.2 %collective-permute-start.22 = (bf16[64,16,128]{2,1,0:T(8,128)(2,1)S(1)}, bf16[64,16,128]{2,1,0:T(8,128)(2,1)S(1)}, u32[]{:S(2)}, u32[]{:S(2)}) collective-permute-start(bf16[64,16,128]{2,1,0:T(8,128)(2,1)S(1)} %slice.172), channel_id=1, source_target_pairs={{2,0},{3,1},{4,2},{5,3},{6,4},{7,5},{0,6},{1,7},{10,8},{11,9},{12,... | collective-permute-start | bytes 786440 | tf_op jit(solution)/shard_map/ppermute | solution.py:167
  120.1 7.6 %collective-permute-start.19 = (bf16[128,16,128]{2,1,0:T(8,128)(2,1)S(1)}, bf16[128,16,128]{2,1,0:T(8,128)(2,1)S(1)}, u32[]{:S(2)}, u32[]{:S(2)}) collective-permute-start(bf16[128,16,128]{2,1,0:T(8,128)(2,1)S(1)} %collective-permute-done.18), channel_id=1, source_target_pairs={{0,1},{1,0},{2,3},{3,2},{4,5},{5,4},{6,7},{7,6},{8,9},{9,8},{10,11... | collective-permute-start | bytes 1572872 | tf_op jit(solution)/shard_map/ppermute | solution.py:170
  127.0 1.5 collective-permute-start.21
  127.1 1.9 collective-permute-start.23
  132.9 2.2 %collective-permute-start.24 = (bf16[4,32,16,128]{3,2,1,0:T(8,128)(2,1)S(1)}, bf16[4,32,16,128]{3,2,1,0:T(8,128)(2,1)S(1)}, u32[]{:S(2)}, u32[]{:S(2)}) collective-permute-start(bf16[4,32,16,128]{3,2,1,0:T(8,128)(2,1)S(1)} %get-tuple-element.24), channel_id=1, source_target_pairs={{0,1},{1,0},{2,3},{3,2},{4,5},{5,4},{6,7},{7,6},{8,9},{9,8},{10,11... | collective-permute-start | bytes 1572872 | tf_op jit(solution)/shard_map/ppermute | solution.py:170
  135.4 7.3 %collective-permute-start.25 = (bf16[32,16,128]{2,1,0:T(8,128)(2,1)S(1)}, bf16[32,16,128]{2,1,0:T(8,128)(2,1)S(1)}, u32[]{:S(2)}, u32[]{:S(2)}) collective-permute-start(bf16[32,16,128]{2,1,0:T(8,128)(2,1)S(1)} %get-tuple-element.38), channel_id=1, source_target_pairs={{6,0},{7,1},{0,2},{1,3},{2,4},{3,5},{4,6},{5,7},{14,8},{15,9},{8,1... | collective-permute-start | bytes 393224 | tf_op jit(solution)/shard_map/ppermute | solution.py:167
  135.4 11.2 %collective-permute-start.26 = (bf16[32,16,128]{2,1,0:T(8,128)(2,1)S(1)}, bf16[32,16,128]{2,1,0:T(8,128)(2,1)S(1)}, u32[]{:S(2)}, u32[]{:S(2)}) collective-permute-start(bf16[32,16,128]{2,1,0:T(8,128)(2,1)S(1)} %get-tuple-element.40), channel_id=1, source_target_pairs={{4,0},{5,1},{6,2},{7,3},{0,4},{1,5},{2,6},{3,7},{12,8},{13,9},{14,... | collective-permute-start | bytes 393224 | tf_op jit(solution)/shard_map/ppermute | solution.py:167
  140.0 6.6 %collective-permute-start.27 = (bf16[32,16,128]{2,1,0:T(8,128)(2,1)S(1)}, bf16[32,16,128]{2,1,0:T(8,128)(2,1)S(1)}, u32[]{:S(2)}, u32[]{:S(2)}) collective-permute-start(bf16[32,16,128]{2,1,0:T(8,128)(2,1)S(1)} %get-tuple-element.39), channel_id=1, source_target_pairs={{2,0},{3,1},{4,2},{5,3},{6,4},{7,5},{0,6},{1,7},{10,8},{11,9},{12,... | collective-permute-start | bytes 393224 | tf_op jit(solution)/shard_map/ppermute | solution.py:167
  163.8 13.4 %collective-permute-start.29 = (bf16[128,16,128]{2,1,0:T(8,128)(2,1)S(1)}, bf16[128,16,128]{2,1,0:T(8,128)(2,1)S(1)}, u32[]{:S(2)}, u32[]{:S(2)}) collective-permute-start(bf16[128,16,128]{2,1,0:T(8,128)(2,1)S(1)} %bitcast.174), channel_id=1, source_target_pairs={{6,0},{7,1},{0,2},{1,3},{2,4},{3,5},{4,6},{5,7},{14,8},{15,9},{8,1... | collective-permute-start | bytes 1572872 | tf_op jit(solution)/shard_map/ppermute | solution.py:167
  164.3 21.7 %collective-permute-start.31 = (bf16[128,16,128]{2,1,0:T(8,128)(2,1)S(1)}, bf16[128,16,128]{2,1,0:T(8,128)(2,1)S(1)}, u32[]{:S(2)}, u32[]{:S(2)}) collective-permute-start(bf16[128,16,128]{2,1,0:T(8,128)(2,1)S(1)} %bitcast.175), channel_id=1, source_target_pairs={{2,0},{3,1},{4,2},{5,3},{6,4},{7,5},{0,6},{1,7},{10,8},{11,9},{12,... | collective-permute-start | bytes 1572872 | tf_op jit(solution)/shard_map/ppermute | solution.py:167
  167.1 21.7 %collective-permute-start.28 = (bf16[128,16,128]{2,1,0:T(8,128)(2,1)S(1)}, bf16[128,16,128]{2,1,0:T(8,128)(2,1)S(1)}, u32[]{:S(2)}, u32[]{:S(2)}) collective-permute-start(bf16[128,16,128]{2,1,0:T(8,128)(2,1)S(1)} %bitcast.176), channel_id=1, source_target_pairs={{0,1},{1,0},{2,3},{3,2},{4,5},{5,4},{6,7},{7,6},{8,9},{9,8},{10,11... | collective-permute-start | bytes 1572872 | tf_op jit(solution)/shard_map/ppermute | solution.py:170
  177.2 18.6 %collective-permute-start.30 = (bf16[128,16,128]{2,1,0:T(8,128)(2,1)S(1)}, bf16[128,16,128]{2,1,0:T(8,128)(2,1)S(1)}, u32[]{:S(2)}, u32[]{:S(2)}) collective-permute-start(bf16[128,16,128]{2,1,0:T(8,128)(2,1)S(1)} %collective-permute-done.29), channel_id=1, source_target_pairs={{0,1},{1,0},{2,3},{3,2},{4,5},{5,4},{6,7},{7,6},{8,9},{9,8},{10,11... | collective-permute-start | bytes 1572872 | tf_op jit(solution)/shard_map/ppermute | solution.py:170
  178.0 25.1 %all-to-all-start.3 = ((bf16[8,4,2,16,128]{4,3,1,2,0:T(8,128)(2,1)}), bf16[8,4,2,16,128]{4,3,1,2,0:T(8,128)(2,1)S(1)}, u32[]{:S(2)}, u32[]{:S(2)}) async-start(bf16[8,4,2,16,128]{4,3,1,2,0:T(8,128)(2,1)} %pad_maximum_fusion), calls=%async_computation.3 | async-start | bytes 524288 | tf_op jit(solution)/shard_map/all_to_all | solution.py:205
  184.9 10.4 %collective-permute-start.33 = (bf16[64,16,128]{2,1,0:T(8,128)(2,1)S(1)}, bf16[64,16,128]{2,1,0:T(8,128)(2,1)S(1)}, u32[]{:S(2)}, u32[]{:S(2)}) collective-permute-start(bf16[64,16,128]{2,1,0:T(8,128)(2,1)S(1)} %slice.179), channel_id=1, source_target_pairs={{6,0},{7,1},{0,2},{1,3},{2,4},{3,5},{4,6},{5,7},{14,8},{15,9},{8,1... | collective-permute-start | bytes 786440 | tf_op jit(solution)/shard_map/ppermute | solution.py:167
  186.0 9.4 %collective-permute-start.35 = (bf16[64,16,128]{2,1,0:T(8,128)(2,1)S(1)}, bf16[64,16,128]{2,1,0:T(8,128)(2,1)S(1)}, u32[]{:S(2)}, u32[]{:S(2)}) collective-permute-start(bf16[64,16,128]{2,1,0:T(8,128)(2,1)S(1)} %slice.180), channel_id=1, source_target_pairs={{2,0},{3,1},{4,2},{5,3},{6,4},{7,5},{0,6},{1,7},{10,8},{11,9},{12,... | collective-permute-start | bytes 786440 | tf_op jit(solution)/shard_map/ppermute | solution.py:167
  188.6 7.4 %collective-permute-start.32 = (bf16[128,16,128]{2,1,0:T(8,128)(2,1)S(1)}, bf16[128,16,128]{2,1,0:T(8,128)(2,1)S(1)}, u32[]{:S(2)}, u32[]{:S(2)}) collective-permute-start(bf16[128,16,128]{2,1,0:T(8,128)(2,1)S(1)} %collective-permute-done.31), channel_id=1, source_target_pairs={{0,1},{1,0},{2,3},{3,2},{4,5},{5,4},{6,7},{7,6},{8,9},{9,8},{10,11... | collective-permute-start | bytes 1572872 | tf_op jit(solution)/shard_map/ppermute | solution.py:170
  195.4 1.5 collective-permute-start.34
  195.4 1.9 collective-permute-start.36
  197.3 4.6 %copy-start = (bf16[4,128,256]{2,1,0:T(8,128)(2,1)S(1)}, bf16[4,128,256]{2,1,0:T(8,128)(2,1)}, u32[]{:S(2)}) copy-start(bf16[4,128,256]{2,1,0:T(8,128)(2,1)} %param.13) | copy-start | bytes 786436
  201.2 2.2 %collective-permute-start.37 = (bf16[4,32,16,128]{3,2,1,0:T(8,128)(2,1)S(1)}, bf16[4,32,16,128]{3,2,1,0:T(8,128)(2,1)S(1)}, u32[]{:S(2)}, u32[]{:S(2)}) collective-permute-start(bf16[4,32,16,128]{3,2,1,0:T(8,128)(2,1)S(1)} %get-tuple-element.28), channel_id=1, source_target_pairs={{0,1},{1,0},{2,3},{3,2},{4,5},{5,4},{6,7},{7,6},{8,9},{9,8},{10,11... | collective-permute-start | bytes 1572872 | tf_op jit(solution)/shard_map/ppermute | solution.py:170
  203.7 7.3 %collective-permute-start.38 = (bf16[32,16,128]{2,1,0:T(8,128)(2,1)S(1)}, bf16[32,16,128]{2,1,0:T(8,128)(2,1)S(1)}, u32[]{:S(2)}, u32[]{:S(2)}) collective-permute-start(bf16[32,16,128]{2,1,0:T(8,128)(2,1)S(1)} %get-tuple-element.35), channel_id=1, source_target_pairs={{6,0},{7,1},{0,2},{1,3},{2,4},{3,5},{4,6},{5,7},{14,8},{15,9},{8,1... | collective-permute-start | bytes 393224 | tf_op jit(solution)/shard_map/ppermute | solution.py:167
  203.8 11.2 %collective-permute-start.39 = (bf16[32,16,128]{2,1,0:T(8,128)(2,1)S(1)}, bf16[32,16,128]{2,1,0:T(8,128)(2,1)S(1)}, u32[]{:S(2)}, u32[]{:S(2)}) collective-permute-start(bf16[32,16,128]{2,1,0:T(8,128)(2,1)S(1)} %get-tuple-element.37), channel_id=1, source_target_pairs={{4,0},{5,1},{6,2},{7,3},{0,4},{1,5},{2,6},{3,7},{12,8},{13,9},{14,... | collective-permute-start | bytes 393224 | tf_op jit(solution)/shard_map/ppermute | solution.py:167
  208.4 6.6 %collective-permute-start.40 = (bf16[32,16,128]{2,1,0:T(8,128)(2,1)S(1)}, bf16[32,16,128]{2,1,0:T(8,128)(2,1)S(1)}, u32[]{:S(2)}, u32[]{:S(2)}) collective-permute-start(bf16[32,16,128]{2,1,0:T(8,128)(2,1)S(1)} %get-tuple-element.36), channel_id=1, source_target_pairs={{2,0},{3,1},{4,2},{5,3},{6,4},{7,5},{0,6},{1,7},{10,8},{11,9},{12,... | collective-permute-start | bytes 393224 | tf_op jit(solution)/shard_map/ppermute | solution.py:167

commit v6 on v4

--- a/solution.py
+++ b/solution.py
@@ -179,20 +179,16 @@
 
     def reduce(peer, mine):
         sums = mine + partner(peer).astype(jnp.float32)
-        sent = [sums[hops].astype(jnp.bfloat16) for hops in range(chips)]
-        half = row_blocks // 2
-        low, high = along(sent[2][:half], -1), along(sent[2][half:], 1)
-        parts = [along(sent[1], -1), along(sent[3], 1)]
-        parts.append(jnp.concatenate([along(low, -1), along(high, 1)], 0))
         total = sums[0]
-        for part in parts:
-            total = total + part.astype(jnp.float32)
+        for hops in range(1, chips):
+            total = total + along(sums[hops].astype(jnp.bfloat16), -hops).astype(jnp.float32)
         return total
 
     served = lax.all_to_all(wanted, "rows", split_axis=0, concat_axis=0, tiled=True)
     blocks = features.reshape(row_blocks, tile, width)
     terms = [lax.dynamic_slice_in_dim(blocks, rank * sub, sub, 1)]
-    own = [lax.dynamic_slice_in_dim(features, rank * share_rows, share_rows, 0)]
+    shares = features.reshape(replicas, share_rows, width)
+    own = [lax.dynamic_index_in_dim(shares, rank, 0, keepdims=False, allow_negative_indices=False)]
 
     def step(degree):
         last = degree == degree_last

time: 218 us -> 217 us (level)
  starting transfers between devices: 65.4 us -> 50.2 us
  waiting for transfers between devices: 69 us -> 80.7 us
  blocking collectives: 48.2 us -> 50.5 us
    ppermute x30 -> x21, starting transfers between devices: 49.5 us -> 34.3 us  [along(): lax.ppermute(x, 'rep', [((i + step) % replicas, i) for i in range(replica...]
    ppermute x30 -> x21, waiting for transfers between devices: 56.1 us -> 67.9 us  [along(): lax.ppermute(x, 'rep', [((i + step) % replicas, i) for i in range(replica...]
    all_to_all x3, blocking collectives: 48.2 us -> 50.5 us  [step(): lax.all_to_all(terms[-1][served], 'rows', split_axis=0, concat_axis=0, ti...]
  transfers between devices with their start and end apart: 50 -> 41, of which waited for: 22 -> 22; matrix products, arithmetic and copies ran while one was open for 2% -> 2% of each run, Pallas kernels for 7% -> 7%
where the time goes in v6:
time: 217 us; the launch traced here: 216 us
  waiting for transfers between devices  80.7 us (37%)
  blocking collectives  50.5 us (23%)
  starting transfers between devices  50.2 us (23%)
  Pallas kernels  22.2 us (10%)
  local copies, waits for them, and re-layouts  6.51 us (3%)
  matrix products  2.44 us (1%)
  other arithmetic  2.39 us (1%)
    ppermute x21, waiting for transfers between devices, along(): lax.ppermute(x, 'rep', [((i + step) % replicas, i) for i in range(replica...  67.9 us
    all_to_all x3, blocking collectives, step(): lax.all_to_all(terms[-1][served], 'rows', split_axis=0, concat_axis=0, ti...  50.5 us
    ppermute x21, starting transfers between devices, along(): lax.ppermute(x, 'rep', [((i + step) % replicas, i) for i in range(replica...  34.3 us
    pallas_call x3, Pallas kernels, tile_sums(): pl.pallas_call(body, out_shape=(pltpu.VMEM(shape, jnp.bfloat16), pltpu.VM...  11.7 us
    pallas_call x3, Pallas kernels, load_live(): pl.pallas_call(body, out_shape=(pltpu.VMEM(values.shape, values.dtype), p...  10.5 us
    all_to_all x1, starting transfers between devices, on_device(): lax.all_to_all(wanted, 'rows', split_axis=0, concat_axis=0, tiled=True)  8.16 us
    all_to_all x1, waiting for transfers between devices, on_device(): lax.all_to_all(wanted, 'rows', split_axis=0, concat_axis=0, tiled=True)  6.58 us
    ppermute x18, waiting for transfers between devices, partner(): return lax.ppermute(x, 'rep', [(i, i ^ 1) for i in range(replicas)])  6.27 us
  transfers between devices with their start and end apart: 41, of which 22 were waited for; matrix products, arithmetic and copies ran while one was open for 2% of the time, Pallas kernels for 7%

profile of v6, /device:TPU:0, one launch (start us, length us, event | category | flops | bytes accessed | tf_op | source)
XLA Modules:
  0.0 216.2 jit_solution(1125302310143029791)
XLA Ops:
  0.0 1.4 copy.20
  1.4 8.2 %all-to-all-start = ((s32[16,1,8]{2,1,0:T(1,128)}), s32[16,1,8]{2,1,0:T(1,128)S(1)}, u32[]{:S(2)}, u32[]{:S(2)}) async-start(s32[16,1,8]{2,1,0:T(1,128)} %copy.20), calls=%async_computation | async-start | bytes 16384 | tf_op jit(solution)/shard_map/all_to_all | solution.py:187
  9.5 0.9 constant_dynamic-slice_fusion
  10.5 6.6 %all-to-all-done = s32[16,1,8]{2,1,0:T(1,128)S(1)} async-done(((s32[16,1,8]{2,1,0:T(1,128)}), s32[16,1,8]{2,1,0:T(1,128)S(1)}, u32[]{:S(2)}, u32[]{:S(2)}) %all-to-all-start) | async-done | bytes 544 | tf_op jit(solution)/shard_map/all_to_all | solution.py:187
  17.3 0.7 gather_fusion
  18.0 13.1 %all_to_all.32 = bf16[16,8,16,128]{3,2,1,0:T(8,128)(2,1)S(1)} all-to-all(bf16[16,8,16,128]{3,2,1,0:T(8,128)(2,1)S(1)} %bitcast.194), channel_id=1, replica_groups=mesh['rows'=16,'rep'=8] {'rows'}, dimensions={0} | all-to-all | bytes 1048576 | tf_op jit(solution)/shard_map/all_to_all | solution.py:197
  31.1 1.5 collective-permute-start.1
  32.6 1.7 collective-permute-start.3
  34.3 9.1 %collective-permute-done.1 = bf16[128,16,128]{2,1,0:T(8,128)(2,1)S(1)} collective-permute-done((bf16[128,16,128]{2,1,0:T(8,128)(2,1)S(1)}, bf16[128,16,128]{2,1,0:T(8,128)(2,1)S(1)}, u32[]{:S(2)}, u32[]{:S(2)}) %collective-permute-start.1) | collective-permute-done | bytes 524320 | tf_op jit(solution)/shard_map/ppermute | solution.py:147
  44.1 3.5 %load_live.3 = (bf16[512,128,128]{2,1,0:T(8,128)(2,1)S(1)}, bf16[8,128,16,128]{3,2,1,0:T(8,128)(2,1)S(1)}) custom-call(s32[11]{0:T(128)S(1)} %stack.52.scalar, bf16[512,128,128]{2,1,0:T(8,128)(2,1)} %bitcast.189, bf16[128,16,128]{2,1,0:T(8,128)(2,1)S(1)} %bitcast.174), custom_call_target="tpu_custom_call" | custom-call | tf_op jit(solution)/shard_map/load_live/pallas_call | solution.py:97
  47.8 3.3 %collective-permute-start.7 = (bf16[64,16,128]{2,1,0:T(8,128)(2,1)S(1)}, bf16[64,16,128]{2,1,0:T(8,128)(2,1)S(1)}, u32[]{:S(2)}, u32[]{:S(2)}) collective-permute-start(bf16[64,16,128]{2,1,0:T(8,128)(2,1)S(1)} %slice.114), channel_id=1, source_target_pairs={{2,0},{3,1},{4,2},{5,3},{6,4},{7,5},{0,6},{1,7},{10,8},{11,9},{12,... | collective-permute-start | bytes 786440 | tf_op jit(solution)/shard_map/ppermute | solution.py:147
  51.5 6.5 %collective-permute-done.5 = bf16[64,16,128]{2,1,0:T(8,128)(2,1)S(1)} collective-permute-done((bf16[64,16,128]{2,1,0:T(8,128)(2,1)S(1)}, bf16[64,16,128]{2,1,0:T(8,128)(2,1)S(1)}, u32[]{:S(2)}, u32[]{:S(2)}) %collective-permute-start.5) | collective-permute-done | bytes 262176 | tf_op jit(solution)/shard_map/ppermute | solution.py:147
  58.8 0.7 collective-permute-done.6
  60.0 3.9 %tile_sums.3 = (bf16[4,32,16,128]{3,2,1,0:T(8,128)(2,1)S(1)}, f32[4,32,16,128]{3,2,1,0:T(8,128)S(1)}) custom-call(s32[11]{0:T(128)S(1)} %stack.52.scalar, s32[512]{0:T(512)S(1)} %bitcast.183, s32[512]{0:T(512)S(1)} %bitcast.186, bf16[8,128,16,128]{3,2,1,0:T(8,128)(2,1)S(1)} %bitcast_dynamic-update-slice_fusion.23.fetched, ...), custom_call_target="tpu_custom_call" | custom-call | tf_op jit(solution)/shard_map/tile_sums/pallas_call | solution.py:57
  63.9 0.7 collective-permute-start.9
  64.6 1.5 collective-permute-done.9
  66.4 4.6 %collective-permute-start.11 = (bf16[32,16,128]{2,1,0:T(8,128)(2,1)S(1)}, bf16[32,16,128]{2,1,0:T(8,128)(2,1)S(1)}, u32[]{:S(2)}, u32[]{:S(2)}) collective-permute-start(bf16[32,16,128]{2,1,0:T(8,128)(2,1)S(1)} %get-tuple-element.43), channel_id=1, source_target_pairs={{4,0},{5,1},{6,2},{7,3},{0,4},{1,5},{2,6},{3,7},{12,8},{13,9},{14,... | collective-permute-start | bytes 393224 | tf_op jit(solution)/shard_map/ppermute | solution.py:147
  71.0 2.6 %collective-permute-done.10 = bf16[32,16,128]{2,1,0:T(8,128)(2,1)S(1)} collective-permute-done((bf16[32,16,128]{2,1,0:T(8,128)(2,1)S(1)}, bf16[32,16,128]{2,1,0:T(8,128)(2,1)S(1)}, u32[]{:S(2)}, u32[]{:S(2)}) %collective-permute-start.10) | collective-permute-done | bytes 131104 | tf_op jit(solution)/shard_map/ppermute | solution.py:147
  73.6 4.0 %collective-permute-done.11 = bf16[32,16,128]{2,1,0:T(8,128)(2,1)S(1)} collective-permute-done((bf16[32,16,128]{2,1,0:T(8,128)(2,1)S(1)}, bf16[32,16,128]{2,1,0:T(8,128)(2,1)S(1)}, u32[]{:S(2)}, u32[]{:S(2)}) %collective-permute-start.11) | collective-permute-done | bytes 131104 | tf_op jit(solution)/shard_map/ppermute | solution.py:147
  78.4 18.5 %all_to_all.33 = bf16[16,8,16,128]{3,2,1,0:T(8,128)(2,1)S(1)} all-to-all(bf16[16,8,16,128]{3,2,1,0:T(8,128)(2,1)S(1)} %bitcast.196), channel_id=1, replica_groups=mesh['rows'=16,'rep'=8] {'rows'}, dimensions={0} | all-to-all | bytes 1048576 | tf_op jit(solution)/shard_map/all_to_all | solution.py:197
  97.1 3.0 %collective-permute-start.16 = (bf16[128,16,128]{2,1,0:T(8,128)(2,1)S(1)}, bf16[128,16,128]{2,1,0:T(8,128)(2,1)S(1)}, u32[]{:S(2)}, u32[]{:S(2)}) collective-permute-start(bf16[128,16,128]{2,1,0:T(8,128)(2,1)S(1)} %bitcast.180), channel_id=1, source_target_pairs={{2,0},{3,1},{4,2},{5,3},{6,4},{7,5},{0,6},{1,7},{10,8},{11,9},{12,... | collective-permute-start | bytes 1572872 | tf_op jit(solution)/shard_map/ppermute | solution.py:147
  100.1 9.9 %collective-permute-done.14 = bf16[128,16,128]{2,1,0:T(8,128)(2,1)S(1)} collective-permute-done((bf16[128,16,128]{2,1,0:T(8,128)(2,1)S(1)}, bf16[128,16,128]{2,1,0:T(8,128)(2,1)S(1)}, u32[]{:S(2)}, u32[]{:S(2)}) %collective-permute-start.14) | collective-permute-done | bytes 524320 | tf_op jit(solution)/shard_map/ppermute | solution.py:147
  110.0 3.5 %load_live.4 = (bf16[512,128,128]{2,1,0:T(8,128)(2,1)S(1)}, bf16[8,128,16,128]{3,2,1,0:T(8,128)(2,1)S(1)}) custom-call(s32[11]{0:T(128)S(1)} %stack.52.scalar, bf16[512,128,128]{2,1,0:T(8,128)(2,1)} %bitcast.190, bf16[128,16,128]{2,1,0:T(8,128)(2,1)S(1)} %bitcast.182), custom_call_target="tpu_custom_call" | custom-call | tf_op jit(solution)/shard_map/load_live/pallas_call | solution.py:97
  113.7 3.3 %collective-permute-start.20 = (bf16[64,16,128]{2,1,0:T(8,128)(2,1)S(1)}, bf16[64,16,128]{2,1,0:T(8,128)(2,1)S(1)}, u32[]{:S(2)}, u32[]{:S(2)}) collective-permute-start(bf16[64,16,128]{2,1,0:T(8,128)(2,1)S(1)} %slice.120), channel_id=1, source_target_pairs={{2,0},{3,1},{4,2},{5,3},{6,4},{7,5},{0,6},{1,7},{10,8},{11,9},{12,... | collective-permute-start | bytes 786440 | tf_op jit(solution)/shard_map/ppermute | solution.py:147
  117.4 6.5 %collective-permute-done.18 = bf16[64,16,128]{2,1,0:T(8,128)(2,1)S(1)} collective-permute-done((bf16[64,16,128]{2,1,0:T(8,128)(2,1)S(1)}, bf16[64,16,128]{2,1,0:T(8,128)(2,1)S(1)}, u32[]{:S(2)}, u32[]{:S(2)}) %collective-permute-start.18) | collective-permute-done | bytes 262176 | tf_op jit(solution)/shard_map/ppermute | solution.py:147
  124.7 0.7 collective-permute-done.19
  125.8 3.9 %tile_sums.4 = (bf16[4,32,16,128]{3,2,1,0:T(8,128)(2,1)S(1)}, f32[4,32,16,128]{3,2,1,0:T(8,128)S(1)}) custom-call(s32[11]{0:T(128)S(1)} %stack.52.scalar, s32[512]{0:T(512)S(1)} %bitcast.184, s32[512]{0:T(512)S(1)} %bitcast.187, bf16[8,128,16,128]{3,2,1,0:T(8,128)(2,1)S(1)} %bitcast_dynamic-update-slice_fusion.19.fetched, ...), custom_call_target="tpu_custom_call" | custom-call | tf_op jit(solution)/shard_map/tile_sums/pallas_call | solution.py:57
  130.4 1.5 collective-permute-done.22
  132.4 4.6 %collective-permute-start.24 = (bf16[32,16,128]{2,1,0:T(8,128)(2,1)S(1)}, bf16[32,16,128]{2,1,0:T(8,128)(2,1)S(1)}, u32[]{:S(2)}, u32[]{:S(2)}) collective-permute-start(bf16[32,16,128]{2,1,0:T(8,128)(2,1)S(1)} %get-tuple-element.40), channel_id=1, source_target_pairs={{4,0},{5,1},{6,2},{7,3},{0,4},{1,5},{2,6},{3,7},{12,8},{13,9},{14,... | collective-permute-start | bytes 393224 | tf_op jit(solution)/shard_map/ppermute | solution.py:147
  137.0 2.6 %collective-permute-done.23 = bf16[32,16,128]{2,1,0:T(8,128)(2,1)S(1)} collective-permute-done((bf16[32,16,128]{2,1,0:T(8,128)(2,1)S(1)}, bf16[32,16,128]{2,1,0:T(8,128)(2,1)S(1)}, u32[]{:S(2)}, u32[]{:S(2)}) %collective-permute-start.23) | collective-permute-done | bytes 131104 | tf_op jit(solution)/shard_map/ppermute | solution.py:147
  139.6 4.0 %collective-permute-done.24 = bf16[32,16,128]{2,1,0:T(8,128)(2,1)S(1)} collective-permute-done((bf16[32,16,128]{2,1,0:T(8,128)(2,1)S(1)}, bf16[32,16,128]{2,1,0:T(8,128)(2,1)S(1)}, u32[]{:S(2)}, u32[]{:S(2)}) %collective-permute-start.24) | collective-permute-done | bytes 131104 | tf_op jit(solution)/shard_map/ppermute | solution.py:147
  143.6 1.0 fusion.12
  145.3 18.9 %all_to_all.34 = bf16[16,8,16,128]{3,2,1,0:T(8,128)(2,1)S(1)} all-to-all(bf16[16,8,16,128]{3,2,1,0:T(8,128)(2,1)S(1)} %bitcast.195), channel_id=1, replica_groups=mesh['rows'=16,'rep'=8] {'rows'}, dimensions={0} | all-to-all | bytes 1048576 | tf_op jit(solution)/shard_map/all_to_all | solution.py:197
  164.5 3.0 %collective-permute-start.29 = (bf16[128,16,128]{2,1,0:T(8,128)(2,1)S(1)}, bf16[128,16,128]{2,1,0:T(8,128)(2,1)S(1)}, u32[]{:S(2)}, u32[]{:S(2)}) collective-permute-start(bf16[128,16,128]{2,1,0:T(8,128)(2,1)S(1)} %bitcast.176), channel_id=1, source_target_pairs={{2,0},{3,1},{4,2},{5,3},{6,4},{7,5},{0,6},{1,7},{10,8},{11,9},{12,... | collective-permute-start | bytes 1572872 | tf_op jit(solution)/shard_map/ppermute | solution.py:147
  167.5 9.9 %collective-permute-done.27 = bf16[128,16,128]{2,1,0:T(8,128)(2,1)S(1)} collective-permute-done((bf16[128,16,128]{2,1,0:T(8,128)(2,1)S(1)}, bf16[128,16,128]{2,1,0:T(8,128)(2,1)S(1)}, u32[]{:S(2)}, u32[]{:S(2)}) %collective-permute-start.27) | collective-permute-done | bytes 524320 | tf_op jit(solution)/shard_map/ppermute | solution.py:147
  177.4 0.7 pad_maximum_fusion
  178.2 3.4 %all-to-all-start.3 = ((bf16[8,4,2,16,128]{4,3,1,2,0:T(8,128)(2,1)}), bf16[8,4,2,16,128]{4,3,1,2,0:T(8,128)(2,1)S(1)}, u32[]{:S(2)}, u32[]{:S(2)}) async-start(bf16[8,4,2,16,128]{4,3,1,2,0:T(8,128)(2,1)} %pad_maximum_fusion), calls=%async_computation.3 | async-start | bytes 524288 | tf_op jit(solution)/shard_map/all_to_all | solution.py:176
  181.6 3.5 %load_live.5 = (bf16[512,128,128]{2,1,0:T(8,128)(2,1)S(1)}, bf16[8,128,16,128]{3,2,1,0:T(8,128)(2,1)S(1)}) custom-call(s32[11]{0:T(128)S(1)} %stack.52.scalar, bf16[512,128,128]{2,1,0:T(8,128)(2,1)} %bitcast.191, bf16[128,16,128]{2,1,0:T(8,128)(2,1)S(1)} %bitcast.178), custom_call_target="tpu_custom_call" | custom-call | tf_op jit(solution)/shard_map/load_live/pallas_call | solution.py:97
  185.1 1.0 collective-permute-start.31
  186.2 2.6 %collective-permute-start.33 = (bf16[64,16,128]{2,1,0:T(8,128)(2,1)S(1)}, bf16[64,16,128]{2,1,0:T(8,128)(2,1)S(1)}, u32[]{:S(2)}, u32[]{:S(2)}) collective-permute-start(bf16[64,16,128]{2,1,0:T(8,128)(2,1)S(1)} %slice.128), channel_id=1, source_target_pairs={{2,0},{3,1},{4,2},{5,3},{6,4},{7,5},{0,6},{1,7},{10,8},{11,9},{12,... | collective-permute-start | bytes 786440 | tf_op jit(solution)/shard_map/ppermute | solution.py:147
  189.1 6.5 %collective-permute-done.31 = bf16[64,16,128]{2,1,0:T(8,128)(2,1)S(1)} collective-permute-done((bf16[64,16,128]{2,1,0:T(8,128)(2,1)S(1)}, bf16[64,16,128]{2,1,0:T(8,128)(2,1)S(1)}, u32[]{:S(2)}, u32[]{:S(2)}) %collective-permute-start.31) | collective-permute-done | bytes 262176 | tf_op jit(solution)/shard_map/ppermute | solution.py:147
  196.4 0.7 collective-permute-done.32
  197.5 3.9 %tile_sums.5 = (bf16[4,32,16,128]{3,2,1,0:T(8,128)(2,1)S(1)}, f32[4,32,16,128]{3,2,1,0:T(8,128)S(1)}) custom-call(s32[11]{0:T(128)S(1)} %stack.52.scalar, s32[512]{0:T(512)S(1)} %bitcast.185, s32[512]{0:T(512)S(1)} %bitcast.188, bf16[8,128,16,128]{3,2,1,0:T(8,128)(2,1)S(1)} %bitcast_dynamic-update-slice_fusion.15.fetched, ...), custom_call_target="tpu_custom_call" | custom-call | tf_op jit(solution)/shard_map/tile_sums/pallas_call | solution.py:57
  202.1 1.1 fusion.17
  203.9 4.6 %collective-permute-start.37 = (bf16[32,16,128]{2,1,0:T(8,128)(2,1)S(1)}, bf16[32,16,128]{2,1,0:T(8,128)(2,1)S(1)}, u32[]{:S(2)}, u32[]{:S(2)}) collective-permute-start(bf16[32,16,128]{2,1,0:T(8,128)(2,1)S(1)} %get-tuple-element.37), channel_id=1, source_target_pairs={{4,0},{5,1},{6,2},{7,3},{0,4},{1,5},{2,6},{3,7},{12,8},{13,9},{14,... | collective-permute-start | bytes 393224 | tf_op jit(solution)/shard_map/ppermute | solution.py:147
  208.8 2.4 %collective-permute-done.36 = bf16[32,16,128]{2,1,0:T(8,128)(2,1)S(1)} collective-permute-done((bf16[32,16,128]{2,1,0:T(8,128)(2,1)S(1)}, bf16[32,16,128]{2,1,0:T(8,128)(2,1)S(1)}, u32[]{:S(2)}, u32[]{:S(2)}) %collective-permute-start.36) | collective-permute-done | bytes 131104 | tf_op jit(solution)/shard_map/ppermute | solution.py:147
  211.1 4.0 %collective-permute-done.37 = bf16[32,16,128]{2,1,0:T(8,128)(2,1)S(1)} collective-permute-done((bf16[32,16,128]{2,1,0:T(8,128)(2,1)S(1)}, bf16[32,16,128]{2,1,0:T(8,128)(2,1)S(1)}, u32[]{:S(2)}, u32[]{:S(2)}) %collective-permute-start.37) | collective-permute-done | bytes 131104 | tf_op jit(solution)/shard_map/ppermute | solution.py:147
  215.2 0.9 fusion
  (109 shorter events, 10.4 us)
Async XLA Ops:
  1.4 15.7 %all-to-all-start = ((s32[16,1,8]{2,1,0:T(1,128)}), s32[16,1,8]{2,1,0:T(1,128)S(1)}, u32[]{:S(2)}, u32[]{:S(2)}) async-start(s32[16,1,8]{2,1,0:T(1,128)} %copy.20), calls=%async_computation | async-start | bytes 16384 | tf_op jit(solution)/shard_map/all_to_all | solution.py:187
  31.1 12.3 %collective-permute-start.1 = (bf16[128,16,128]{2,1,0:T(8,128)(2,1)S(1)}, bf16[128,16,128]{2,1,0:T(8,128)(2,1)S(1)}, u32[]{:S(2)}, u32[]{:S(2)}) collective-permute-start(bf16[128,16,128]{2,1,0:T(8,128)(2,1)S(1)} %bitcast.171), channel_id=1, source_target_pairs={{6,0},{7,1},{0,2},{1,3},{2,4},{3,5},{4,6},{5,7},{14,8},{15,9},{8,1... | collective-permute-start | bytes 1572872 | tf_op jit(solution)/shard_map/ppermute | solution.py:147
  32.6 15.2 %collective-permute-start.3 = (bf16[128,16,128]{2,1,0:T(8,128)(2,1)S(1)}, bf16[128,16,128]{2,1,0:T(8,128)(2,1)S(1)}, u32[]{:S(2)}, u32[]{:S(2)}) collective-permute-start(bf16[128,16,128]{2,1,0:T(8,128)(2,1)S(1)} %bitcast.172), channel_id=1, source_target_pairs={{2,0},{3,1},{4,2},{5,3},{6,4},{7,5},{0,6},{1,7},{10,8},{11,9},{12,... | collective-permute-start | bytes 1572872 | tf_op jit(solution)/shard_map/ppermute | solution.py:147
  34.3 17.0 %collective-permute-start = (bf16[128,16,128]{2,1,0:T(8,128)(2,1)S(1)}, bf16[128,16,128]{2,1,0:T(8,128)(2,1)S(1)}, u32[]{:S(2)}, u32[]{:S(2)}) collective-permute-start(bf16[128,16,128]{2,1,0:T(8,128)(2,1)S(1)} %bitcast.173), channel_id=1, source_target_pairs={{0,1},{1,0},{2,3},{3,2},{4,5},{5,4},{6,7},{7,6},{8,9},{9,8},{10,11... | collective-permute-start | bytes 1572872 | tf_op jit(solution)/shard_map/ppermute | solution.py:150
  43.4 15.1 %collective-permute-start.2 = (bf16[128,16,128]{2,1,0:T(8,128)(2,1)S(1)}, bf16[128,16,128]{2,1,0:T(8,128)(2,1)S(1)}, u32[]{:S(2)}, u32[]{:S(2)}) collective-permute-start(bf16[128,16,128]{2,1,0:T(8,128)(2,1)S(1)} %collective-permute-done.1), channel_id=1, source_target_pairs={{0,1},{1,0},{2,3},{3,2},{4,5},{5,4},{6,7},{7,6},{8,9},{9,8},{10,11... | collective-permute-start | bytes 1572872 | tf_op jit(solution)/shard_map/ppermute | solution.py:150
  47.7 12.3 %copy-start = (s32[1,1,512]{2,1,0:T(1,128)S(1)}, s32[1,1,512]{2,1,0:T(1,128)}, u32[]{:S(2)}) copy-start(s32[1,1,512]{2,1,0:T(1,128)} %param.9) | copy-start | bytes 6148
  47.7 12.3 %copy-start.1 = (s32[1,1,512]{2,1,0:T(1,128)S(1)}, s32[1,1,512]{2,1,0:T(1,128)}, u32[]{:S(2)}) copy-start(s32[1,1,512]{2,1,0:T(1,128)} %param.10) | copy-start | bytes 6148
  47.7 10.3 %collective-permute-start.5 = (bf16[64,16,128]{2,1,0:T(8,128)(2,1)S(1)}, bf16[64,16,128]{2,1,0:T(8,128)(2,1)S(1)}, u32[]{:S(2)}, u32[]{:S(2)}) collective-permute-start(bf16[64,16,128]{2,1,0:T(8,128)(2,1)S(1)} %slice.113), channel_id=1, source_target_pairs={{6,0},{7,1},{0,2},{1,3},{2,4},{3,5},{4,6},{5,7},{14,8},{15,9},{8,1... | collective-permute-start | bytes 786440 | tf_op jit(solution)/shard_map/ppermute | solution.py:147
  47.8 10.2 %collective-permute-start.7 = (bf16[64,16,128]{2,1,0:T(8,128)(2,1)S(1)}, bf16[64,16,128]{2,1,0:T(8,128)(2,1)S(1)}, u32[]{:S(2)}, u32[]{:S(2)}) collective-permute-start(bf16[64,16,128]{2,1,0:T(8,128)(2,1)S(1)} %slice.114), channel_id=1, source_target_pairs={{2,0},{3,1},{4,2},{5,3},{6,4},{7,5},{0,6},{1,7},{10,8},{11,9},{12,... | collective-permute-start | bytes 786440 | tf_op jit(solution)/shard_map/ppermute | solution.py:147
  51.1 7.6 %collective-permute-start.4 = (bf16[128,16,128]{2,1,0:T(8,128)(2,1)S(1)}, bf16[128,16,128]{2,1,0:T(8,128)(2,1)S(1)}, u32[]{:S(2)}, u32[]{:S(2)}) collective-permute-start(bf16[128,16,128]{2,1,0:T(8,128)(2,1)S(1)} %collective-permute-done.3), channel_id=1, source_target_pairs={{0,1},{1,0},{2,3},{3,2},{4,5},{5,4},{6,7},{7,6},{8,9},{9,8},{10,11... | collective-permute-start | bytes 1572872 | tf_op jit(solution)/shard_map/ppermute | solution.py:150
  58.0 1.5 collective-permute-start.6
  58.0 1.9 collective-permute-start.8
  63.9 2.3 %collective-permute-start.9 = (bf16[4,32,16,128]{3,2,1,0:T(8,128)(2,1)S(1)}, bf16[4,32,16,128]{3,2,1,0:T(8,128)(2,1)S(1)}, u32[]{:S(2)}, u32[]{:S(2)}) collective-permute-start(bf16[4,32,16,128]{3,2,1,0:T(8,128)(2,1)S(1)} %get-tuple-element.20), channel_id=1, source_target_pairs={{0,1},{1,0},{2,3},{3,2},{4,5},{5,4},{6,7},{7,6},{8,9},{9,8},{10,11... | collective-permute-start | bytes 1572872 | tf_op jit(solution)/shard_map/ppermute | solution.py:150
  66.3 7.2 %collective-permute-start.10 = (bf16[32,16,128]{2,1,0:T(8,128)(2,1)S(1)}, bf16[32,16,128]{2,1,0:T(8,128)(2,1)S(1)}, u32[]{:S(2)}, u32[]{:S(2)}) collective-permute-start(bf16[32,16,128]{2,1,0:T(8,128)(2,1)S(1)} %get-tuple-element.41), channel_id=1, source_target_pairs={{6,0},{7,1},{0,2},{1,3},{2,4},{3,5},{4,6},{5,7},{14,8},{15,9},{8,1... | collective-permute-start | bytes 393224 | tf_op jit(solution)/shard_map/ppermute | solution.py:147
  66.4 11.1 %collective-permute-start.11 = (bf16[32,16,128]{2,1,0:T(8,128)(2,1)S(1)}, bf16[32,16,128]{2,1,0:T(8,128)(2,1)S(1)}, u32[]{:S(2)}, u32[]{:S(2)}) collective-permute-start(bf16[32,16,128]{2,1,0:T(8,128)(2,1)S(1)} %get-tuple-element.43), channel_id=1, source_target_pairs={{4,0},{5,1},{6,2},{7,3},{0,4},{1,5},{2,6},{3,7},{12,8},{13,9},{14,... | collective-permute-start | bytes 393224 | tf_op jit(solution)/shard_map/ppermute | solution.py:147
  71.0 6.6 %collective-permute-start.12 = (bf16[32,16,128]{2,1,0:T(8,128)(2,1)S(1)}, bf16[32,16,128]{2,1,0:T(8,128)(2,1)S(1)}, u32[]{:S(2)}, u32[]{:S(2)}) collective-permute-start(bf16[32,16,128]{2,1,0:T(8,128)(2,1)S(1)} %get-tuple-element.42), channel_id=1, source_target_pairs={{2,0},{3,1},{4,2},{5,3},{6,4},{7,5},{0,6},{1,7},{10,8},{11,9},{12,... | collective-permute-start | bytes 393224 | tf_op jit(solution)/shard_map/ppermute | solution.py:147
  96.8 13.2 %collective-permute-start.14 = (bf16[128,16,128]{2,1,0:T(8,128)(2,1)S(1)}, bf16[128,16,128]{2,1,0:T(8,128)(2,1)S(1)}, u32[]{:S(2)}, u32[]{:S(2)}) collective-permute-start(bf16[128,16,128]{2,1,0:T(8,128)(2,1)S(1)} %bitcast.179), channel_id=1, source_target_pairs={{6,0},{7,1},{0,2},{1,3},{2,4},{3,5},{4,6},{5,7},{14,8},{15,9},{8,1... | collective-permute-start | bytes 1572872 | tf_op jit(solution)/shard_map/ppermute | solution.py:147
  97.1 16.5 %collective-permute-start.16 = (bf16[128,16,128]{2,1,0:T(8,128)(2,1)S(1)}, bf16[128,16,128]{2,1,0:T(8,128)(2,1)S(1)}, u32[]{:S(2)}, u32[]{:S(2)}) collective-permute-start(bf16[128,16,128]{2,1,0:T(8,128)(2,1)S(1)} %bitcast.180), channel_id=1, source_target_pairs={{2,0},{3,1},{4,2},{5,3},{6,4},{7,5},{0,6},{1,7},{10,8},{11,9},{12,... | collective-permute-start | bytes 1572872 | tf_op jit(solution)/shard_map/ppermute | solution.py:147
  100.1 17.1 %collective-permute-start.13 = (bf16[128,16,128]{2,1,0:T(8,128)(2,1)S(1)}, bf16[128,16,128]{2,1,0:T(8,128)(2,1)S(1)}, u32[]{:S(2)}, u32[]{:S(2)}) collective-permute-start(bf16[128,16,128]{2,1,0:T(8,128)(2,1)S(1)} %bitcast.181), channel_id=1, source_target_pairs={{0,1},{1,0},{2,3},{3,2},{4,5},{5,4},{6,7},{7,6},{8,9},{9,8},{10,11... | collective-permute-start | bytes 1572872 | tf_op jit(solution)/shard_map/ppermute | solution.py:150
  110.0 14.4 %collective-permute-start.15 = (bf16[128,16,128]{2,1,0:T(8,128)(2,1)S(1)}, bf16[128,16,128]{2,1,0:T(8,128)(2,1)S(1)}, u32[]{:S(2)}, u32[]{:S(2)}) collective-permute-start(bf16[128,16,128]{2,1,0:T(8,128)(2,1)S(1)} %collective-permute-done.14), channel_id=1, source_target_pairs={{0,1},{1,0},{2,3},{3,2},{4,5},{5,4},{6,7},{7,6},{8,9},{9,8},{10,11... | collective-permute-start | bytes 1572872 | tf_op jit(solution)/shard_map/ppermute | solution.py:150
  113.6 10.3 %collective-permute-start.18 = (bf16[64,16,128]{2,1,0:T(8,128)(2,1)S(1)}, bf16[64,16,128]{2,1,0:T(8,128)(2,1)S(1)}, u32[]{:S(2)}, u32[]{:S(2)}) collective-permute-start(bf16[64,16,128]{2,1,0:T(8,128)(2,1)S(1)} %slice.119), channel_id=1, source_target_pairs={{6,0},{7,1},{0,2},{1,3},{2,4},{3,5},{4,6},{5,7},{14,8},{15,9},{8,1... | collective-permute-start | bytes 786440 | tf_op jit(solution)/shard_map/ppermute | solution.py:147
  113.7 10.2 %collective-permute-start.20 = (bf16[64,16,128]{2,1,0:T(8,128)(2,1)S(1)}, bf16[64,16,128]{2,1,0:T(8,128)(2,1)S(1)}, u32[]{:S(2)}, u32[]{:S(2)}) collective-permute-start(bf16[64,16,128]{2,1,0:T(8,128)(2,1)S(1)} %slice.120), channel_id=1, source_target_pairs={{2,0},{3,1},{4,2},{5,3},{6,4},{7,5},{0,6},{1,7},{10,8},{11,9},{12,... | collective-permute-start | bytes 786440 | tf_op jit(solution)/shard_map/ppermute | solution.py:147
  117.0 7.6 %collective-permute-start.17 = (bf16[128,16,128]{2,1,0:T(8,128)(2,1)S(1)}, bf16[128,16,128]{2,1,0:T(8,128)(2,1)S(1)}, u32[]{:S(2)}, u32[]{:S(2)}) collective-permute-start(bf16[128,16,128]{2,1,0:T(8,128)(2,1)S(1)} %collective-permute-done.16), channel_id=1, source_target_pairs={{0,1},{1,0},{2,3},{3,2},{4,5},{5,4},{6,7},{7,6},{8,9},{9,8},{10,11... | collective-permute-start | bytes 1572872 | tf_op jit(solution)/shard_map/ppermute | solution.py:150
  123.9 1.5 collective-permute-start.19
  123.9 1.9 collective-permute-start.21
  129.7 2.2 %collective-permute-start.22 = (bf16[4,32,16,128]{3,2,1,0:T(8,128)(2,1)S(1)}, bf16[4,32,16,128]{3,2,1,0:T(8,128)(2,1)S(1)}, u32[]{:S(2)}, u32[]{:S(2)}) collective-permute-start(bf16[4,32,16,128]{3,2,1,0:T(8,128)(2,1)S(1)} %get-tuple-element.24), channel_id=1, source_target_pairs={{0,1},{1,0},{2,3},{3,2},{4,5},{5,4},{6,7},{7,6},{8,9},{9,8},{10,11... | collective-permute-start | bytes 1572872 | tf_op jit(solution)/shard_map/ppermute | solution.py:150
  132.2 7.4 %collective-permute-start.23 = (bf16[32,16,128]{2,1,0:T(8,128)(2,1)S(1)}, bf16[32,16,128]{2,1,0:T(8,128)(2,1)S(1)}, u32[]{:S(2)}, u32[]{:S(2)}) collective-permute-start(bf16[32,16,128]{2,1,0:T(8,128)(2,1)S(1)} %get-tuple-element.38), channel_id=1, source_target_pairs={{6,0},{7,1},{0,2},{1,3},{2,4},{3,5},{4,6},{5,7},{14,8},{15,9},{8,1... | collective-permute-start | bytes 393224 | tf_op jit(solution)/shard_map/ppermute | solution.py:147
  132.4 11.2 %collective-permute-start.24 = (bf16[32,16,128]{2,1,0:T(8,128)(2,1)S(1)}, bf16[32,16,128]{2,1,0:T(8,128)(2,1)S(1)}, u32[]{:S(2)}, u32[]{:S(2)}) collective-permute-start(bf16[32,16,128]{2,1,0:T(8,128)(2,1)S(1)} %get-tuple-element.40), channel_id=1, source_target_pairs={{4,0},{5,1},{6,2},{7,3},{0,4},{1,5},{2,6},{3,7},{12,8},{13,9},{14,... | collective-permute-start | bytes 393224 | tf_op jit(solution)/shard_map/ppermute | solution.py:147
  137.0 6.6 %collective-permute-start.25 = (bf16[32,16,128]{2,1,0:T(8,128)(2,1)S(1)}, bf16[32,16,128]{2,1,0:T(8,128)(2,1)S(1)}, u32[]{:S(2)}, u32[]{:S(2)}) collective-permute-start(bf16[32,16,128]{2,1,0:T(8,128)(2,1)S(1)} %get-tuple-element.39), channel_id=1, source_target_pairs={{2,0},{3,1},{4,2},{5,3},{6,4},{7,5},{0,6},{1,7},{10,8},{11,9},{12,... | collective-permute-start | bytes 393224 | tf_op jit(solution)/shard_map/ppermute | solution.py:147
  164.3 13.2 %collective-permute-start.27 = (bf16[128,16,128]{2,1,0:T(8,128)(2,1)S(1)}, bf16[128,16,128]{2,1,0:T(8,128)(2,1)S(1)}, u32[]{:S(2)}, u32[]{:S(2)}) collective-permute-start(bf16[128,16,128]{2,1,0:T(8,128)(2,1)S(1)} %bitcast.175), channel_id=1, source_target_pairs={{6,0},{7,1},{0,2},{1,3},{2,4},{3,5},{4,6},{5,7},{14,8},{15,9},{8,1... | collective-permute-start | bytes 1572872 | tf_op jit(solution)/shard_map/ppermute | solution.py:147
  164.5 21.6 %collective-permute-start.29 = (bf16[128,16,128]{2,1,0:T(8,128)(2,1)S(1)}, bf16[128,16,128]{2,1,0:T(8,128)(2,1)S(1)}, u32[]{:S(2)}, u32[]{:S(2)}) collective-permute-start(bf16[128,16,128]{2,1,0:T(8,128)(2,1)S(1)} %bitcast.176), channel_id=1, source_target_pairs={{2,0},{3,1},{4,2},{5,3},{6,4},{7,5},{0,6},{1,7},{10,8},{11,9},{12,... | collective-permute-start | bytes 1572872 | tf_op jit(solution)/shard_map/ppermute | solution.py:147
  167.5 21.4 %collective-permute-start.26 = (bf16[128,16,128]{2,1,0:T(8,128)(2,1)S(1)}, bf16[128,16,128]{2,1,0:T(8,128)(2,1)S(1)}, u32[]{:S(2)}, u32[]{:S(2)}) collective-permute-start(bf16[128,16,128]{2,1,0:T(8,128)(2,1)S(1)} %bitcast.177), channel_id=1, source_target_pairs={{0,1},{1,0},{2,3},{3,2},{4,5},{5,4},{6,7},{7,6},{8,9},{9,8},{10,11... | collective-permute-start | bytes 1572872 | tf_op jit(solution)/shard_map/ppermute | solution.py:150
  177.4 18.6 %collective-permute-start.28 = (bf16[128,16,128]{2,1,0:T(8,128)(2,1)S(1)}, bf16[128,16,128]{2,1,0:T(8,128)(2,1)S(1)}, u32[]{:S(2)}, u32[]{:S(2)}) collective-permute-start(bf16[128,16,128]{2,1,0:T(8,128)(2,1)S(1)} %collective-permute-done.27), channel_id=1, source_target_pairs={{0,1},{1,0},{2,3},{3,2},{4,5},{5,4},{6,7},{7,6},{8,9},{9,8},{10,11... | collective-permute-start | bytes 1572872 | tf_op jit(solution)/shard_map/ppermute | solution.py:150
  178.2 25.1 %all-to-all-start.3 = ((bf16[8,4,2,16,128]{4,3,1,2,0:T(8,128)(2,1)}), bf16[8,4,2,16,128]{4,3,1,2,0:T(8,128)(2,1)S(1)}, u32[]{:S(2)}, u32[]{:S(2)}) async-start(bf16[8,4,2,16,128]{4,3,1,2,0:T(8,128)(2,1)} %pad_maximum_fusion), calls=%async_computation.3 | async-start | bytes 524288 | tf_op jit(solution)/shard_map/all_to_all | solution.py:176
  185.1 10.4 %collective-permute-start.31 = (bf16[64,16,128]{2,1,0:T(8,128)(2,1)S(1)}, bf16[64,16,128]{2,1,0:T(8,128)(2,1)S(1)}, u32[]{:S(2)}, u32[]{:S(2)}) collective-permute-start(bf16[64,16,128]{2,1,0:T(8,128)(2,1)S(1)} %slice.127), channel_id=1, source_target_pairs={{6,0},{7,1},{0,2},{1,3},{2,4},{3,5},{4,6},{5,7},{14,8},{15,9},{8,1... | collective-permute-start | bytes 786440 | tf_op jit(solution)/shard_map/ppermute | solution.py:147
  186.2 9.4 %collective-permute-start.33 = (bf16[64,16,128]{2,1,0:T(8,128)(2,1)S(1)}, bf16[64,16,128]{2,1,0:T(8,128)(2,1)S(1)}, u32[]{:S(2)}, u32[]{:S(2)}) collective-permute-start(bf16[64,16,128]{2,1,0:T(8,128)(2,1)S(1)} %slice.128), channel_id=1, source_target_pairs={{2,0},{3,1},{4,2},{5,3},{6,4},{7,5},{0,6},{1,7},{10,8},{11,9},{12,... | collective-permute-start | bytes 786440 | tf_op jit(solution)/shard_map/ppermute | solution.py:147
  188.8 7.4 %collective-permute-start.30 = (bf16[128,16,128]{2,1,0:T(8,128)(2,1)S(1)}, bf16[128,16,128]{2,1,0:T(8,128)(2,1)S(1)}, u32[]{:S(2)}, u32[]{:S(2)}) collective-permute-start(bf16[128,16,128]{2,1,0:T(8,128)(2,1)S(1)} %collective-permute-done.29), channel_id=1, source_target_pairs={{0,1},{1,0},{2,3},{3,2},{4,5},{5,4},{6,7},{7,6},{8,9},{9,8},{10,11... | collective-permute-start | bytes 1572872 | tf_op jit(solution)/shard_map/ppermute | solution.py:150
  195.6 1.5 collective-permute-start.32
  195.6 1.9 collective-permute-start.34
  197.5 4.6 %copy-start.2 = (bf16[4,128,256]{2,1,0:T(8,128)(2,1)S(1)}, bf16[4,128,256]{2,1,0:T(8,128)(2,1)}, u32[]{:S(2)}) copy-start(bf16[4,128,256]{2,1,0:T(8,128)(2,1)} %param.13) | copy-start | bytes 786436
  201.4 2.2 %collective-permute-start.35 = (bf16[4,32,16,128]{3,2,1,0:T(8,128)(2,1)S(1)}, bf16[4,32,16,128]{3,2,1,0:T(8,128)(2,1)S(1)}, u32[]{:S(2)}, u32[]{:S(2)}) collective-permute-start(bf16[4,32,16,128]{3,2,1,0:T(8,128)(2,1)S(1)} %get-tuple-element.28), channel_id=1, source_target_pairs={{0,1},{1,0},{2,3},{3,2},{4,5},{5,4},{6,7},{7,6},{8,9},{9,8},{10,11... | collective-permute-start | bytes 1572872 | tf_op jit(solution)/shard_map/ppermute | solution.py:150
  203.9 7.3 %collective-permute-start.36 = (bf16[32,16,128]{2,1,0:T(8,128)(2,1)S(1)}, bf16[32,16,128]{2,1,0:T(8,128)(2,1)S(1)}, u32[]{:S(2)}, u32[]{:S(2)}) collective-permute-start(bf16[32,16,128]{2,1,0:T(8,128)(2,1)S(1)} %get-tuple-element.35), channel_id=1, source_target_pairs={{6,0},{7,1},{0,2},{1,3},{2,4},{3,5},{4,6},{5,7},{14,8},{15,9},{8,1... | collective-permute-start | bytes 393224 | tf_op jit(solution)/shard_map/ppermute | solution.py:147
  203.9 11.2 %collective-permute-start.37 = (bf16[32,16,128]{2,1,0:T(8,128)(2,1)S(1)}, bf16[32,16,128]{2,1,0:T(8,128)(2,1)S(1)}, u32[]{:S(2)}, u32[]{:S(2)}) collective-permute-start(bf16[32,16,128]{2,1,0:T(8,128)(2,1)S(1)} %get-tuple-element.37), channel_id=1, source_target_pairs={{4,0},{5,1},{6,2},{7,3},{0,4},{1,5},{2,6},{3,7},{12,8},{13,9},{14,... | collective-permute-start | bytes 393224 | tf_op jit(solution)/shard_map/ppermute | solution.py:147
  208.6 6.6 %collective-permute-start.38 = (bf16[32,16,128]{2,1,0:T(8,128)(2,1)S(1)}, bf16[32,16,128]{2,1,0:T(8,128)(2,1)S(1)}, u32[]{:S(2)}, u32[]{:S(2)}) collective-permute-start(bf16[32,16,128]{2,1,0:T(8,128)(2,1)S(1)} %get-tuple-element.36), channel_id=1, source_target_pairs={{2,0},{3,1},{4,2},{5,3},{6,4},{7,5},{0,6},{1,7},{10,8},{11,9},{12,... | collective-permute-start | bytes 393224 | tf_op jit(solution)/shard_map/ppermute | solution.py:147
